TPU v7x, 32 devices: a whole 2x2x4 slice. The times are simulated.
32 devices in a mesh: seq: 8 (over z, y), head: 4 (over x, core).
Axes of the slice: x: 2, y: 2, z: 4, core: 2. Of those that a mesh axis runs over, the one named last changes fastest.
Arguments:
- queries: bfloat16 [1024, 8, 128], P('seq', 'head'), may hold values from -16 to 16
- values: bfloat16 [1024, 8, 128], P('seq', 'head'), may hold values from -6 to 6
- codes: int32 [8, 1024], P('head', 'seq'), may hold values from 0 to 511, as said below
- codebook: bfloat16 [8, 512, 128], P('head'), may hold values from -0.5 to 0.5
- out_weight: bfloat16 [1024, 2048], P('head'), may hold values from -0.1875 to 0.1875
- grad_out: bfloat16 [1024, 2048], P('seq', 'head'), may hold values from -6 to 6
Outputs:
- grad_queries: bfloat16 [1024, 8, 128], P('seq', 'head')
- grad_values: bfloat16 [1024, 8, 128], P('seq', 'head')
- grad_codebook: float32 [8, 512, 128], P('head')
- grad_weight: bfloat16 [1024, 2048], P('head')
Inputs may be any that keep to these rules, and one draw needn't show every extreme that they name: `codes`: each head's key codeword at each token; both 0 and 511 occur.
All inputs are finite; a program needn't handle non-finite values.
Results may differ from a plain program's by a relative error of at most 0.0065.
Values may be sent and summed in bfloat16 or wider, within the bound.
No kernel may reach another device: no remote copies, remote signals or barrier semaphores. Data moves between devices by JAX's collectives and lax.ppermute only.
A program may use at most 256 MiB of HBM per device.

v0:
```python
import jax
import jax.numpy as jnp
from jax import lax
from jax.sharding import PartitionSpec as P

BLOCK = 128


def entering(value, axis, join, neutral, backward):
    count, mine = (lax.axis_size(axis), lax.axis_index(axis))
    pieces = jax.tree.map(lambda part: lax.all_gather(part, axis), value)
    if backward:
        pieces = jax.tree.map(lambda part: part[::-1], pieces)
        mine = count - 1 - mine
    so_far = jax.tree.map(
        lambda part, zero: jnp.full_like(part, 0) + jnp.asarray(zero, part.dtype), value, neutral
    )

    def turn(position, so_far):
        longer = join(so_far, jax.tree.map(lambda part: part[position], pieces))
        return jax.tree.map(lambda new, old: jnp.where(position < mine, new, old), longer, so_far)

    return lax.fori_loop(0, count - 1, turn, so_far)


def inner_rows(left_side, right_side):
    return lax.dot_general(
        left_side, right_side, (((0,), (0,)), ((), ())), preferred_element_type=jnp.float32
    )


def block_core(query_rows, code_rows, value_rows, grad_rows, cache_sum, cache_count, codebook_head):
    key_rows = jnp.take(codebook_head, code_rows, axis=0)
    contract_last = (((1,), (1,)), ((), ()))
    local_score = lax.dot_general(
        query_rows, key_rows, contract_last, preferred_element_type=jnp.float32
    )
    code_score = lax.dot_general(
        query_rows, codebook_head, contract_last, preferred_element_type=jnp.float32
    )
    length = query_rows.shape[0]
    row_index = lax.broadcasted_iota(jnp.int32, (length, length), 0)
    col_index = lax.broadcasted_iota(jnp.int32, (length, length), 1)
    causal = col_index <= row_index
    top_score = jnp.maximum(
        jnp.max(jnp.where(causal, local_score, -jnp.inf), axis=1), jnp.max(code_score, axis=1)
    )
    weights = jnp.where(causal, jnp.exp(local_score - top_score[:, None]), jnp.float32(0.0))
    cache_weight = jnp.exp(code_score - top_score[:, None])
    denominator = jnp.sum(weights, axis=1) + jnp.sum(cache_weight * cache_count[None, :], axis=1)
    cache_round = cache_sum.astype(jnp.bfloat16)
    numerator = jnp.dot(
        weights.astype(jnp.bfloat16), value_rows, preferred_element_type=jnp.float32
    )
    numerator = numerator + jnp.dot(
        cache_weight.astype(jnp.bfloat16), cache_round, preferred_element_type=jnp.float32
    )
    attended = numerator / denominator[:, None]
    row_delta = jnp.sum(grad_rows.astype(jnp.float32) * attended, axis=1)
    local_grad = lax.dot_general(
        grad_rows, value_rows, contract_last, preferred_element_type=jnp.float32
    )
    cache_grad = lax.dot_general(
        grad_rows, cache_round, contract_last, preferred_element_type=jnp.float32
    )
    grad_local = (weights * (local_grad - row_delta[:, None]) / denominator[:, None]).astype(
        jnp.bfloat16
    )
    grad_cache = (
        cache_weight
        * (cache_grad - row_delta[:, None] * cache_count[None, :])
        / denominator[:, None]
    ).astype(jnp.bfloat16)
    grad_query = jnp.dot(grad_local, key_rows, preferred_element_type=jnp.float32)
    grad_query = (
        grad_query + jnp.dot(grad_cache, codebook_head, preferred_element_type=jnp.float32)
    ).astype(jnp.bfloat16)
    grad_key = inner_rows(grad_local, query_rows)
    key_high = grad_key.astype(jnp.bfloat16)
    key_low = (grad_key - key_high.astype(jnp.float32)).astype(jnp.bfloat16)
    selector = (
        code_rows[:, None] == jnp.arange(codebook_head.shape[0], dtype=jnp.int32)[None, :]
    ).astype(jnp.bfloat16)
    grad_book = inner_rows(selector, key_high) + inner_rows(selector, key_low)
    grad_book = grad_book + inner_rows(grad_cache, query_rows)
    local_share = (weights / denominator[:, None]).astype(jnp.bfloat16)
    cache_share = (cache_weight / denominator[:, None]).astype(jnp.bfloat16)
    grad_value = inner_rows(local_share, grad_rows)
    grad_sum = inner_rows(cache_share, grad_rows)
    return (grad_query, grad_value, grad_sum, grad_book, attended.astype(jnp.bfloat16))


def exclusive_forward(stacked):
    summed = jnp.cumsum(stacked, axis=1)
    return jnp.concatenate([jnp.zeros_like(stacked), summed[:, :-1]], axis=1)


def exclusive_backward(stacked):
    summed = jnp.flip(jnp.cumsum(jnp.flip(stacked, axis=1), axis=1), axis=1)
    return jnp.concatenate([summed[:, 1:], jnp.zeros_like(stacked)], axis=1)


def on_device(queries, values, codes, codebook, out_weight, grad_out):
    tok_here, heads_here, head_width = queries.shape
    code_total = codebook.shape[1]
    blocks = tok_here // BLOCK
    full_grad = lax.all_gather(grad_out, "head", axis=1, tiled=True)
    grad_flat = lax.dot_general(
        full_grad, out_weight, (((1,), (1,)), ((), ())), preferred_element_type=jnp.float32
    ).astype(jnp.bfloat16)
    grad_heads = grad_flat.reshape(tok_here, heads_here, head_width)

    def to_blocks(array):
        return jnp.moveaxis(array.reshape(blocks, BLOCK, heads_here, head_width), 2, 0)

    def from_blocks(array):
        return jnp.moveaxis(array, 0, 2).reshape(tok_here, heads_here, head_width)

    def flatten(array):
        return array.reshape((heads_here * blocks,) + array.shape[2:])

    def unflatten(array):
        return array.reshape((heads_here, blocks) + array.shape[1:])

    code_blocks = codes.reshape(heads_here, blocks, BLOCK)
    query_blocks = to_blocks(queries)
    value_blocks = to_blocks(values)
    grad_blocks = to_blocks(grad_heads)
    selector = (code_blocks[..., None] == jnp.arange(code_total, dtype=jnp.int32)).astype(
        jnp.bfloat16
    )
    block_sums = jnp.einsum(
        "hnbc,hnbd->hncd", selector, value_blocks, preferred_element_type=jnp.float32
    )
    block_counts = jnp.sum(selector, axis=2, dtype=jnp.float32)
    device_parts = (jnp.sum(block_sums, axis=1), jnp.sum(block_counts, axis=1))
    earlier = entering(
        device_parts,
        "seq",
        lambda first_part, second_part: (
            first_part[0] + second_part[0],
            first_part[1] + second_part[1],
        ),
        (jnp.zeros_like(device_parts[0]), jnp.zeros_like(device_parts[1])),
        False,
    )
    cache_sums = earlier[0][:, None] + exclusive_forward(block_sums)
    cache_counts = earlier[1][:, None] + exclusive_forward(block_counts)
    books = jnp.repeat(codebook, blocks, axis=0)
    results = lax.map(
        lambda block_items: block_core(*block_items),
        (
            flatten(query_blocks),
            flatten(code_blocks),
            flatten(value_blocks),
            flatten(grad_blocks),
            flatten(cache_sums),
            flatten(cache_counts),
            books,
        ),
    )
    grad_query = unflatten(results[0])
    grad_value = unflatten(results[1])
    grad_sums = unflatten(results[2])
    grad_books = unflatten(results[3])
    attended = unflatten(results[4])
    device_grad = jnp.sum(grad_sums, axis=1)
    later_grad = entering(
        device_grad,
        "seq",
        lambda first_part, second_part: first_part + second_part,
        jnp.zeros_like(device_grad),
        True,
    )
    carried = later_grad[:, None] + exclusive_backward(grad_sums)
    picked = jax.vmap(jax.vmap(lambda table_rows, indices: jnp.take(table_rows, indices, axis=0)))(
        carried, code_blocks
    )
    grad_values = (grad_value + picked).astype(jnp.bfloat16)
    book_here = jnp.sum(grad_books, axis=1)
    attended_flat = from_blocks(attended).reshape(tok_here, heads_here * head_width)
    weight_term = inner_rows(attended_flat, full_grad)
    summed_weight, summed_book = lax.psum((weight_term, book_here), "seq")
    grad_weight = summed_weight.astype(jnp.bfloat16)
    return (from_blocks(grad_query), from_blocks(grad_values), summed_book, grad_weight)


def solution(mesh):
    return jax.shard_map(
        on_device,
        mesh=mesh,
        in_specs=(
            P("seq", "head", None),
            P("seq", "head", None),
            P("head", "seq"),
            P("head", None, None),
            P("head", None),
            P("seq", "head"),
        ),
        out_specs=(
            P("seq", "head", None),
            P("seq", "head", None),
            P("head", None, None),
            P("head", None),
        ),
        check_vma=False,
    )
```

profile of v0, /device:TPU:27, one launch (start us, length us, event | category | flops | bytes accessed | tf_op | source)
XLA Modules:
  0.0 316.9 jit_solution(7390471878237787274)
XLA Ops:
  7.2 2.0 fusion.71
  10.2 7.5 %all_gather.21 = bf16[128,2048]{1,0:T(8,128)(2,1)S(1)} all-gather(bf16[128,512]{1,0:T(8,128)(2,1)} %param.17), channel_id=1, replica_groups=mesh['seq'=8,'head'=4] {'head'}, dimensions={1}, use_global_device_ids=true | all-gather | bytes 655360 | tf_op jit(solution)/shard_map/all_gather | solution.py:107
  18.3 0.9 copy.55
  20.0 22.2 %all-gather.3 = f32[8,2,512]{2,1,0:T(2,128)S(1)} all-gather(f32[1,2,512]{2,1,0:T(2,128)S(1)} %bitcast.203), channel_id=3, replica_groups=mesh['seq'=8,'head'=4] {'seq'}, dimensions={0}, use_global_device_ids=true | all-gather | bytes 36864 | tf_op jit(solution)/shard_map/all_gather | solution.py:11
  42.2 41.0 %all-gather.7.cloned.1.call-done = f32[16,512,128]{2,1,0:T(8,128)} async-done(((f32[2,512,128]{2,1,0:T(8,128)}), f32[16,512,128]{2,1,0:T(8,128)}) %all-gather.7.cloned.1.call-update) | async-done | bytes 4194320 | tf_op jit(solution)/shard_map/all_gather | solution.py:11
  83.2 8.7 %while.49 = (s32[]{:T(128)}, f32[2,512,128]{2,1,0:T(8,128)S(1)}, f32[2,512]{1,0:T(2,128)S(1)}, s32[]{:T(128)}, f32[8,2,512,128]{3,2,1,0:T(8,128)}, /*index=5*/f32[8,2,512]{2,1,0:T(2,128)S(1)}, s32[]{:T(128)}, s32[]{:T(128)}) while((s32[]{:T(128)}, f32[2,512,128]{2,1,0:T(8,128)S(1)}, f32[2,512]{1,0:T(2,128)S(1)}, s32[]{:T(128)}, ...), condition=%wide.region_2.0_spmd.clone, body=%wide.region_1.0_spmd.clone.sunk | while | flops 396292 | bytes 1585267 | solution.py:23
  83.2 1.2 add_select_fusion.6
  84.5 1.2 add_select_fusion.6
  85.8 1.2 add_select_fusion.6
  87.0 1.2 add_select_fusion.6
  88.3 1.2 add_select_fusion.6
  89.5 1.2 add_select_fusion.6
  90.8 1.2 add_select_fusion.6
  92.1 14.3 %while.48 = (s32[]{:T(128)}, bf16[2,128,128]{2,1,0:T(8,128)(2,1)}, f32[2,128,128]{2,0,1:T(2,128)}, f32[2,512,128]{2,1,0:T(8,128)}, f32[2,512,128]{2,1,0:T(8,128)...) while((s32[]{:T(128)}, bf16[2,128,128]{2,1,0:T(8,128)(2,1)}, ...), condition=%wide.region_9.10_spmd, body=%wide.region_3.9_spmd.sunk | while | flops 161253120 | bytes 12096661 | solution.py:150
  96.7 1.4 dynamic_update_slice.31
  103.8 1.4 dynamic_update_slice.31
  106.8 2.6 fusion.86
  109.4 1.5 copy.53
  110.9 114.5 %all-reduce.4 = bf16[256,2048]{1,0:T(8,128)(2,1)} all-reduce(f32[256,2048]{1,0:T(8,128)} %fusion.86), channel_id=1, replica_groups=mesh['seq'=8,'head'=4] {'seq'}, use_global_device_ids=true, to_apply=%region_13.14 | all-reduce | flops 524288 | bytes 3145728 | tf_op jit(solution)/shard_map/psum | solution.py:183
  225.4 9.3 %all-gather.9.cloned.1.call-done = f32[16,512,128]{2,1,0:T(8,128)} async-done(((f32[2,512,128]{2,1,0:T(8,128)}), f32[16,512,128]{2,1,0:T(8,128)}) %all-gather.9.cloned.1.call-update) | async-done | bytes 4194320 | tf_op jit(solution)/shard_map/all_gather | solution.py:11
  234.8 4.5 %rev.3 = f32[8,2,512,128]{3,2,1,0:T(8,128)} reverse(f32[8,2,512,128]{3,2,1,0:T(8,128)} %bitcast.193), dimensions={0} | reverse | bytes 8388608 | tf_op jit(solution)/shard_map/rev | solution.py:13
  239.3 8.6 %while.50 = (s32[]{:T(128)}, f32[2,512,128]{2,1,0:T(8,128)S(1)}, s32[]{:T(128)}, f32[8,2,512,128]{3,2,1,0:T(8,128)}, s32[]{:T(128)}, /*index=5*/s32[]{:T(128)}) while((s32[]{:T(128)}, f32[2,512,128]{2,1,0:T(8,128)S(1)}, s32[]{:T(128)}, f32[8,2,512,128]{3,2,1,0:T(8,128)}, s32[]{:T(128)}, /*index=5*/s32[]{:T(128)}) %tuple.98), condition=%wide.region_11.12_spmd.clone, body=%wide.region_10.11_spmd.clone.sunk | while | flops 393220 | bytes 1572957 | solution.py:23
  239.3 1.2 add_select_fusion.8
  240.6 1.2 add_select_fusion.8
  241.8 1.2 add_select_fusion.8
  243.0 1.2 add_select_fusion.8
  244.2 1.2 add_select_fusion.8
  245.5 1.2 add_select_fusion.8
  246.7 1.2 add_select_fusion.8
  247.9 1.9 gather_fusion.1
  250.7 57.8 %all-reduce.3.cloned.1.call-done = f32[2,512,128]{2,1,0:T(8,128)} async-done(((f32[2,512,128]{2,1,0:T(8,128)}), f32[2,512,128]{2,1,0:T(8,128)}) %all-reduce.3.cloned.1.call-update) | async-done | bytes 524304 | tf_op jit(solution)/shard_map/psum | solution.py:183
  308.5 1.9 copy.97
  (126 shorter events, 14.9 us)
Async XLA Ops:
  7.2 10.5 %copy-start = (bf16[256,2048]{1,0:T(8,128)(2,1)S(1)}, bf16[256,2048]{1,0:T(8,128)(2,1)}, u32[]{:S(2)}) copy-start(bf16[256,2048]{1,0:T(8,128)(2,1)} %param.16) | copy-start | bytes 3145732
  7.2 76.1 %all-gather.7.cloned.1.call-start = ((), (), s32[]{:S(2)}) async-start(), calls=%async_computation.1 | async-start | bytes 4718592 | tf_op jit(solution)/shard_map/all_gather | solution.py:11
  9.2 225.6 %all-gather.9.cloned.1.call-start = ((), (), s32[]{:S(2)}) async-start(), calls=%async_computation.2 | async-start | bytes 4718592 | tf_op jit(solution)/shard_map/all_gather | solution.py:11
  83.2 8.8 %copy-start.1 = (bf16[2,512,128]{2,1,0:T(8,128)(2,1)S(1)}, bf16[2,512,128]{2,1,0:T(8,128)(2,1)}, u32[]{:S(2)}) copy-start(bf16[2,512,128]{2,1,0:T(8,128)(2,1)} %param.15) | copy-start | bytes 786436
  83.2 8.8 %copy-start.12 = (s32[2,128]{1,0:T(2,128)S(1)}, s32[2,128]{1,0:T(2,128)}, u32[]{:S(2)}) copy-start(s32[2,128]{1,0:T(2,128)} %param.14) | copy-start | bytes 3076
  92.1 4.6 %copy-start.5 = (f32[2,128,128]{2,0,1:T(2,128)S(1)}, f32[2,128,128]{2,0,1:T(2,128)}, u32[]{:S(2)}) copy-start(f32[2,128,128]{2,0,1:T(2,128)} %get-tuple-element.601) | copy-start | bytes 393220 | tf_op jit(solution)/shard_map/while
  92.1 6.3 %copy-start.8 = (bf16[2,128,128]{2,1,0:T(8,128)(2,1)S(1)}, bf16[2,128,128]{2,1,0:T(8,128)(2,1)}, u32[]{:S(2)}) copy-start(bf16[2,128,128]{2,1,0:T(8,128)(2,1)} %get-tuple-element.600) | copy-start | bytes 196612 | tf_op jit(solution)/shard_map/while
  92.1 6.5 %copy-start.10 = (bf16[2,128,128]{1,2,0:T(8,128)(2,1)S(1)}, bf16[2,128,128]{1,2,0:T(8,128)(2,1)}, u32[]{:S(2)}) copy-start(bf16[2,128,128]{1,2,0:T(8,128)(2,1)} %get-tuple-element.604) | copy-start | bytes 196612 | tf_op jit(solution)/shard_map/while
  92.9 2.7 copy-start.3
  95.9 0.8 copy-start.4
  98.1 0.7 copy-start.6
  98.6 0.6 copy-start.9
  98.6 0.6 copy-start.11
  99.3 4.6 %copy-start.5 = (f32[2,128,128]{2,0,1:T(2,128)S(1)}, f32[2,128,128]{2,0,1:T(2,128)}, u32[]{:S(2)}) copy-start(f32[2,128,128]{2,0,1:T(2,128)} %get-tuple-element.601) | copy-start | bytes 393220 | tf_op jit(solution)/shard_map/while
  99.3 6.3 %copy-start.8 = (bf16[2,128,128]{2,1,0:T(8,128)(2,1)S(1)}, bf16[2,128,128]{2,1,0:T(8,128)(2,1)}, u32[]{:S(2)}) copy-start(bf16[2,128,128]{2,1,0:T(8,128)(2,1)} %get-tuple-element.600) | copy-start | bytes 196612 | tf_op jit(solution)/shard_map/while
  99.3 6.5 %copy-start.10 = (bf16[2,128,128]{1,2,0:T(8,128)(2,1)S(1)}, bf16[2,128,128]{1,2,0:T(8,128)(2,1)}, u32[]{:S(2)}) copy-start(bf16[2,128,128]{1,2,0:T(8,128)(2,1)} %get-tuple-element.604) | copy-start | bytes 196612 | tf_op jit(solution)/shard_map/while
  100.0 2.7 copy-start.3
  103.0 0.8 copy-start.4
  105.3 0.7 copy-start.6
  105.7 0.6 copy-start.9
  105.8 0.6 copy-start.11
  106.4 119.0 %copy-start.2 = (f32[2,512,128]{2,1,0:T(8,128)}, f32[2,512,128]{2,1,0:T(8,128)S(1)}, u32[]{:S(2)}) copy-start(f32[2,512,128]{2,1,0:T(8,128)S(1)} %get-tuple-element.270) | copy-start | bytes 1572868
  106.4 202.1 %all-reduce.3.cloned.1.call-start = ((), (), s32[]{:S(2)}) async-start(), calls=%async_computation | async-start | bytes 1048576 | tf_op jit(solution)/shard_map/psum | solution.py:183
  239.3 10.5 %copy-start.7 = (f32[2,128,128]{2,0,1:T(2,128)S(1)}, f32[2,128,128]{2,0,1:T(2,128)}, u32[]{:S(2)}) copy-start(f32[2,128,128]{2,0,1:T(2,128)} %get-tuple-element.267) | copy-start | bytes 393220
Sparse Core Ops, SparseCore 0:
  10.7 72.5 all-gather.6
  106.5 128.1 all-gather.8
  238.2 70.2 all-reduce.2
where the time goes:
time: 323 us; the launch traced here: 317 us
  blocking collectives  144 us (45%)
  waiting for transfers between devices  108 us (33%)
  other arithmetic  19.4 us (6%)
  local copies, waits for them, and re-layouts  18.8 us (6%)
  between operations  13.9 us (4%)
  matrix products  11.5 us (4%)
    psum x1, blocking collectives, on_device(): summed_weight, summed_book = lax.psum((weight_term, book_here), 'seq')  114 us
    psum x1, waiting for transfers between devices, on_device(): summed_weight, summed_book = lax.psum((weight_term, book_here), 'seq')  57.8 us
    all_gather x2, waiting for transfers between devices, entering(): pieces = jax.tree.map(lambda part: lax.all_gather(part, axis), value)  50.4 us
    all_gather x1, blocking collectives, entering(): pieces = jax.tree.map(lambda part: lax.all_gather(part, axis), value)  22.2 us
    select_n x21, other arithmetic, turn(): jnp.where(position < mine, new, old)  17 us
    all_gather x1, blocking collectives, on_device(): full_grad = lax.all_gather(grad_out, 'head', axis=1, tiled=True)  7.49 us
  transfers between devices with their start and end apart: 3, of which 3 were waited for; matrix products, arithmetic and copies ran while one was open for 7% of the time, Pallas kernels for 0%

commit v1 on v0

--- a/solution.py
+++ b/solution.py
@@ -1,6 +1,10 @@
+import functools
+
 import jax
 import jax.numpy as jnp
 from jax import lax
+from jax.experimental import pallas as pl
+from jax.experimental.pallas import tpu as pltpu
 from jax.sharding import PartitionSpec as P
 
 BLOCK = 128
@@ -185,9 +189,269 @@
     return (from_blocks(grad_query), from_blocks(grad_values), summed_book, grad_weight)
 
 
+F32 = jnp.float32
+BF16 = jnp.bfloat16
+ANY = pl.BlockSpec(memory_space=pl.ANY)
+VMEM = pl.BlockSpec(memory_space=pltpu.VMEM)
+SMEM = pl.BlockSpec(memory_space=pltpu.SMEM)
+TILE = 256
+
+
+def dot_nn(a, b):
+    return lax.dot_general(a, b, (((1,), (0,)), ((), ())), preferred_element_type=F32)
+
+
+def dot_nt(a, b):
+    return lax.dot_general(a, b, (((1,), (1,)), ((), ())), preferred_element_type=F32)
+
+
+def dot_tn(a, b):
+    return lax.dot_general(a, b, (((0,), (0,)), ((), ())), preferred_element_type=F32)
+
+
+def slot_rows(me, slot, half, blocks):
+    outer = blocks // 2
+    z, y = me // 2, me % 2
+    block = lax.rem(z + outer - slot, outer) * 2 + jnp.where(half == 1, 1 - y, y)
+    return block
+
+
+def one_hot_rows(code_rows, block, head, code_total):
+    high = code_rows[block, 0:1, head * 2 * BLOCK : head * 2 * BLOCK + BLOCK].astype(F32)
+    low = code_rows[block, 0:1, head * 2 * BLOCK + BLOCK : (head + 1) * 2 * BLOCK].astype(F32)
+    code = (high * 2.0 + low).astype(jnp.int32)
+    rows = lax.broadcasted_iota(jnp.int32, (code_total, BLOCK), 0)
+    return jnp.where(rows == code, 1.0, 0.0).astype(BF16)
+
+
+def masked_exp(scores_t, offset_row, base):
+    weights = jnp.exp(scores_t - offset_row)
+    return weights
+
+
+def causal_tile():
+    key_at = lax.broadcasted_iota(jnp.int32, (TILE, TILE), 0)
+    query_at = lax.broadcasted_iota(jnp.int32, (TILE, TILE), 1)
+    return key_at <= query_at
+
+
+def forward_kernel(blocks, heads, width, code_total, me_ref, *refs):
+    slots = refs[:blocks]
+    book_ref = refs[blocks]
+    att_t_ref, lse_ref, q_ref, k_ref, v_ref, hot_ref = refs[blocks + 1 : blocks + 7]
+    codes_ref, v_t_ref, sems = refs[blocks + 7 :]
+    tokens = blocks * BLOCK
+    wide = heads * width
+    me = me_ref[0]
+    copies = []
+    for at in range(blocks):
+        block = slot_rows(me, at // 2, at % 2, blocks)
+        rows = pl.ds(pl.multiple_of(block * BLOCK, BLOCK), BLOCK)
+        source = slots[at]
+        copies.append(pltpu.make_async_copy(
+            source.at[pl.ds(BLOCK, BLOCK), pl.ds(0, wide)], q_ref.at[rows, :], sems.at[0, at]))
+        copies.append(pltpu.make_async_copy(
+            source.at[pl.ds(BLOCK, BLOCK), pl.ds(wide, wide)], v_ref.at[rows, :], sems.at[1, at]))
+        copies.append(pltpu.make_async_copy(
+            source.at[pl.ds(2 * BLOCK, 16), :], codes_ref.at[block], sems.at[2, at]))
+    for copy in copies:
+        copy.start()
+    for copy in copies:
+        copy.wait()
+    for head in range(heads):
+        columns = slice(head * width, (head + 1) * width)
+        for block in range(blocks):
+            hot = one_hot_rows(codes_ref, block, head, code_total)
+            hot_ref[head, :, block * BLOCK : (block + 1) * BLOCK] = hot
+        k_ref[:, columns] = dot_tn(hot_ref[head], book_ref[head]).astype(BF16)
+        v_t_ref[columns, :] = v_ref[:, columns].astype(F32).T.astype(BF16)
+    for head in range(heads):
+        columns = slice(head * width, (head + 1) * width)
+        for tile in range(tokens // TILE):
+            here = slice(tile * TILE, (tile + 1) * TILE)
+            seen = (tile + 1) * TILE
+            scores = dot_nt(k_ref[:seen, columns], q_ref[here, columns])
+            last = jnp.where(causal_tile(), scores[seen - TILE :], -jnp.inf)
+            scores = last if tile == 0 else jnp.concatenate([scores[: seen - TILE], last], axis=0)
+            top = jnp.max(scores, axis=0, keepdims=True)
+            weights = jnp.exp(scores - top)
+            total = jnp.sum(weights, axis=0, keepdims=True)
+            mixed = dot_nn(v_t_ref[columns, :seen], weights.astype(BF16))
+            att_t_ref[columns, here] = (mixed / total).astype(BF16)
+            lse_ref[head : head + 1, here] = top + jnp.log(total)
+
+
+def backward_kernel(blocks, heads, width, code_total, me_ref, quarter_ref, *refs):
+    grads = refs[: 4 * blocks]
+    (weight_ref, att_t_ref, lse_ref, q_ref, k_ref, v_ref, hot_ref) = refs[4 * blocks : 4 * blocks + 7]
+    (dq_ref, dv_ref, dbook_ref, dweight_ref) = refs[4 * blocks + 7 : 4 * blocks + 11]
+    (go_ref, do_t_ref, dk_ref, delta_ref, rows_ref, own_ref, sems) = refs[4 * blocks + 11 :]
+    tokens = blocks * BLOCK
+    part = grads[0].shape[1]
+    model = 4 * part
+    me = me_ref[0]
+    quarter = quarter_ref[0]
+    copies = []
+    for at in range(blocks):
+        block = slot_rows(me, at // 2, at % 2, blocks)
+        rows = pl.ds(pl.multiple_of(block * BLOCK, BLOCK), BLOCK)
+        for piece in range(4):
+            column = pl.multiple_of(jnp.bitwise_xor(quarter, piece) * part, part)
+            copies.append(pltpu.make_async_copy(
+                grads[4 * at + piece].at[pl.ds(0, BLOCK), :],
+                go_ref.at[rows, pl.ds(column, part)], sems.at[at, piece]))
+    for copy in copies:
+        copy.start()
+    for copy in copies:
+        copy.wait()
+
+    for tile in range(tokens // TILE):
+        here = slice(tile * TILE, (tile + 1) * TILE)
+        do_t_ref[:, here] = dot_nt(weight_ref[...], go_ref[here, :]).astype(BF16)
+
+    @pl.loop(0, model // TILE)
+    def _(step):
+        columns = pl.ds(pl.multiple_of(step * TILE, TILE), TILE)
+        dweight_ref[:, columns] = dot_nn(att_t_ref[...], go_ref[:, columns]).astype(BF16)
+
+    mine = pl.ds(pl.multiple_of(me * BLOCK, BLOCK), BLOCK)
+    for head in range(heads):
+        columns = slice(head * width, (head + 1) * width)
+        delta_ref[head : head + 1, :] = jnp.sum(
+            do_t_ref[columns, :].astype(F32) * att_t_ref[columns, :].astype(F32), axis=0, keepdims=True)
+        for tile in range(tokens // TILE):
+            here = slice(tile * TILE, (tile + 1) * TILE)
+            seen = (tile + 1) * TILE
+            scores = dot_nt(k_ref[:seen, columns], q_ref[here, columns])
+            weights = jnp.exp(scores - lse_ref[head : head + 1, here])
+            last = jnp.where(causal_tile(), weights[seen - TILE :], 0.0)
+            weights = last if tile == 0 else jnp.concatenate([weights[: seen - TILE], last], axis=0)
+            grad = dot_nn(v_ref[:seen, columns], do_t_ref[columns, here])
+            grad = (weights * (grad - delta_ref[head : head + 1, here])).astype(BF16)
+            term = dot_nn(grad, q_ref[here, columns])
+            if tile == 0:
+                dk_ref[:seen, :] = term
+            else:
+                dk_ref[: seen - TILE, :] += term[: seen - TILE]
+                dk_ref[seen - TILE : seen, :] = term[seen - TILE :]
+        dbook_ref[head] = dot_nn(hot_ref[head], dk_ref[...].astype(BF16))
+        scores = dot_nt(k_ref[mine, columns], q_ref[:, columns])
+        key_at = lax.broadcasted_iota(jnp.int32, (BLOCK, tokens), 0) + me * BLOCK
+        query_at = lax.broadcasted_iota(jnp.int32, (BLOCK, tokens), 1)
+        weights = jnp.exp(jnp.where(key_at <= query_at, scores - lse_ref[head : head + 1, :], -jnp.inf))
+        dv_ref[:, columns] = dot_nt(weights.astype(BF16), do_t_ref[columns, :]).astype(BF16)
+        for block in range(blocks):
+            span = slice(block * BLOCK, (block + 1) * BLOCK)
+            rows_ref[0, block : block + 1, :] = lse_ref[head : head + 1, span]
+            rows_ref[1, block : block + 1, :] = delta_ref[head : head + 1, span]
+            own_ref[block] = do_t_ref[columns, span]
+        own_lse = rows_ref[0, pl.ds(me, 1), :]
+        own_delta = rows_ref[1, pl.ds(me, 1), :]
+        scores = dot_nt(k_ref[:, columns], q_ref[mine, columns])
+        key_at = lax.broadcasted_iota(jnp.int32, (tokens, BLOCK), 0)
+        query_at = lax.broadcasted_iota(jnp.int32, (tokens, BLOCK), 1) + me * BLOCK
+        weights = jnp.exp(jnp.where(key_at <= query_at, scores - own_lse, -jnp.inf))
+        grad = dot_nn(v_ref[:, columns], own_ref[me])
+        grad = (weights * (grad - own_delta)).astype(BF16)
+        dq_ref[:, columns] = dot_tn(grad, k_ref[:, columns]).astype(BF16)
+
+
+def gathered_on_device(queries, values, codes, codebook, out_weight, grad_out):
+    blocks = lax.axis_size("seq")
+    tok_here, heads, width = queries.shape
+    code_total = codebook.shape[1]
+    wide = heads * width
+    part = grad_out.shape[1]
+    if tok_here != BLOCK or part != 2 * wide or 2 * wide != 4 * BLOCK:
+        raise ValueError("unexpected shapes")
+    tokens = blocks * BLOCK
+    outer = blocks // 2
+    me = lax.axis_index("seq").astype(jnp.int32).reshape(1)
+    quarter = lax.axis_index("head").astype(jnp.int32).reshape(1)
+
+    digits = jnp.stack([codes // 2, codes % 2], axis=1).astype(BF16).reshape(1, 4 * BLOCK)
+    payload = jnp.concatenate([
+        grad_out,
+        jnp.concatenate([queries.reshape(BLOCK, wide), values.reshape(BLOCK, wide)], axis=1),
+        jnp.broadcast_to(digits, (16, 4 * BLOCK)),
+    ], axis=0)
+
+    def along_z(array, step):
+        pairs = [(z * 2 + y, (z + step) % outer * 2 + y) for z in range(outer) for y in range(2)]
+        return lax.ppermute(array, "seq", pairs)
+
+    def along_y(array):
+        return lax.ppermute(array, "seq", [(i, i ^ 1) for i in range(blocks)])
+
+    def along_x(array):
+        return lax.ppermute(array, "head", [(i, i ^ 2) for i in range(4)])
+
+    def to_core(array):
+        return lax.ppermute(array, "head", [(i, i ^ 1) for i in range(4)])
+
+    slots = []
+    for step in range(outer):
+        held = payload if step == 0 else along_z(payload, step)
+        slots.append(held)
+        slots.append(along_y(held))
+    grads = []
+    for held in slots:
+        own = held[:BLOCK]
+        across = along_x(own)
+        grads += [own, to_core(own), across, to_core(across)]
+
+    q_all, k_all, v_all = (jax.ShapeDtypeStruct((tokens, wide), BF16),) * 3
+    att_t, lse, q_all, k_all, v_all, hot = pl.pallas_call(
+        functools.partial(forward_kernel, blocks, heads, width, code_total),
+        out_shape=(
+            jax.ShapeDtypeStruct((wide, tokens), BF16),
+            jax.ShapeDtypeStruct((8, tokens), F32),
+            q_all, k_all, v_all,
+            jax.ShapeDtypeStruct((heads, code_total, tokens), BF16),
+        ),
+        in_specs=[SMEM] + [ANY] * blocks + [VMEM],
+        out_specs=(VMEM,) * 6,
+        scratch_shapes=[
+            pltpu.VMEM((blocks, 16, 4 * BLOCK), BF16),
+            pltpu.VMEM((wide, tokens), BF16),
+            pltpu.SemaphoreType.DMA((3, blocks)),
+        ],
+        cost_estimate=pl.CostEstimate(flops=10**9, bytes_accessed=4 * 10**6, transcendentals=10**6),
+        name="forward",
+    )(me, *slots, codebook)
+
+    dq, dv, dbook, dweight = pl.pallas_call(
+        functools.partial(backward_kernel, blocks, heads, width, code_total),
+        out_shape=(
+            jax.ShapeDtypeStruct((BLOCK, wide), BF16),
+            jax.ShapeDtypeStruct((BLOCK, wide), BF16),
+            jax.ShapeDtypeStruct((heads, code_total, width), F32),
+            jax.ShapeDtypeStruct((wide, 4 * part), BF16),
+        ),
+        in_specs=[SMEM, SMEM] + [ANY] * (4 * blocks) + [VMEM] * 7,
+        out_specs=(VMEM,) * 4,
+        scratch_shapes=[
+            pltpu.VMEM((tokens, 4 * part), BF16),
+            pltpu.VMEM((wide, tokens), BF16),
+            pltpu.VMEM((tokens, width), F32),
+            pltpu.VMEM((8, tokens), F32),
+            pltpu.VMEM((2, blocks, BLOCK), F32),
+            pltpu.VMEM((blocks, width, BLOCK), BF16),
+            pltpu.SemaphoreType.DMA((blocks, 4)),
+        ],
+        cost_estimate=pl.CostEstimate(flops=4 * 10**9, bytes_accessed=8 * 10**6, transcendentals=10**6),
+        name="backward",
+    )(me, quarter, *grads, out_weight, att_t, lse, q_all, k_all, v_all, hot)
+    shape = (tok_here, heads, width)
+    return (dq.reshape(shape), dv.reshape(shape), dbook, dweight)
+
+
 def solution(mesh):
+    body = on_device
+    if mesh.shape["seq"] == 8 and mesh.shape["head"] == 4:
+        body = gathered_on_device
     return jax.shard_map(
-        on_device,
+        body,
         mesh=mesh,
         in_specs=(
             P("seq", "head", None),

time: 323 us -> 88.9 us (0.28); the launches traced: 317 us -> 88.5 us
  blocking collectives: 144 us -> 0 us
  waiting for transfers between devices: 108 us -> 27.7 us
  starting transfers between devices: 0.12 us -> 31.9 us
  Pallas kernels: 0 us -> 21.5 us
  other arithmetic: 19.4 us -> 1.63 us
  local copies, waits for them, and re-layouts: 18.8 us -> 4.56 us
  between operations: 13.9 us -> 1.09 us
  matrix products: 11.5 us -> 0 us
    psum x1 -> x0, blocking collectives: 114 us -> none  [on_device(): summed_weight, summed_book = lax.psum((weight_term, book_here), 'seq')]
    psum x1 -> x0, waiting for transfers between devices: 57.8 us -> none  [on_device(): summed_weight, summed_book = lax.psum((weight_term, book_here), 'seq')]
    all_gather x2 -> x0, waiting for transfers between devices: 50.4 us -> none  [entering(): pieces = jax.tree.map(lambda part: lax.all_gather(part, axis), value)]
    ppermute x0 -> x31, starting transfers between devices: none -> 31.9 us  [the longest x16 22.3 us: to_core(): return lax.ppermute(array, 'head', [(i, i ^ 1) for i in range(4)])]
    all_gather x2 -> x0, blocking collectives: 29.7 us -> none  [the longest x1 22.2 us: entering(): pieces = jax.tree.map(lambda part: lax.all_gather(part, axis), value)]
    ppermute x0 -> x31, waiting for transfers between devices: none -> 27.7 us  [the longest x3 15.9 us: along_z(): return lax.ppermute(array, 'seq', pairs)]
    pallas_call x0 -> x2, Pallas kernels: none -> 21.5 us  [the longest x1 13.8 us: gathered_on_device(): pl.pallas_call(functools.partial(backward_kernel, blocks, heads, width, c...]
    select_n x23 -> x0, other arithmetic: 17.1 us -> none  [the longest x21 17 us: turn(): jnp.where(position < mine, new, old)]
  transfers between devices with their start and end apart: 3 -> 31, of which waited for: 3 -> 9; matrix products, arithmetic and copies ran while one was open for 7% -> 0% of each run, Pallas kernels for 0% -> 9%
where the time goes in v1:
time: 88.9 us; the launch traced here: 88.5 us
  starting transfers between devices  31.9 us (36%)
  waiting for transfers between devices  27.7 us (31%)
  Pallas kernels  21.5 us (24%)
  local copies, waits for them, and re-layouts  4.56 us (5%)
  other arithmetic  1.63 us (2%)
  between operations  1.09 us (1%)
    ppermute x16, starting transfers between devices, to_core(): return lax.ppermute(array, 'head', [(i, i ^ 1) for i in range(4)])  22.3 us
    ppermute x3, waiting for transfers between devices, along_z(): return lax.ppermute(array, 'seq', pairs)  15.9 us
    pallas_call x1, Pallas kernels, gathered_on_device(): pl.pallas_call(functools.partial(backward_kernel, blocks, heads, width, c...  13.8 us
    ppermute x8, waiting for transfers between devices, along_x(): return lax.ppermute(array, 'head', [(i, i ^ 2) for i in range(4)])  10.4 us
    pallas_call x1, Pallas kernels, gathered_on_device(): pl.pallas_call(functools.partial(forward_kernel, blocks, heads, width, co...  7.73 us
    ppermute x8, starting transfers between devices, along_x(): return lax.ppermute(array, 'head', [(i, i ^ 2) for i in range(4)])  4.15 us
    ppermute x4, starting transfers between devices, along_y(): return lax.ppermute(array, 'seq', [(i, i ^ 1) for i in range(blocks)])  3.95 us
    reshape x2, local copies, waits for them, and re-layouts, gathered_on_device(): return (dq.reshape(shape), dv.reshape(shape), dbook, dweight)  2.98 us
  transfers between devices with their start and end apart: 31, of which 9 were waited for; matrix products, arithmetic and copies ran while one was open for 0% of the time, Pallas kernels for 9%

profile of v1, /device:TPU:27, one launch (start us, length us, event | category | flops | bytes accessed | tf_op | source)
XLA Modules:
  0.0 88.5 jit_solution(12348053536600620465)
XLA Ops:
  0.6 0.7 fusion.3
  1.3 0.9 %copy_bitcast_fusion = (bf16[128,256]{1,0:T(8,128)(2,1)S(1)}, bf16[128,256]{1,0:T(8,128)(2,1)S(1)}) fusion(bf16[16,8,2,128]{3,2,1,0:T(2,128)(2,1)} %bitcast.13, bf16[16,8,2,128]{3,2,1,0:T(2,128)(2,1)} %bitcast.14), kind=kLoop, calls=%fused_computation.1 | loop fusion | bytes 262144 | tf_op jit(solution)/shard_map/reshape | solution.py:375
  2.2 0.9 %pad_maximum_fusion.refs_0_ = bf16[272,512]{1,0:T(8,128)(2,1)S(1)} fusion(bf16[16,512]{1,0:T(8,128)(2,1)S(1)} %broadcast_in_dim.2, bf16[128,256]{1,0:T(8,128)(2,1)S(1)} %get-tuple-element.26, bf16[128,256]{1,0:T(8,128)(2,1)S(1)} %get-tuple-element.27, bf16[128,512]{1,0:T(8,128)(2,1)} %refs_0_.1), kind=kLoop, calls=%fused_computation | loop fusion | flops 1114112 | bytes 557056 | tf_op jit(solution)/shard_map/concatenate | solution.py:373
  3.3 1.3 %collective-permute-start.15 = (bf16[272,512]{1,0:T(8,128)(2,1)S(1)}, bf16[272,512]{1,0:T(8,128)(2,1)S(1)}, u32[]{:S(2)}, u32[]{:S(2)}) collective-permute-start(bf16[272,512]{1,0:T(8,128)(2,1)S(1)} %pad_maximum_fusion.refs_0_), channel_id=1, source_target_pairs={{0,16},{4,20},{8,24},{12,28},{16,0},{20,4},{24,8},{28,12},{1,17},{... | collective-permute-start | bytes 835592 | tf_op jit(solution)/shard_map/ppermute | solution.py:381
  5.0 1.2 %collective-permute-start.3 = (bf16[272,512]{1,0:T(8,128)(2,1)S(1)}, bf16[272,512]{1,0:T(8,128)(2,1)S(1)}, u32[]{:S(2)}, u32[]{:S(2)}) collective-permute-start(bf16[272,512]{1,0:T(8,128)(2,1)S(1)} %pad_maximum_fusion.refs_0_), channel_id=1, source_target_pairs={{0,4},{4,0},{8,12},{12,8},{16,20},{20,16},{24,28},{28,24},{1,5},{5... | collective-permute-start | bytes 835592 | tf_op jit(solution)/shard_map/ppermute | solution.py:384
  6.3 2.7 %collective-permute-done.1.refs_2_ = bf16[128,512]{1,0:T(8,128)(2,1)S(1)} collective-permute-done((bf16[128,512]{1,0:T(8,128)(2,1)}, bf16[128,512]{1,0:T(8,128)(2,1)S(1)}, u32[]{:S(2)}, u32[]{:S(2)}) %collective-permute-start.1) | collective-permute-done | bytes 131104 | tf_op jit(solution)/shard_map/ppermute | solution.py:387
  8.9 2.1 %collective-permute-start = (bf16[128,512]{1,0:T(8,128)(2,1)}, bf16[128,512]{1,0:T(8,128)(2,1)S(1)}, u32[]{:S(2)}, u32[]{:S(2)}) collective-permute-start(bf16[128,512]{1,0:T(8,128)(2,1)} %refs_0_.1), channel_id=1, source_target_pairs={{0,1},{1,0},{2,3},{3,2},{4,5},{5,4},{6,7},{7,6},{8,9},{9,8},{10,11... | collective-permute-start | bytes 393224 | tf_op jit(solution)/shard_map/ppermute | solution.py:390
  11.0 1.7 %collective-permute-start.2 = (bf16[128,512]{1,0:T(8,128)(2,1)S(1)}, bf16[128,512]{1,0:T(8,128)(2,1)S(1)}, u32[]{:S(2)}, u32[]{:S(2)}) collective-permute-start(bf16[128,512]{1,0:T(8,128)(2,1)S(1)} %collective-permute-done.1.refs_2_), channel_id=1, source_target_pairs={{0,1},{1,0},{2,3},{3,2},{4,5},{5,4},{6,7},{7,6},{8,9},{9,8},{10,11... | collective-permute-start | bytes 393224 | tf_op jit(solution)/shard_map/ppermute | solution.py:390
  12.7 15.9 %collective-permute-done.15.refs_4_ = bf16[272,512]{1,0:T(8,128)(2,1)S(1)} collective-permute-done((bf16[272,512]{1,0:T(8,128)(2,1)S(1)}, bf16[272,512]{1,0:T(8,128)(2,1)S(1)}, u32[]{:S(2)}, u32[]{:S(2)}) %collective-permute-start.15) | collective-permute-done | bytes 278560 | tf_op jit(solution)/shard_map/ppermute | solution.py:381
  28.9 1.3 %collective-permute-start.17 = (bf16[128,512]{1,0:T(8,128)(2,1)S(1)}, bf16[128,512]{1,0:T(8,128)(2,1)S(1)}, u32[]{:S(2)}, u32[]{:S(2)}) collective-permute-start(bf16[128,512]{1,0:T(8,128)(2,1)S(1)} %slice.31.refs_16_), channel_id=1, source_target_pairs={{0,2},{1,3},{2,0},{3,1},{4,6},{5,7},{6,4},{7,5},{8,10},{9,11},{10,... | collective-permute-start | bytes 393224 | tf_op jit(solution)/shard_map/ppermute | solution.py:387
  30.2 1.2 %collective-permute-start.11 = (bf16[272,512]{1,0:T(8,128)(2,1)S(1)}, bf16[272,512]{1,0:T(8,128)(2,1)S(1)}, u32[]{:S(2)}, u32[]{:S(2)}) collective-permute-start(bf16[272,512]{1,0:T(8,128)(2,1)S(1)} %collective-permute-done.7.refs_2_), channel_id=1, source_target_pairs={{0,4},{4,0},{8,12},{12,8},{16,20},{20,16},{24,28},{28,24},{1,5},{5... | collective-permute-start | bytes 835592 | tf_op jit(solution)/shard_map/ppermute | solution.py:384
  31.6 1.2 %collective-permute-start.27 = (bf16[272,512]{1,0:T(8,128)(2,1)S(1)}, bf16[272,512]{1,0:T(8,128)(2,1)S(1)}, u32[]{:S(2)}, u32[]{:S(2)}) collective-permute-start(bf16[272,512]{1,0:T(8,128)(2,1)S(1)} %collective-permute-done.23.refs_6_), channel_id=1, source_target_pairs={{0,4},{4,0},{8,12},{12,8},{16,20},{20,16},{24,28},{28,24},{1,5},{5... | collective-permute-start | bytes 835592 | tf_op jit(solution)/shard_map/ppermute | solution.py:384
  33.3 1.6 %collective-permute-done.17.refs_18_ = bf16[128,512]{1,0:T(8,128)(2,1)S(1)} collective-permute-done((bf16[128,512]{1,0:T(8,128)(2,1)S(1)}, bf16[128,512]{1,0:T(8,128)(2,1)S(1)}, u32[]{:S(2)}, u32[]{:S(2)}) %collective-permute-start.17) | collective-permute-done | bytes 131104 | tf_op jit(solution)/shard_map/ppermute | solution.py:387
  35.2 3.1 %collective-permute-done.25.refs_26_ = bf16[128,512]{1,0:T(8,128)(2,1)S(1)} collective-permute-done((bf16[128,512]{1,0:T(8,128)(2,1)S(1)}, bf16[128,512]{1,0:T(8,128)(2,1)S(1)}, u32[]{:S(2)}, u32[]{:S(2)}) %collective-permute-start.25) | collective-permute-done | bytes 131104 | tf_op jit(solution)/shard_map/ppermute | solution.py:387
  38.3 3.2 %collective-permute-start.16 = (bf16[128,512]{1,0:T(8,128)(2,1)S(1)}, bf16[128,512]{1,0:T(8,128)(2,1)S(1)}, u32[]{:S(2)}, u32[]{:S(2)}) collective-permute-start(bf16[128,512]{1,0:T(8,128)(2,1)S(1)} %slice.31.refs_16_), channel_id=1, source_target_pairs={{0,1},{1,0},{2,3},{3,2},{4,5},{5,4},{6,7},{7,6},{8,9},{9,8},{10,11... | collective-permute-start | bytes 393224 | tf_op jit(solution)/shard_map/ppermute | solution.py:390
  41.5 1.9 %collective-permute-start.24 = (bf16[128,512]{1,0:T(8,128)(2,1)S(1)}, bf16[128,512]{1,0:T(8,128)(2,1)S(1)}, u32[]{:S(2)}, u32[]{:S(2)}) collective-permute-start(bf16[128,512]{1,0:T(8,128)(2,1)S(1)} %slice.33.refs_24_), channel_id=1, source_target_pairs={{0,1},{1,0},{2,3},{3,2},{4,5},{5,4},{6,7},{7,6},{8,9},{9,8},{10,11... | collective-permute-start | bytes 393224 | tf_op jit(solution)/shard_map/ppermute | solution.py:390
  43.5 0.9 %collective-permute-done.24.refs_25_ = bf16[128,512]{1,0:T(8,128)(2,1)S(1)} collective-permute-done((bf16[128,512]{1,0:T(8,128)(2,1)S(1)}, bf16[128,512]{1,0:T(8,128)(2,1)S(1)}, u32[]{:S(2)}, u32[]{:S(2)}) %collective-permute-start.24) | collective-permute-done | bytes 131104 | tf_op jit(solution)/shard_map/ppermute | solution.py:390
  45.0 2.8 %collective-permute-start.18 = (bf16[128,512]{1,0:T(8,128)(2,1)S(1)}, bf16[128,512]{1,0:T(8,128)(2,1)S(1)}, u32[]{:S(2)}, u32[]{:S(2)}) collective-permute-start(bf16[128,512]{1,0:T(8,128)(2,1)S(1)} %collective-permute-done.17.refs_18_), channel_id=1, source_target_pairs={{0,1},{1,0},{2,3},{3,2},{4,5},{5,4},{6,7},{7,6},{8,9},{9,8},{10,11... | collective-permute-start | bytes 393224 | tf_op jit(solution)/shard_map/ppermute | solution.py:390
  48.2 2.9 %collective-permute-start.26 = (bf16[128,512]{1,0:T(8,128)(2,1)S(1)}, bf16[128,512]{1,0:T(8,128)(2,1)S(1)}, u32[]{:S(2)}, u32[]{:S(2)}) collective-permute-start(bf16[128,512]{1,0:T(8,128)(2,1)S(1)} %collective-permute-done.25.refs_26_), channel_id=1, source_target_pairs={{0,1},{1,0},{2,3},{3,2},{4,5},{5,4},{6,7},{7,6},{8,9},{9,8},{10,11... | collective-permute-start | bytes 393224 | tf_op jit(solution)/shard_map/ppermute | solution.py:390
  51.7 1.2 %collective-permute-start.21 = (bf16[128,512]{1,0:T(8,128)(2,1)S(1)}, bf16[128,512]{1,0:T(8,128)(2,1)}, u32[]{:S(2)}, u32[]{:S(2)}) collective-permute-start(bf16[128,512]{1,0:T(8,128)(2,1)S(1)} %slice.32.refs_20_), channel_id=1, source_target_pairs={{0,2},{1,3},{2,0},{3,1},{4,6},{5,7},{6,4},{7,5},{8,10},{9,11},{10,... | collective-permute-start | bytes 393224 | tf_op jit(solution)/shard_map/ppermute | solution.py:387
  53.2 1.3 %collective-permute-start.12 = (bf16[128,512]{1,0:T(8,128)(2,1)S(1)}, bf16[128,512]{1,0:T(8,128)(2,1)S(1)}, u32[]{:S(2)}, u32[]{:S(2)}) collective-permute-start(bf16[128,512]{1,0:T(8,128)(2,1)S(1)} %slice.30.refs_12_), channel_id=1, source_target_pairs={{0,1},{1,0},{2,3},{3,2},{4,5},{5,4},{6,7},{7,6},{8,9},{9,8},{10,11... | collective-permute-start | bytes 393224 | tf_op jit(solution)/shard_map/ppermute | solution.py:390
  54.5 1.7 %collective-permute-done.13.refs_14_ = bf16[128,512]{1,0:T(8,128)(2,1)} collective-permute-done((bf16[128,512]{1,0:T(8,128)(2,1)S(1)}, bf16[128,512]{1,0:T(8,128)(2,1)}, u32[]{:S(2)}, u32[]{:S(2)}) %collective-permute-start.13) | collective-permute-done | bytes 131104 | tf_op jit(solution)/shard_map/ppermute | solution.py:387
  56.2 2.1 %collective-permute-start.28 = (bf16[128,512]{1,0:T(8,128)(2,1)S(1)}, bf16[128,512]{1,0:T(8,128)(2,1)}, u32[]{:S(2)}, u32[]{:S(2)}) collective-permute-start(bf16[128,512]{1,0:T(8,128)(2,1)S(1)} %slice.34.refs_28_), channel_id=1, source_target_pairs={{0,1},{1,0},{2,3},{3,2},{4,5},{5,4},{6,7},{7,6},{8,9},{9,8},{10,11... | collective-permute-start | bytes 393224 | tf_op jit(solution)/shard_map/ppermute | solution.py:390
  58.3 0.7 collective-permute-done.21.refs_22_
  59.0 2.1 %collective-permute-start.14 = (bf16[128,512]{1,0:T(8,128)(2,1)}, bf16[128,512]{1,0:T(8,128)(2,1)}, u32[]{:S(2)}, u32[]{:S(2)}) collective-permute-start(bf16[128,512]{1,0:T(8,128)(2,1)} %collective-permute-done.13.refs_14_), channel_id=1, source_target_pairs={{0,1},{1,0},{2,3},{3,2},{4,5},{5,4},{6,7},{7,6},{8,9},{9,8},{10,11... | collective-permute-start | bytes 393224 | tf_op jit(solution)/shard_map/ppermute | solution.py:390
  61.1 0.7 collective-permute-done.29.refs_30_
  61.8 1.3 %collective-permute-start.22 = (bf16[128,512]{1,0:T(8,128)(2,1)}, bf16[128,512]{1,0:T(8,128)(2,1)}, u32[]{:S(2)}, u32[]{:S(2)}) collective-permute-start(bf16[128,512]{1,0:T(8,128)(2,1)} %collective-permute-done.21.refs_22_), channel_id=1, source_target_pairs={{0,1},{1,0},{2,3},{3,2},{4,5},{5,4},{6,7},{7,6},{8,9},{9,8},{10,11... | collective-permute-start | bytes 393224 | tf_op jit(solution)/shard_map/ppermute | solution.py:390
  63.3 0.5 copy-done.30
  63.8 7.7 %forward.1 = (bf16[256,1024]{1,0:T(8,128)(2,1)}, f32[8,1024]{1,0:T(8,128)}, bf16[1024,256]{1,0:T(8,128)(2,1)}, bf16[1024,256]{1,0:T(8,128)(2,1)}, bf16[1024,256]...) custom-call(s32[1]{0:T(128)} %bitcast.me_ref, bf16[272,512]{1,0:T(8,128)(2,1)} %copy-done, bf16[272,512]{1,0:T(8,128)(2,1)} %copy-done.11, ...), custom_call_target="tpu_custom_call" | custom-call | flops 1000000000 | bytes 4000000 | tf_op jit(solution)/shard_map/forward/pallas_call | solution.py:404
  71.7 13.8 %backward.1 = (bf16[128,256]{1,0:T(8,128)(2,1)}, bf16[128,256]{1,0:T(8,128)(2,1)}, f32[2,512,128]{2,1,0:T(8,128)}, bf16[256,2048]{1,0:T(8,128)(2,1)}) custom-call(s32[1]{0:T(128)} %bitcast.me_ref, s32[1]{0:T(128)} %bitcast.1.quarter_ref, bf16[128,512]{1,0:T(8,128)(2,1)} %refs_0_.1, bf16[128,512]{1,0:T(8,128)(2,1)} %copy-done.16, ...), custom_call_target="tpu_custom_call" | custom-call | flops 4000000000 | bytes 8000000 | tf_op jit(solution)/shard_map/backward/pallas_call | solution.py:423
  85.5 1.5 %reshape.37 = bf16[128,2,128]{2,1,0:T(2,128)(2,1)} reshape(bf16[128,256]{1,0:T(8,128)(2,1)} %get-tuple-element.20) | data formatting | bytes 131072 | tf_op jit(solution)/shard_map/reshape | solution.py:446
  87.0 1.5 %reshape.38 = bf16[128,2,128]{2,1,0:T(2,128)(2,1)} reshape(bf16[128,256]{1,0:T(8,128)(2,1)} %get-tuple-element.21) | data formatting | bytes 131072 | tf_op jit(solution)/shard_map/reshape | solution.py:446
  (109 shorter events, 3.7 us)
Async XLA Ops:
  3.2 7.8 %collective-permute-start.7 = (bf16[272,512]{1,0:T(8,128)(2,1)S(1)}, bf16[272,512]{1,0:T(8,128)(2,1)S(1)}, u32[]{:S(2)}, u32[]{:S(2)}) collective-permute-start(bf16[272,512]{1,0:T(8,128)(2,1)S(1)} %pad_maximum_fusion.refs_0_), channel_id=1, source_target_pairs={{0,8},{4,12},{8,16},{12,20},{16,24},{20,28},{24,0},{28,4},{1,9},{5... | collective-permute-start | bytes 835592 | tf_op jit(solution)/shard_map/ppermute | solution.py:381
  3.3 25.3 %collective-permute-start.15 = (bf16[272,512]{1,0:T(8,128)(2,1)S(1)}, bf16[272,512]{1,0:T(8,128)(2,1)S(1)}, u32[]{:S(2)}, u32[]{:S(2)}) collective-permute-start(bf16[272,512]{1,0:T(8,128)(2,1)S(1)} %pad_maximum_fusion.refs_0_), channel_id=1, source_target_pairs={{0,16},{4,20},{8,24},{12,28},{16,0},{20,4},{24,8},{28,12},{1,17},{... | collective-permute-start | bytes 835592 | tf_op jit(solution)/shard_map/ppermute | solution.py:381
  4.6 4.3 %collective-permute-start.1 = (bf16[128,512]{1,0:T(8,128)(2,1)}, bf16[128,512]{1,0:T(8,128)(2,1)S(1)}, u32[]{:S(2)}, u32[]{:S(2)}) collective-permute-start(bf16[128,512]{1,0:T(8,128)(2,1)} %refs_0_.1), channel_id=1, source_target_pairs={{0,2},{1,3},{2,0},{3,1},{4,6},{5,7},{6,4},{7,5},{8,10},{9,11},{10,... | collective-permute-start | bytes 393224 | tf_op jit(solution)/shard_map/ppermute | solution.py:387
  4.8 26.6 %collective-permute-start.23 = (bf16[272,512]{1,0:T(8,128)(2,1)S(1)}, bf16[272,512]{1,0:T(8,128)(2,1)S(1)}, u32[]{:S(2)}, u32[]{:S(2)}) collective-permute-start(bf16[272,512]{1,0:T(8,128)(2,1)S(1)} %pad_maximum_fusion.refs_0_), channel_id=1, source_target_pairs={{0,24},{4,28},{8,0},{12,4},{16,8},{20,12},{24,16},{28,20},{1,25},{... | collective-permute-start | bytes 835592 | tf_op jit(solution)/shard_map/ppermute | solution.py:381
  5.0 26.6 %collective-permute-start.3 = (bf16[272,512]{1,0:T(8,128)(2,1)S(1)}, bf16[272,512]{1,0:T(8,128)(2,1)S(1)}, u32[]{:S(2)}, u32[]{:S(2)}) collective-permute-start(bf16[272,512]{1,0:T(8,128)(2,1)S(1)} %pad_maximum_fusion.refs_0_), channel_id=1, source_target_pairs={{0,4},{4,0},{8,12},{12,8},{16,20},{20,16},{24,28},{28,24},{1,5},{5... | collective-permute-start | bytes 835592 | tf_op jit(solution)/shard_map/ppermute | solution.py:384
  8.9 62.7 %copy-start.15 = (bf16[128,512]{1,0:T(8,128)(2,1)}, bf16[128,512]{1,0:T(8,128)(2,1)S(1)}, u32[]{:S(2)}) copy-start(bf16[128,512]{1,0:T(8,128)(2,1)S(1)} %collective-permute-done.1.refs_2_) | copy-start | bytes 393220
  8.9 19.9 %collective-permute-start = (bf16[128,512]{1,0:T(8,128)(2,1)}, bf16[128,512]{1,0:T(8,128)(2,1)S(1)}, u32[]{:S(2)}, u32[]{:S(2)}) collective-permute-start(bf16[128,512]{1,0:T(8,128)(2,1)} %refs_0_.1), channel_id=1, source_target_pairs={{0,1},{1,0},{2,3},{3,2},{4,5},{5,4},{6,7},{7,6},{8,9},{9,8},{10,11... | collective-permute-start | bytes 393224 | tf_op jit(solution)/shard_map/ppermute | solution.py:390
  11.0 19.1 %collective-permute-start.2 = (bf16[128,512]{1,0:T(8,128)(2,1)S(1)}, bf16[128,512]{1,0:T(8,128)(2,1)S(1)}, u32[]{:S(2)}, u32[]{:S(2)}) collective-permute-start(bf16[128,512]{1,0:T(8,128)(2,1)S(1)} %collective-permute-done.1.refs_2_), channel_id=1, source_target_pairs={{0,1},{1,0},{2,3},{3,2},{4,5},{5,4},{6,7},{7,6},{8,9},{9,8},{10,11... | collective-permute-start | bytes 393224 | tf_op jit(solution)/shard_map/ppermute | solution.py:390
  28.6 4.4 %collective-permute-start.9 = (bf16[128,512]{1,0:T(8,128)(2,1)S(1)}, bf16[128,512]{1,0:T(8,128)(2,1)S(1)}, u32[]{:S(2)}, u32[]{:S(2)}) collective-permute-start(bf16[128,512]{1,0:T(8,128)(2,1)S(1)} %slice.29.refs_8_), channel_id=1, source_target_pairs={{0,2},{1,3},{2,0},{3,1},{4,6},{5,7},{6,4},{7,5},{8,10},{9,11},{10,... | collective-permute-start | bytes 393224 | tf_op jit(solution)/shard_map/ppermute | solution.py:387
  28.9 6.0 %collective-permute-start.17 = (bf16[128,512]{1,0:T(8,128)(2,1)S(1)}, bf16[128,512]{1,0:T(8,128)(2,1)S(1)}, u32[]{:S(2)}, u32[]{:S(2)}) collective-permute-start(bf16[128,512]{1,0:T(8,128)(2,1)S(1)} %slice.31.refs_16_), channel_id=1, source_target_pairs={{0,2},{1,3},{2,0},{3,1},{4,6},{5,7},{6,4},{7,5},{8,10},{9,11},{10,... | collective-permute-start | bytes 393224 | tf_op jit(solution)/shard_map/ppermute | solution.py:387
  30.2 14.6 %collective-permute-start.11 = (bf16[272,512]{1,0:T(8,128)(2,1)S(1)}, bf16[272,512]{1,0:T(8,128)(2,1)S(1)}, u32[]{:S(2)}, u32[]{:S(2)}) collective-permute-start(bf16[272,512]{1,0:T(8,128)(2,1)S(1)} %collective-permute-done.7.refs_2_), channel_id=1, source_target_pairs={{0,4},{4,0},{8,12},{12,8},{16,20},{20,16},{24,28},{28,24},{1,5},{5... | collective-permute-start | bytes 835592 | tf_op jit(solution)/shard_map/ppermute | solution.py:384
  31.4 13.6 %collective-permute-start.19 = (bf16[272,512]{1,0:T(8,128)(2,1)S(1)}, bf16[272,512]{1,0:T(8,128)(2,1)S(1)}, u32[]{:S(2)}, u32[]{:S(2)}) collective-permute-start(bf16[272,512]{1,0:T(8,128)(2,1)S(1)} %collective-permute-done.15.refs_4_), channel_id=1, source_target_pairs={{0,4},{4,0},{8,12},{12,8},{16,20},{20,16},{24,28},{28,24},{1,5},{5... | collective-permute-start | bytes 835592 | tf_op jit(solution)/shard_map/ppermute | solution.py:384
  31.6 16.6 %collective-permute-start.27 = (bf16[272,512]{1,0:T(8,128)(2,1)S(1)}, bf16[272,512]{1,0:T(8,128)(2,1)S(1)}, u32[]{:S(2)}, u32[]{:S(2)}) collective-permute-start(bf16[272,512]{1,0:T(8,128)(2,1)S(1)} %collective-permute-done.23.refs_6_), channel_id=1, source_target_pairs={{0,4},{4,0},{8,12},{12,8},{16,20},{20,16},{24,28},{28,24},{1,5},{5... | collective-permute-start | bytes 835592 | tf_op jit(solution)/shard_map/ppermute | solution.py:384
  32.9 5.4 %collective-permute-start.25 = (bf16[128,512]{1,0:T(8,128)(2,1)S(1)}, bf16[128,512]{1,0:T(8,128)(2,1)S(1)}, u32[]{:S(2)}, u32[]{:S(2)}) collective-permute-start(bf16[128,512]{1,0:T(8,128)(2,1)S(1)} %slice.33.refs_24_), channel_id=1, source_target_pairs={{0,2},{1,3},{2,0},{3,1},{4,6},{5,7},{6,4},{7,5},{8,10},{9,11},{10,... | collective-permute-start | bytes 393224 | tf_op jit(solution)/shard_map/ppermute | solution.py:387
  34.9 6.6 %collective-permute-start.5 = (bf16[128,512]{1,0:T(8,128)(2,1)S(1)}, bf16[128,512]{1,0:T(8,128)(2,1)S(1)}, u32[]{:S(2)}, u32[]{:S(2)}) collective-permute-start(bf16[128,512]{1,0:T(8,128)(2,1)S(1)} %slice.28.refs_4_), channel_id=1, source_target_pairs={{0,2},{1,3},{2,0},{3,1},{4,6},{5,7},{6,4},{7,5},{8,10},{9,11},{10,... | collective-permute-start | bytes 393224 | tf_op jit(solution)/shard_map/ppermute | solution.py:387
  38.3 5.1 %collective-permute-start.16 = (bf16[128,512]{1,0:T(8,128)(2,1)S(1)}, bf16[128,512]{1,0:T(8,128)(2,1)S(1)}, u32[]{:S(2)}, u32[]{:S(2)}) collective-permute-start(bf16[128,512]{1,0:T(8,128)(2,1)S(1)} %slice.31.refs_16_), channel_id=1, source_target_pairs={{0,1},{1,0},{2,3},{3,2},{4,5},{5,4},{6,7},{7,6},{8,9},{9,8},{10,11... | collective-permute-start | bytes 393224 | tf_op jit(solution)/shard_map/ppermute | solution.py:390
  41.5 2.9 %collective-permute-start.24 = (bf16[128,512]{1,0:T(8,128)(2,1)S(1)}, bf16[128,512]{1,0:T(8,128)(2,1)S(1)}, u32[]{:S(2)}, u32[]{:S(2)}) collective-permute-start(bf16[128,512]{1,0:T(8,128)(2,1)S(1)} %slice.33.refs_24_), channel_id=1, source_target_pairs={{0,1},{1,0},{2,3},{3,2},{4,5},{5,4},{6,7},{7,6},{8,9},{9,8},{10,11... | collective-permute-start | bytes 393224 | tf_op jit(solution)/shard_map/ppermute | solution.py:390
  43.5 7.8 %collective-permute-start.8 = (bf16[128,512]{1,0:T(8,128)(2,1)S(1)}, bf16[128,512]{1,0:T(8,128)(2,1)S(1)}, u32[]{:S(2)}, u32[]{:S(2)}) collective-permute-start(bf16[128,512]{1,0:T(8,128)(2,1)S(1)} %slice.29.refs_8_), channel_id=1, source_target_pairs={{0,1},{1,0},{2,3},{3,2},{4,5},{5,4},{6,7},{7,6},{8,9},{9,8},{10,11... | collective-permute-start | bytes 393224 | tf_op jit(solution)/shard_map/ppermute | solution.py:390
  44.4 6.9 %collective-permute-start.4 = (bf16[128,512]{1,0:T(8,128)(2,1)S(1)}, bf16[128,512]{1,0:T(8,128)(2,1)S(1)}, u32[]{:S(2)}, u32[]{:S(2)}) collective-permute-start(bf16[128,512]{1,0:T(8,128)(2,1)S(1)} %slice.28.refs_4_), channel_id=1, source_target_pairs={{0,1},{1,0},{2,3},{3,2},{4,5},{5,4},{6,7},{7,6},{8,9},{9,8},{10,11... | collective-permute-start | bytes 393224 | tf_op jit(solution)/shard_map/ppermute | solution.py:390
  44.8 6.9 %collective-permute-start.10 = (bf16[128,512]{1,0:T(8,128)(2,1)S(1)}, bf16[128,512]{1,0:T(8,128)(2,1)S(1)}, u32[]{:S(2)}, u32[]{:S(2)}) collective-permute-start(bf16[128,512]{1,0:T(8,128)(2,1)S(1)} %collective-permute-done.9.refs_10_), channel_id=1, source_target_pairs={{0,1},{1,0},{2,3},{3,2},{4,5},{5,4},{6,7},{7,6},{8,9},{9,8},{10,11... | collective-permute-start | bytes 393224 | tf_op jit(solution)/shard_map/ppermute | solution.py:390
  45.0 8.0 %collective-permute-start.18 = (bf16[128,512]{1,0:T(8,128)(2,1)S(1)}, bf16[128,512]{1,0:T(8,128)(2,1)S(1)}, u32[]{:S(2)}, u32[]{:S(2)}) collective-permute-start(bf16[128,512]{1,0:T(8,128)(2,1)S(1)} %collective-permute-done.17.refs_18_), channel_id=1, source_target_pairs={{0,1},{1,0},{2,3},{3,2},{4,5},{5,4},{6,7},{7,6},{8,9},{9,8},{10,11... | collective-permute-start | bytes 393224 | tf_op jit(solution)/shard_map/ppermute | solution.py:390
  48.2 5.0 %collective-permute-start.26 = (bf16[128,512]{1,0:T(8,128)(2,1)S(1)}, bf16[128,512]{1,0:T(8,128)(2,1)S(1)}, u32[]{:S(2)}, u32[]{:S(2)}) collective-permute-start(bf16[128,512]{1,0:T(8,128)(2,1)S(1)} %collective-permute-done.25.refs_26_), channel_id=1, source_target_pairs={{0,1},{1,0},{2,3},{3,2},{4,5},{5,4},{6,7},{7,6},{8,9},{9,8},{10,11... | collective-permute-start | bytes 393224 | tf_op jit(solution)/shard_map/ppermute | solution.py:390
  51.3 3.2 %collective-permute-start.6 = (bf16[128,512]{1,0:T(8,128)(2,1)S(1)}, bf16[128,512]{1,0:T(8,128)(2,1)S(1)}, u32[]{:S(2)}, u32[]{:S(2)}) collective-permute-start(bf16[128,512]{1,0:T(8,128)(2,1)S(1)} %collective-permute-done.5.refs_6_), channel_id=1, source_target_pairs={{0,1},{1,0},{2,3},{3,2},{4,5},{5,4},{6,7},{7,6},{8,9},{9,8},{10,11... | collective-permute-start | bytes 393224 | tf_op jit(solution)/shard_map/ppermute | solution.py:390
  51.4 4.8 %collective-permute-start.13 = (bf16[128,512]{1,0:T(8,128)(2,1)S(1)}, bf16[128,512]{1,0:T(8,128)(2,1)}, u32[]{:S(2)}, u32[]{:S(2)}) collective-permute-start(bf16[128,512]{1,0:T(8,128)(2,1)S(1)} %slice.30.refs_12_), channel_id=1, source_target_pairs={{0,2},{1,3},{2,0},{3,1},{4,6},{5,7},{6,4},{7,5},{8,10},{9,11},{10,... | collective-permute-start | bytes 393224 | tf_op jit(solution)/shard_map/ppermute | solution.py:387
  51.7 7.3 %collective-permute-start.21 = (bf16[128,512]{1,0:T(8,128)(2,1)S(1)}, bf16[128,512]{1,0:T(8,128)(2,1)}, u32[]{:S(2)}, u32[]{:S(2)}) collective-permute-start(bf16[128,512]{1,0:T(8,128)(2,1)S(1)} %slice.32.refs_20_), channel_id=1, source_target_pairs={{0,2},{1,3},{2,0},{3,1},{4,6},{5,7},{6,4},{7,5},{8,10},{9,11},{10,... | collective-permute-start | bytes 393224 | tf_op jit(solution)/shard_map/ppermute | solution.py:387
  52.9 8.9 %collective-permute-start.29 = (bf16[128,512]{1,0:T(8,128)(2,1)S(1)}, bf16[128,512]{1,0:T(8,128)(2,1)}, u32[]{:S(2)}, u32[]{:S(2)}) collective-permute-start(bf16[128,512]{1,0:T(8,128)(2,1)S(1)} %slice.34.refs_28_), channel_id=1, source_target_pairs={{0,2},{1,3},{2,0},{3,1},{4,6},{5,7},{6,4},{7,5},{8,10},{9,11},{10,... | collective-permute-start | bytes 393224 | tf_op jit(solution)/shard_map/ppermute | solution.py:387
  53.2 9.9 %collective-permute-start.12 = (bf16[128,512]{1,0:T(8,128)(2,1)S(1)}, bf16[128,512]{1,0:T(8,128)(2,1)S(1)}, u32[]{:S(2)}, u32[]{:S(2)}) collective-permute-start(bf16[128,512]{1,0:T(8,128)(2,1)S(1)} %slice.30.refs_12_), channel_id=1, source_target_pairs={{0,1},{1,0},{2,3},{3,2},{4,5},{5,4},{6,7},{7,6},{8,9},{9,8},{10,11... | collective-permute-start | bytes 393224 | tf_op jit(solution)/shard_map/ppermute | solution.py:390
  54.4 17.1 %collective-permute-start.20 = (bf16[128,512]{1,0:T(8,128)(2,1)S(1)}, bf16[128,512]{1,0:T(8,128)(2,1)}, u32[]{:S(2)}, u32[]{:S(2)}) collective-permute-start(bf16[128,512]{1,0:T(8,128)(2,1)S(1)} %slice.32.refs_20_), channel_id=1, source_target_pairs={{0,1},{1,0},{2,3},{3,2},{4,5},{5,4},{6,7},{7,6},{8,9},{9,8},{10,11... | collective-permute-start | bytes 393224 | tf_op jit(solution)/shard_map/ppermute | solution.py:390
  56.2 15.4 %collective-permute-start.28 = (bf16[128,512]{1,0:T(8,128)(2,1)S(1)}, bf16[128,512]{1,0:T(8,128)(2,1)}, u32[]{:S(2)}, u32[]{:S(2)}) collective-permute-start(bf16[128,512]{1,0:T(8,128)(2,1)S(1)} %slice.34.refs_28_), channel_id=1, source_target_pairs={{0,1},{1,0},{2,3},{3,2},{4,5},{5,4},{6,7},{7,6},{8,9},{9,8},{10,11... | collective-permute-start | bytes 393224 | tf_op jit(solution)/shard_map/ppermute | solution.py:390
  59.0 12.6 %collective-permute-start.14 = (bf16[128,512]{1,0:T(8,128)(2,1)}, bf16[128,512]{1,0:T(8,128)(2,1)}, u32[]{:S(2)}, u32[]{:S(2)}) collective-permute-start(bf16[128,512]{1,0:T(8,128)(2,1)} %collective-permute-done.13.refs_14_), channel_id=1, source_target_pairs={{0,1},{1,0},{2,3},{3,2},{4,5},{5,4},{6,7},{7,6},{8,9},{9,8},{10,11... | collective-permute-start | bytes 393224 | tf_op jit(solution)/shard_map/ppermute | solution.py:390
  61.8 9.8 %collective-permute-start.22 = (bf16[128,512]{1,0:T(8,128)(2,1)}, bf16[128,512]{1,0:T(8,128)(2,1)}, u32[]{:S(2)}, u32[]{:S(2)}) collective-permute-start(bf16[128,512]{1,0:T(8,128)(2,1)} %collective-permute-done.21.refs_22_), channel_id=1, source_target_pairs={{0,1},{1,0},{2,3},{3,2},{4,5},{5,4},{6,7},{7,6},{8,9},{9,8},{10,11... | collective-permute-start | bytes 393224 | tf_op jit(solution)/shard_map/ppermute | solution.py:390
  63.1 8.5 %collective-permute-start.30 = (bf16[128,512]{1,0:T(8,128)(2,1)}, bf16[128,512]{1,0:T(8,128)(2,1)}, u32[]{:S(2)}, u32[]{:S(2)}) collective-permute-start(bf16[128,512]{1,0:T(8,128)(2,1)} %collective-permute-done.29.refs_30_), channel_id=1, source_target_pairs={{0,1},{1,0},{2,3},{3,2},{4,5},{5,4},{6,7},{7,6},{8,9},{9,8},{10,11... | collective-permute-start | bytes 393224 | tf_op jit(solution)/shard_map/ppermute | solution.py:390
  (30 other events, 772.2 us)

commit v2 on v1

--- a/solution.py
+++ b/solution.py
@@ -6,6 +6,7 @@
 from jax.experimental import pallas as pl
 from jax.experimental.pallas import tpu as pltpu
 from jax.sharding import PartitionSpec as P
+
 
 BLOCK = 128
 
@@ -205,28 +206,16 @@
     return lax.dot_general(a, b, (((1,), (1,)), ((), ())), preferred_element_type=F32)
 
 
-def dot_tn(a, b):
-    return lax.dot_general(a, b, (((0,), (0,)), ((), ())), preferred_element_type=F32)
-
-
-def slot_rows(me, slot, half, blocks):
-    outer = blocks // 2
-    z, y = me // 2, me % 2
-    block = lax.rem(z + outer - slot, outer) * 2 + jnp.where(half == 1, 1 - y, y)
-    return block
-
-
-def one_hot_rows(code_rows, block, head, code_total):
-    high = code_rows[block, 0:1, head * 2 * BLOCK : head * 2 * BLOCK + BLOCK].astype(F32)
-    low = code_rows[block, 0:1, head * 2 * BLOCK + BLOCK : (head + 1) * 2 * BLOCK].astype(F32)
-    code = (high * 2.0 + low).astype(jnp.int32)
-    rows = lax.broadcasted_iota(jnp.int32, (code_total, BLOCK), 0)
-    return jnp.where(rows == code, 1.0, 0.0).astype(BF16)
-
-
-def masked_exp(scores_t, offset_row, base):
-    weights = jnp.exp(scores_t - offset_row)
-    return weights
+def slot_block(me, slot, half):
+    return jnp.bitwise_xor(me, 2 * slot + half)
+
+
+def by_head(rows, flip):
+    token_major = lax.broadcasted_iota(jnp.int32, (2 * rows, 2 * rows), 1 - flip)
+    head_major = lax.broadcasted_iota(jnp.int32, (2 * rows, 2 * rows), flip)
+    head = jnp.where(head_major >= rows, 1, 0)
+    same = token_major == 2 * (head_major - rows * head) + head
+    return jnp.where(same, 1.0, 0.0).astype(BF16)
 
 
 def causal_tile():
@@ -235,35 +224,76 @@
     return key_at <= query_at
 
 
-def forward_kernel(blocks, heads, width, code_total, me_ref, *refs):
+def pack_kernel(query_ref, value_ref, code_ref, out_ref):
+    rows = code_ref.shape[1]
+    width = query_ref.shape[1]
+    both = jnp.concatenate([query_ref[...], value_ref[...]], axis=1)
+    both = dot_nn(by_head(rows, 0), both).astype(BF16)
+    for head in range(2):
+        for which in range(2):
+            column = (2 * which + head) * width
+            out_ref[:rows, column : column + width] = both[
+                head * rows : (head + 1) * rows, which * width : (which + 1) * width]
+        code = code_ref[head : head + 1, :]
+        high = lax.shift_right_logical(code, 1)
+        for digit, at in ((high, 2 * head), (code - 2 * high, 2 * head + 1)):
+            digit = jnp.broadcast_to(digit.astype(F32), (16, rows)).astype(BF16)
+            out_ref[rows : rows + 16, at * rows : (at + 1) * rows] = digit
+
+
+def main_kernel(blocks, heads, width, code_total, me_ref, quarter_ref, *refs):
     slots = refs[:blocks]
-    book_ref = refs[blocks]
-    att_t_ref, lse_ref, q_ref, k_ref, v_ref, hot_ref = refs[blocks + 1 : blocks + 7]
-    codes_ref, v_t_ref, sems = refs[blocks + 7 :]
+    grads = refs[blocks : 5 * blocks]
+    book_any, weight_any = refs[5 * blocks : 5 * blocks + 2]
+    dq_ref, dv_ref, dbook_any, dweight_any = refs[5 * blocks + 2 : 5 * blocks + 6]
+    (q_ref, k_ref, v_ref, k_t_ref, v_t_ref, hot_ref, codes_ref, att_t_ref, lse_ref, weight_ref, go_ref,
+     do_t_ref, dk_ref, delta_ref, rows_ref, own_ref, dbook_ref, dweight_ref, book_ref, sems, go_sems, out_sems,
+     ) = refs[5 * blocks + 6 :]
     tokens = blocks * BLOCK
     wide = heads * width
+    part = grads[0].shape[1]
+    model = 4 * part
     me = me_ref[0]
-    copies = []
+    quarter = quarter_ref[0]
+
+    inputs, late = [pltpu.make_async_copy(book_any, book_ref, out_sems.at[2 + heads])], []
     for at in range(blocks):
-        block = slot_rows(me, at // 2, at % 2, blocks)
+        block = slot_block(me, at // 2, at % 2)
         rows = pl.ds(pl.multiple_of(block * BLOCK, BLOCK), BLOCK)
         source = slots[at]
-        copies.append(pltpu.make_async_copy(
-            source.at[pl.ds(BLOCK, BLOCK), pl.ds(0, wide)], q_ref.at[rows, :], sems.at[0, at]))
-        copies.append(pltpu.make_async_copy(
-            source.at[pl.ds(BLOCK, BLOCK), pl.ds(wide, wide)], v_ref.at[rows, :], sems.at[1, at]))
-        copies.append(pltpu.make_async_copy(
-            source.at[pl.ds(2 * BLOCK, 16), :], codes_ref.at[block], sems.at[2, at]))
-    for copy in copies:
+        inputs.append(pltpu.make_async_copy(
+            source.at[pl.ds(BLOCK, 16), :], codes_ref.at[block], sems.at[2, at]))
+        inputs.append(pltpu.make_async_copy(
+            source.at[pl.ds(0, BLOCK), pl.ds(0, wide)], q_ref.at[rows, :], sems.at[0, at]))
+        inputs.append(pltpu.make_async_copy(
+            source.at[pl.ds(0, BLOCK), pl.ds(wide, wide)], v_ref.at[rows, :], sems.at[1, at]))
+    late.append(pltpu.make_async_copy(weight_any, weight_ref, out_sems.at[0]))
+    for at in range(blocks):
+        block = slot_block(me, at // 2, at % 2)
+        rows = pl.ds(pl.multiple_of(block * BLOCK, BLOCK), BLOCK)
+        for piece in range(4):
+            column = pl.multiple_of(jnp.bitwise_xor(quarter, piece) * part, part)
+            late.append(pltpu.make_async_copy(
+                grads[4 * at + piece].at[pl.ds(0, BLOCK), :],
+                go_ref.at[rows, pl.ds(column, part)], go_sems.at[at, piece]))
+    for copy in inputs + late:
         copy.start()
-    for copy in copies:
+    for copy in inputs:
         copy.wait()
+
     for head in range(heads):
         columns = slice(head * width, (head + 1) * width)
         for block in range(blocks):
-            hot = one_hot_rows(codes_ref, block, head, code_total)
+            at = head * 2 * BLOCK
+            high = codes_ref[block, 0:1, at : at + BLOCK].astype(F32)
+            low = codes_ref[block, 0:1, at + BLOCK : at + 2 * BLOCK].astype(F32)
+            code = (high * 2.0 + low).astype(jnp.int32)
+            rows = lax.broadcasted_iota(jnp.int32, (code_total, BLOCK), 0)
+            hot = jnp.where(rows == code, 1.0, 0.0).astype(BF16)
             hot_ref[head, :, block * BLOCK : (block + 1) * BLOCK] = hot
-        k_ref[:, columns] = dot_tn(hot_ref[head], book_ref[head]).astype(BF16)
+        key_t = dot_nn(book_ref[head].astype(F32).T.astype(BF16), hot_ref[head])
+        k_t_ref[columns, :] = key_t.astype(BF16)
+        k_ref[:, columns] = key_t.T.astype(BF16)
         v_t_ref[columns, :] = v_ref[:, columns].astype(F32).T.astype(BF16)
     for head in range(heads):
         columns = slice(head * width, (head + 1) * width)
@@ -280,41 +310,19 @@
             att_t_ref[columns, here] = (mixed / total).astype(BF16)
             lse_ref[head : head + 1, here] = top + jnp.log(total)
 
-
-def backward_kernel(blocks, heads, width, code_total, me_ref, quarter_ref, *refs):
-    grads = refs[: 4 * blocks]
-    (weight_ref, att_t_ref, lse_ref, q_ref, k_ref, v_ref, hot_ref) = refs[4 * blocks : 4 * blocks + 7]
-    (dq_ref, dv_ref, dbook_ref, dweight_ref) = refs[4 * blocks + 7 : 4 * blocks + 11]
-    (go_ref, do_t_ref, dk_ref, delta_ref, rows_ref, own_ref, sems) = refs[4 * blocks + 11 :]
-    tokens = blocks * BLOCK
-    part = grads[0].shape[1]
-    model = 4 * part
-    me = me_ref[0]
-    quarter = quarter_ref[0]
-    copies = []
-    for at in range(blocks):
-        block = slot_rows(me, at // 2, at % 2, blocks)
-        rows = pl.ds(pl.multiple_of(block * BLOCK, BLOCK), BLOCK)
-        for piece in range(4):
-            column = pl.multiple_of(jnp.bitwise_xor(quarter, piece) * part, part)
-            copies.append(pltpu.make_async_copy(
-                grads[4 * at + piece].at[pl.ds(0, BLOCK), :],
-                go_ref.at[rows, pl.ds(column, part)], sems.at[at, piece]))
-    for copy in copies:
-        copy.start()
-    for copy in copies:
+    for copy in late:
         copy.wait()
-
+    for tile in range(model // TILE):
+        columns = slice(tile * TILE, (tile + 1) * TILE)
+        dweight_ref[:, columns] = dot_nn(att_t_ref[...], go_ref[:, columns]).astype(BF16)
+    outputs = [pltpu.make_async_copy(dweight_ref, dweight_any, out_sems.at[1])]
+    outputs[0].start()
     for tile in range(tokens // TILE):
         here = slice(tile * TILE, (tile + 1) * TILE)
         do_t_ref[:, here] = dot_nt(weight_ref[...], go_ref[here, :]).astype(BF16)
 
-    @pl.loop(0, model // TILE)
-    def _(step):
-        columns = pl.ds(pl.multiple_of(step * TILE, TILE), TILE)
-        dweight_ref[:, columns] = dot_nn(att_t_ref[...], go_ref[:, columns]).astype(BF16)
-
     mine = pl.ds(pl.multiple_of(me * BLOCK, BLOCK), BLOCK)
+    dq_heads, dv_heads = [], []
     for head in range(heads):
         columns = slice(head * width, (head + 1) * width)
         delta_ref[head : head + 1, :] = jnp.sum(
@@ -335,11 +343,13 @@
                 dk_ref[: seen - TILE, :] += term[: seen - TILE]
                 dk_ref[seen - TILE : seen, :] = term[seen - TILE :]
         dbook_ref[head] = dot_nn(hot_ref[head], dk_ref[...].astype(BF16))
+        outputs.append(pltpu.make_async_copy(dbook_ref.at[head], dbook_any.at[head], out_sems.at[2 + head]))
+        outputs[-1].start()
         scores = dot_nt(k_ref[mine, columns], q_ref[:, columns])
         key_at = lax.broadcasted_iota(jnp.int32, (BLOCK, tokens), 0) + me * BLOCK
         query_at = lax.broadcasted_iota(jnp.int32, (BLOCK, tokens), 1)
         weights = jnp.exp(jnp.where(key_at <= query_at, scores - lse_ref[head : head + 1, :], -jnp.inf))
-        dv_ref[:, columns] = dot_nt(weights.astype(BF16), do_t_ref[columns, :]).astype(BF16)
+        dv_heads.append(dot_nt(weights.astype(BF16), do_t_ref[columns, :]).astype(BF16))
         for block in range(blocks):
             span = slice(block * BLOCK, (block + 1) * BLOCK)
             rows_ref[0, block : block + 1, :] = lse_ref[head : head + 1, span]
@@ -353,10 +363,19 @@
         weights = jnp.exp(jnp.where(key_at <= query_at, scores - own_lse, -jnp.inf))
         grad = dot_nn(v_ref[:, columns], own_ref[me])
         grad = (weights * (grad - own_delta)).astype(BF16)
-        dq_ref[:, columns] = dot_tn(grad, k_ref[:, columns]).astype(BF16)
-
-
-def gathered_on_device(queries, values, codes, codebook, out_weight, grad_out):
+        dq_heads.append(dot_nn(k_t_ref[columns, :], grad).T.astype(BF16))
+    mix = by_head(BLOCK, 1)
+    dq_ref[...] = dot_nn(mix, jnp.concatenate(dq_heads, axis=0)).astype(BF16)
+    dv_ref[...] = dot_nn(mix, jnp.concatenate(dv_heads, axis=0)).astype(BF16)
+    for copy in outputs:
+        copy.wait()
+
+
+def gathered_on_device(*arrays):
+    return gathered_body(*arrays)
+
+
+def gathered_body(queries, values, codes, codebook, out_weight, grad_out):
     blocks = lax.axis_size("seq")
     tok_here, heads, width = queries.shape
     code_total = codebook.shape[1]
@@ -365,90 +384,86 @@
     if tok_here != BLOCK or part != 2 * wide or 2 * wide != 4 * BLOCK:
         raise ValueError("unexpected shapes")
     tokens = blocks * BLOCK
-    outer = blocks // 2
     me = lax.axis_index("seq").astype(jnp.int32).reshape(1)
     quarter = lax.axis_index("head").astype(jnp.int32).reshape(1)
 
-    digits = jnp.stack([codes // 2, codes % 2], axis=1).astype(BF16).reshape(1, 4 * BLOCK)
-    payload = jnp.concatenate([
-        grad_out,
-        jnp.concatenate([queries.reshape(BLOCK, wide), values.reshape(BLOCK, wide)], axis=1),
-        jnp.broadcast_to(digits, (16, 4 * BLOCK)),
-    ], axis=0)
-
-    def along_z(array, step):
-        pairs = [(z * 2 + y, (z + step) % outer * 2 + y) for z in range(outer) for y in range(2)]
-        return lax.ppermute(array, "seq", pairs)
-
-    def along_y(array):
-        return lax.ppermute(array, "seq", [(i, i ^ 1) for i in range(blocks)])
-
-    def along_x(array):
-        return lax.ppermute(array, "head", [(i, i ^ 2) for i in range(4)])
-
-    def to_core(array):
-        return lax.ppermute(array, "head", [(i, i ^ 1) for i in range(4)])
-
-    slots = []
-    for step in range(outer):
-        held = payload if step == 0 else along_z(payload, step)
-        slots.append(held)
-        slots.append(along_y(held))
+    payload = pl.pallas_call(
+        pack_kernel,
+        out_shape=jax.ShapeDtypeStruct((BLOCK + 16, part), BF16),
+        in_specs=[VMEM] * 3,
+        out_specs=VMEM,
+        name="pack",
+    )(queries.reshape(heads * BLOCK, width), values.reshape(heads * BLOCK, width), codes)
+
+    def exchange(array, axis, flip):
+        pairs = [(i, i ^ flip) for i in range(lax.axis_size(axis))]
+        return lax.ppermute(array, axis, pairs)
+
+    def along_seq(array):
+        near = exchange(array, "seq", 2)
+        far = exchange(array, "seq", 4)
+        held = []
+        for block in (array, near, far, exchange(far, "seq", 2)):
+            held += [block, exchange(block, "seq", 1)]
+        return held
+
+    slots = along_seq(payload)
     grads = []
-    for held in slots:
-        own = held[:BLOCK]
-        across = along_x(own)
-        grads += [own, to_core(own), across, to_core(across)]
-
-    q_all, k_all, v_all = (jax.ShapeDtypeStruct((tokens, wide), BF16),) * 3
-    att_t, lse, q_all, k_all, v_all, hot = pl.pallas_call(
-        functools.partial(forward_kernel, blocks, heads, width, code_total),
+    for own in along_seq(grad_out):
+        across = exchange(own, "head", 2)
+        grads += [own, exchange(own, "head", 1), across, exchange(across, "head", 1)]
+
+    main = pl.pallas_call(
+        functools.partial(main_kernel, blocks, heads, width, code_total),
         out_shape=(
-            jax.ShapeDtypeStruct((wide, tokens), BF16),
-            jax.ShapeDtypeStruct((8, tokens), F32),
-            q_all, k_all, v_all,
-            jax.ShapeDtypeStruct((heads, code_total, tokens), BF16),
-        ),
-        in_specs=[SMEM] + [ANY] * blocks + [VMEM],
-        out_specs=(VMEM,) * 6,
-        scratch_shapes=[
-            pltpu.VMEM((blocks, 16, 4 * BLOCK), BF16),
-            pltpu.VMEM((wide, tokens), BF16),
-            pltpu.SemaphoreType.DMA((3, blocks)),
-        ],
-        cost_estimate=pl.CostEstimate(flops=10**9, bytes_accessed=4 * 10**6, transcendentals=10**6),
-        name="forward",
-    )(me, *slots, codebook)
-
-    dq, dv, dbook, dweight = pl.pallas_call(
-        functools.partial(backward_kernel, blocks, heads, width, code_total),
-        out_shape=(
-            jax.ShapeDtypeStruct((BLOCK, wide), BF16),
-            jax.ShapeDtypeStruct((BLOCK, wide), BF16),
+            jax.ShapeDtypeStruct((heads * BLOCK, width), BF16),
+            jax.ShapeDtypeStruct((heads * BLOCK, width), BF16),
             jax.ShapeDtypeStruct((heads, code_total, width), F32),
             jax.ShapeDtypeStruct((wide, 4 * part), BF16),
         ),
-        in_specs=[SMEM, SMEM] + [ANY] * (4 * blocks) + [VMEM] * 7,
-        out_specs=(VMEM,) * 4,
+        in_specs=[SMEM, SMEM] + [ANY] * (5 * blocks + 2),
+        out_specs=(VMEM, VMEM, ANY, ANY),
         scratch_shapes=[
+            pltpu.VMEM((tokens, wide), BF16),
+            pltpu.VMEM((tokens, wide), BF16),
+            pltpu.VMEM((tokens, wide), BF16),
+            pltpu.VMEM((wide, tokens), BF16),
+            pltpu.VMEM((wide, tokens), BF16),
+            pltpu.VMEM((heads, code_total, tokens), BF16),
+            pltpu.VMEM((blocks, 16, 4 * BLOCK), BF16),
+            pltpu.VMEM((wide, tokens), BF16),
+            pltpu.VMEM((8, tokens), F32),
+            pltpu.VMEM((wide, 4 * part), BF16),
             pltpu.VMEM((tokens, 4 * part), BF16),
             pltpu.VMEM((wide, tokens), BF16),
             pltpu.VMEM((tokens, width), F32),
             pltpu.VMEM((8, tokens), F32),
             pltpu.VMEM((2, blocks, BLOCK), F32),
             pltpu.VMEM((blocks, width, BLOCK), BF16),
+            pltpu.VMEM((heads, code_total, width), F32),
+            pltpu.VMEM((wide, 4 * part), BF16),
+            pltpu.VMEM((heads, code_total, width), BF16),
+            pltpu.SemaphoreType.DMA((3, blocks)),
             pltpu.SemaphoreType.DMA((blocks, 4)),
+            pltpu.SemaphoreType.DMA((3 + heads,)),
         ],
-        cost_estimate=pl.CostEstimate(flops=4 * 10**9, bytes_accessed=8 * 10**6, transcendentals=10**6),
-        name="backward",
-    )(me, quarter, *grads, out_weight, att_t, lse, q_all, k_all, v_all, hot)
+        compiler_params=pltpu.CompilerParams(vmem_limit_bytes=28 * 2**20),
+        cost_estimate=pl.CostEstimate(flops=5 * 10**9, bytes_accessed=8 * 10**6, transcendentals=10**6),
+        name="main",
+    )
+    slots[0], grads[0], codebook, out_weight = (
+        pltpu.with_memory_space_constraint(array, pltpu.HBM)
+        for array in (slots[0], grads[0], codebook, out_weight)
+    )
+    dq, dv, dbook, dweight = main(me, quarter, *slots, *grads, codebook, out_weight)
     shape = (tok_here, heads, width)
     return (dq.reshape(shape), dv.reshape(shape), dbook, dweight)
 
 
 def solution(mesh):
     body = on_device
-    if mesh.shape["seq"] == 8 and mesh.shape["head"] == 4:
+    gathered = mesh.shape["seq"] == 8 and mesh.shape["head"] == 4
+    if gathered:
         body = gathered_on_device
     return jax.shard_map(
         body,

time: 88.9 us -> 74.7 us (0.84)
  the two profiles are of different devices: /device:TPU:27 before, /device:TPU:0 now
where the time goes in v2:
time: 74.7 us; the launch traced here: 74.5 us
  waiting for transfers between devices  27.8 us (37%)
  starting transfers between devices  25.8 us (35%)
  Pallas kernels  15.4 us (21%)
  local copies, waits for them, and re-layouts  4.69 us (6%)
  between operations  0.87 us (1%)
    ppermute x38, waiting for transfers between devices, exchange(): return lax.ppermute(array, axis, pairs)  27.8 us
    ppermute x38, starting transfers between devices, exchange(): return lax.ppermute(array, axis, pairs)  25.8 us
    pallas_call x1, Pallas kernels, gathered_body(): main(me, quarter, *slots, *grads, codebook, out_weight)  13.6 us
    unnamed x14, local copies, waits for them, and re-layouts  4.69 us
    pallas_call x1, Pallas kernels, gathered_body(): pl.pallas_call(pack_kernel, out_shape=jax.ShapeDtypeStruct((BLOCK + 16, p...  1.76 us
  transfers between devices with their start and end apart: 38, of which 11 were waited for; matrix products, arithmetic and copies ran while one was open for 0% of the time, Pallas kernels for 2%

profile of v2, /device:TPU:0, one launch (start us, length us, event | category | flops | bytes accessed | tf_op | source)
XLA Modules:
  0.0 74.5 jit_solution(1344821088997152025)
XLA Ops:
  0.6 3.1 %collective-permute-start.14 = (bf16[128,512]{1,0:T(8,128)(2,1)}, bf16[128,512]{1,0:T(8,128)(2,1)S(1)}, u32[]{:S(2)}, u32[]{:S(2)}) collective-permute-start(bf16[128,512]{1,0:T(8,128)(2,1)} %refs_8_.1), channel_id=1, source_target_pairs={{0,8},{4,12},{8,0},{12,4},{16,24},{20,28},{24,16},{28,20},{1,9},{5... | collective-permute-start | bytes 393224 | tf_op jit(solution)/shard_map/ppermute | solution.py:400
  3.7 1.5 %collective-permute-start.10 = (bf16[128,512]{1,0:T(8,128)(2,1)}, bf16[128,512]{1,0:T(8,128)(2,1)S(1)}, u32[]{:S(2)}, u32[]{:S(2)}) collective-permute-start(bf16[128,512]{1,0:T(8,128)(2,1)} %refs_8_.1), channel_id=1, source_target_pairs={{0,4},{4,0},{8,12},{12,8},{16,20},{20,16},{24,28},{28,24},{1,5},{5... | collective-permute-start | bytes 393224 | tf_op jit(solution)/shard_map/ppermute | solution.py:400
  5.3 1.5 %collective-permute-start.8 = (bf16[128,512]{1,0:T(8,128)(2,1)}, bf16[128,512]{1,0:T(8,128)(2,1)S(1)}, u32[]{:S(2)}, u32[]{:S(2)}) collective-permute-start(bf16[128,512]{1,0:T(8,128)(2,1)} %refs_8_.1), channel_id=1, source_target_pairs={{0,2},{1,3},{2,0},{3,1},{4,6},{5,7},{6,4},{7,5},{8,10},{9,11},{10,... | collective-permute-start | bytes 393224 | tf_op jit(solution)/shard_map/ppermute | solution.py:400
  6.8 1.8 %pack.1.refs_0_ = bf16[144,512]{1,0:T(8,128)(2,1)} custom-call(bf16[256,128]{1,0:T(8,128)(2,1)} %bitcast.6, bf16[256,128]{1,0:T(8,128)(2,1)} %bitcast.7, s32[2,128]{1,0:T(2,128)} %code_ref.1), custom_call_target="tpu_custom_call" | custom-call | tf_op jit(solution)/shard_map/pack/pallas_call | solution.py:390
  8.5 2.6 %collective-permute-start.3 = (bf16[144,512]{1,0:T(8,128)(2,1)}, bf16[144,512]{1,0:T(8,128)(2,1)S(1)}, u32[]{:S(2)}, u32[]{:S(2)}) collective-permute-start(bf16[144,512]{1,0:T(8,128)(2,1)} %pack.1.refs_0_), channel_id=1, source_target_pairs={{0,16},{4,20},{8,24},{12,28},{16,0},{20,4},{24,8},{28,12},{1,17},{... | collective-permute-start | bytes 442376 | tf_op jit(solution)/shard_map/ppermute | solution.py:400
  12.0 1.3 %collective-permute-start = (bf16[144,512]{1,0:T(8,128)(2,1)}, bf16[144,512]{1,0:T(8,128)(2,1)S(1)}, u32[]{:S(2)}, u32[]{:S(2)}) collective-permute-start(bf16[144,512]{1,0:T(8,128)(2,1)} %pack.1.refs_0_), channel_id=1, source_target_pairs={{0,4},{4,0},{8,12},{12,8},{16,20},{20,16},{24,28},{28,24},{1,5},{5... | collective-permute-start | bytes 442376 | tf_op jit(solution)/shard_map/ppermute | solution.py:400
  13.3 0.7 collective-permute-start.18
  14.0 9.1 %collective-permute-done.22.refs_24_ = bf16[128,512]{1,0:T(8,128)(2,1)S(1)} collective-permute-done((bf16[128,512]{1,0:T(8,128)(2,1)S(1)}, bf16[128,512]{1,0:T(8,128)(2,1)S(1)}, u32[]{:S(2)}, u32[]{:S(2)}) %collective-permute-start.22) | collective-permute-done | bytes 131104 | tf_op jit(solution)/shard_map/ppermute | solution.py:400
  23.7 1.6 %collective-permute-start.12 = (bf16[128,512]{1,0:T(8,128)(2,1)S(1)}, bf16[128,512]{1,0:T(8,128)(2,1)S(1)}, u32[]{:S(2)}, u32[]{:S(2)}) collective-permute-start(bf16[128,512]{1,0:T(8,128)(2,1)S(1)} %collective-permute-done.10.refs_12_), channel_id=1, source_target_pairs={{0,2},{1,3},{2,0},{3,1},{4,6},{5,7},{6,4},{7,5},{8,10},{9,11},{10,... | collective-permute-start | bytes 393224 | tf_op jit(solution)/shard_map/ppermute | solution.py:400
  25.8 3.7 %collective-permute-done.16.refs_18_ = bf16[128,512]{1,0:T(8,128)(2,1)S(1)} collective-permute-done((bf16[128,512]{1,0:T(8,128)(2,1)S(1)}, bf16[128,512]{1,0:T(8,128)(2,1)S(1)}, u32[]{:S(2)}, u32[]{:S(2)}) %collective-permute-start.16) | collective-permute-done | bytes 131104 | tf_op jit(solution)/shard_map/ppermute | solution.py:400
  30.0 1.0 %collective-permute-done.12.refs_14_ = bf16[128,512]{1,0:T(8,128)(2,1)S(1)} collective-permute-done((bf16[128,512]{1,0:T(8,128)(2,1)S(1)}, bf16[128,512]{1,0:T(8,128)(2,1)S(1)}, u32[]{:S(2)}, u32[]{:S(2)}) %collective-permute-start.12) | collective-permute-done | bytes 131104 | tf_op jit(solution)/shard_map/ppermute | solution.py:400
  31.6 0.7 collective-permute-start.5
  32.2 2.3 %collective-permute-done.30.refs_32_ = bf16[128,512]{1,0:T(8,128)(2,1)S(1)} collective-permute-done((bf16[128,512]{1,0:T(8,128)(2,1)S(1)}, bf16[128,512]{1,0:T(8,128)(2,1)S(1)}, u32[]{:S(2)}, u32[]{:S(2)}) %collective-permute-start.30) | collective-permute-done | bytes 131104 | tf_op jit(solution)/shard_map/ppermute | solution.py:400
  35.0 1.5 %collective-permute-start.2 = (bf16[144,512]{1,0:T(8,128)(2,1)S(1)}, bf16[144,512]{1,0:T(8,128)(2,1)S(1)}, u32[]{:S(2)}, u32[]{:S(2)}) collective-permute-start(bf16[144,512]{1,0:T(8,128)(2,1)S(1)} %collective-permute-done.1.refs_2_), channel_id=1, source_target_pairs={{0,4},{4,0},{8,12},{12,8},{16,20},{20,16},{24,28},{28,24},{1,5},{5... | collective-permute-start | bytes 442376 | tf_op jit(solution)/shard_map/ppermute | solution.py:400
  36.6 1.2 %collective-permute-done.5.refs_6_ = bf16[144,512]{1,0:T(8,128)(2,1)S(1)} collective-permute-done((bf16[144,512]{1,0:T(8,128)(2,1)S(1)}, bf16[144,512]{1,0:T(8,128)(2,1)S(1)}, u32[]{:S(2)}, u32[]{:S(2)}) %collective-permute-start.5) | collective-permute-done | bytes 147488 | tf_op jit(solution)/shard_map/ppermute | solution.py:400
  37.8 1.9 %collective-permute-done.4.refs_5_ = bf16[144,512]{1,0:T(8,128)(2,1)S(1)} collective-permute-done((bf16[144,512]{1,0:T(8,128)(2,1)S(1)}, bf16[144,512]{1,0:T(8,128)(2,1)S(1)}, u32[]{:S(2)}, u32[]{:S(2)}) %collective-permute-start.4) | collective-permute-done | bytes 147488 | tf_op jit(solution)/shard_map/ppermute | solution.py:400
  39.7 1.6 %collective-permute-done.2.refs_3_ = bf16[144,512]{1,0:T(8,128)(2,1)S(1)} collective-permute-done((bf16[144,512]{1,0:T(8,128)(2,1)S(1)}, bf16[144,512]{1,0:T(8,128)(2,1)S(1)}, u32[]{:S(2)}, u32[]{:S(2)}) %collective-permute-start.2) | collective-permute-done | bytes 147488 | tf_op jit(solution)/shard_map/ppermute | solution.py:400
  41.3 1.5 %collective-permute-start.34 = (bf16[128,512]{1,0:T(8,128)(2,1)S(1)}, bf16[128,512]{1,0:T(8,128)(2,1)}, u32[]{:S(2)}, u32[]{:S(2)}) collective-permute-start(bf16[128,512]{1,0:T(8,128)(2,1)S(1)} %collective-permute-done.30.refs_32_), channel_id=1, source_target_pairs={{0,4},{4,0},{8,12},{12,8},{16,20},{20,16},{24,28},{28,24},{1,5},{5... | collective-permute-start | bytes 393224 | tf_op jit(solution)/shard_map/ppermute | solution.py:400
  42.8 2.0 %collective-permute-start.32 = (bf16[128,512]{1,0:T(8,128)(2,1)S(1)}, bf16[128,512]{1,0:T(8,128)(2,1)}, u32[]{:S(2)}, u32[]{:S(2)}) collective-permute-start(bf16[128,512]{1,0:T(8,128)(2,1)S(1)} %collective-permute-done.30.refs_32_), channel_id=1, source_target_pairs={{0,2},{1,3},{2,0},{3,1},{4,6},{5,7},{6,4},{7,5},{8,10},{9,11},{10,... | collective-permute-start | bytes 393224 | tf_op jit(solution)/shard_map/ppermute | solution.py:400
  44.8 0.6 collective-permute-start.6
  45.4 0.9 %collective-permute-done.34.refs_36_ = bf16[128,512]{1,0:T(8,128)(2,1)} collective-permute-done((bf16[128,512]{1,0:T(8,128)(2,1)S(1)}, bf16[128,512]{1,0:T(8,128)(2,1)}, u32[]{:S(2)}, u32[]{:S(2)}) %collective-permute-start.34) | collective-permute-done | bytes 131104 | tf_op jit(solution)/shard_map/ppermute | solution.py:400
  46.4 2.2 %collective-permute-done.32.refs_34_ = bf16[128,512]{1,0:T(8,128)(2,1)} collective-permute-done((bf16[128,512]{1,0:T(8,128)(2,1)S(1)}, bf16[128,512]{1,0:T(8,128)(2,1)}, u32[]{:S(2)}, u32[]{:S(2)}) %collective-permute-start.32) | collective-permute-done | bytes 131104 | tf_op jit(solution)/shard_map/ppermute | solution.py:400
  48.6 0.7 copy-done
  49.3 2.6 %collective-permute-start.36 = (bf16[128,512]{1,0:T(8,128)(2,1)}, bf16[128,512]{1,0:T(8,128)(2,1)}, u32[]{:S(2)}, u32[]{:S(2)}) collective-permute-start(bf16[128,512]{1,0:T(8,128)(2,1)} %collective-permute-done.34.refs_36_), channel_id=1, source_target_pairs={{0,2},{1,3},{2,0},{3,1},{4,6},{5,7},{6,4},{7,5},{8,10},{9,11},{10,... | collective-permute-start | bytes 393224 | tf_op jit(solution)/shard_map/ppermute | solution.py:400
  52.1 0.7 copy-done.2
  53.0 0.7 copy-done.4
  54.2 2.1 %collective-permute-done.36.refs_38_ = bf16[128,512]{1,0:T(8,128)(2,1)} collective-permute-done((bf16[128,512]{1,0:T(8,128)(2,1)}, bf16[128,512]{1,0:T(8,128)(2,1)}, u32[]{:S(2)}, u32[]{:S(2)}) %collective-permute-start.36) | collective-permute-done | bytes 131104 | tf_op jit(solution)/shard_map/ppermute | solution.py:400
  56.4 1.7 %collective-permute-done.37.refs_39_ = bf16[128,512]{1,0:T(8,128)(2,1)} collective-permute-done((bf16[128,512]{1,0:T(8,128)(2,1)}, bf16[128,512]{1,0:T(8,128)(2,1)}, u32[]{:S(2)}, u32[]{:S(2)}) %collective-permute-start.37) | collective-permute-done | bytes 131104 | tf_op jit(solution)/shard_map/ppermute | solution.py:400
  58.0 0.9 %copy-done.1 = bf16[128,512]{1,0:T(8,128)(2,1)S(1)} copy-done((bf16[128,512]{1,0:T(8,128)(2,1)S(1)}, bf16[128,512]{1,0:T(8,128)(2,1)}, u32[]{:S(2)}) %copy-start.1) | copy-done | bytes 131096
  58.9 0.9 %copy-done.3 = bf16[128,512]{1,0:T(8,128)(2,1)S(1)} copy-done((bf16[128,512]{1,0:T(8,128)(2,1)S(1)}, bf16[128,512]{1,0:T(8,128)(2,1)}, u32[]{:S(2)}) %copy-start.3) | copy-done | bytes 131096
  59.8 0.9 %copy-done.5 = bf16[128,512]{1,0:T(8,128)(2,1)S(1)} copy-done((bf16[128,512]{1,0:T(8,128)(2,1)S(1)}, bf16[128,512]{1,0:T(8,128)(2,1)}, u32[]{:S(2)}) %copy-start.5) | copy-done | bytes 131096
  60.7 13.6 %main.1 = (bf16[256,128]{1,0:T(8,128)(2,1)}, bf16[256,128]{1,0:T(8,128)(2,1)}, f32[2,512,128]{2,1,0:T(8,128)}, bf16[256,2048]{1,0:T(8,128)(2,1)}) custom-call(s32[1]{0:T(128)} %bitcast.me_ref, s32[1]{0:T(128)} %bitcast.1.quarter_ref, bf16[144,512]{1,0:T(8,128)(2,1)} %pack.1.refs_0_, bf16[144,512]{1,0:T(8,128)(2,1)S(1)} %collective-permute-done.refs_1_, ...), custom_call_target="tpu_custom_call" | custom-call | flops 5000000000 | bytes 8000000 | tf_op jit(solution)/shard_map/main/pallas_call | solution.py:458
  (60 shorter events, 4.8 us)
Async XLA Ops:
  0.6 10.5 %collective-permute-start.14 = (bf16[128,512]{1,0:T(8,128)(2,1)}, bf16[128,512]{1,0:T(8,128)(2,1)S(1)}, u32[]{:S(2)}, u32[]{:S(2)}) collective-permute-start(bf16[128,512]{1,0:T(8,128)(2,1)} %refs_8_.1), channel_id=1, source_target_pairs={{0,8},{4,12},{8,0},{12,4},{16,24},{20,28},{24,16},{28,20},{1,9},{5... | collective-permute-start | bytes 393224 | tf_op jit(solution)/shard_map/ppermute | solution.py:400
  3.7 7.8 %collective-permute-start.10 = (bf16[128,512]{1,0:T(8,128)(2,1)}, bf16[128,512]{1,0:T(8,128)(2,1)S(1)}, u32[]{:S(2)}, u32[]{:S(2)}) collective-permute-start(bf16[128,512]{1,0:T(8,128)(2,1)} %refs_8_.1), channel_id=1, source_target_pairs={{0,4},{4,0},{8,12},{12,8},{16,20},{20,16},{24,28},{28,24},{1,5},{5... | collective-permute-start | bytes 393224 | tf_op jit(solution)/shard_map/ppermute | solution.py:400
  5.3 6.7 %collective-permute-start.8 = (bf16[128,512]{1,0:T(8,128)(2,1)}, bf16[128,512]{1,0:T(8,128)(2,1)S(1)}, u32[]{:S(2)}, u32[]{:S(2)}) collective-permute-start(bf16[128,512]{1,0:T(8,128)(2,1)} %refs_8_.1), channel_id=1, source_target_pairs={{0,2},{1,3},{2,0},{3,1},{4,6},{5,7},{6,4},{7,5},{8,10},{9,11},{10,... | collective-permute-start | bytes 393224 | tf_op jit(solution)/shard_map/ppermute | solution.py:400
  8.5 15.2 %collective-permute-start.3 = (bf16[144,512]{1,0:T(8,128)(2,1)}, bf16[144,512]{1,0:T(8,128)(2,1)S(1)}, u32[]{:S(2)}, u32[]{:S(2)}) collective-permute-start(bf16[144,512]{1,0:T(8,128)(2,1)} %pack.1.refs_0_), channel_id=1, source_target_pairs={{0,16},{4,20},{8,24},{12,28},{16,0},{20,4},{24,8},{28,12},{1,17},{... | collective-permute-start | bytes 442376 | tf_op jit(solution)/shard_map/ppermute | solution.py:400
  11.1 12.0 %collective-permute-start.22 = (bf16[128,512]{1,0:T(8,128)(2,1)S(1)}, bf16[128,512]{1,0:T(8,128)(2,1)S(1)}, u32[]{:S(2)}, u32[]{:S(2)}) collective-permute-start(bf16[128,512]{1,0:T(8,128)(2,1)S(1)} %copy-done.6), channel_id=1, source_target_pairs={{0,16},{4,20},{8,24},{12,28},{16,0},{20,4},{24,8},{28,12},{1,17},{... | collective-permute-start | bytes 393224 | tf_op jit(solution)/shard_map/ppermute | solution.py:400
  11.5 12.2 %collective-permute-start.1 = (bf16[144,512]{1,0:T(8,128)(2,1)}, bf16[144,512]{1,0:T(8,128)(2,1)S(1)}, u32[]{:S(2)}, u32[]{:S(2)}) collective-permute-start(bf16[144,512]{1,0:T(8,128)(2,1)} %pack.1.refs_0_), channel_id=1, source_target_pairs={{0,8},{4,12},{8,0},{12,4},{16,24},{20,28},{24,16},{28,20},{1,9},{5... | collective-permute-start | bytes 442376 | tf_op jit(solution)/shard_map/ppermute | solution.py:400
  12.0 13.3 %collective-permute-start = (bf16[144,512]{1,0:T(8,128)(2,1)}, bf16[144,512]{1,0:T(8,128)(2,1)S(1)}, u32[]{:S(2)}, u32[]{:S(2)}) collective-permute-start(bf16[144,512]{1,0:T(8,128)(2,1)} %pack.1.refs_0_), channel_id=1, source_target_pairs={{0,4},{4,0},{8,12},{12,8},{16,20},{20,16},{24,28},{28,24},{1,5},{5... | collective-permute-start | bytes 442376 | tf_op jit(solution)/shard_map/ppermute | solution.py:400
  13.3 12.1 %collective-permute-start.18 = (bf16[128,512]{1,0:T(8,128)(2,1)S(1)}, bf16[128,512]{1,0:T(8,128)(2,1)S(1)}, u32[]{:S(2)}, u32[]{:S(2)}) collective-permute-start(bf16[128,512]{1,0:T(8,128)(2,1)S(1)} %collective-permute-done.14.refs_16_), channel_id=1, source_target_pairs={{0,4},{4,0},{8,12},{12,8},{16,20},{20,16},{24,28},{28,24},{1,5},{5... | collective-permute-start | bytes 393224 | tf_op jit(solution)/shard_map/ppermute | solution.py:400
  23.1 6.4 %collective-permute-start.16 = (bf16[128,512]{1,0:T(8,128)(2,1)S(1)}, bf16[128,512]{1,0:T(8,128)(2,1)S(1)}, u32[]{:S(2)}, u32[]{:S(2)}) collective-permute-start(bf16[128,512]{1,0:T(8,128)(2,1)S(1)} %collective-permute-done.14.refs_16_), channel_id=1, source_target_pairs={{0,2},{1,3},{2,0},{3,1},{4,6},{5,7},{6,4},{7,5},{8,10},{9,11},{10,... | collective-permute-start | bytes 393224 | tf_op jit(solution)/shard_map/ppermute | solution.py:400
  23.7 5.8 %collective-permute-start.15 = (bf16[128,512]{1,0:T(8,128)(2,1)S(1)}, bf16[128,512]{1,0:T(8,128)(2,1)S(1)}, u32[]{:S(2)}, u32[]{:S(2)}) collective-permute-start(bf16[128,512]{1,0:T(8,128)(2,1)S(1)} %collective-permute-done.14.refs_16_), channel_id=1, source_target_pairs={{0,1},{1,0},{2,3},{3,2},{4,5},{5,4},{6,7},{7,6},{8,9},{9,8},{10,11... | collective-permute-start | bytes 393224 | tf_op jit(solution)/shard_map/ppermute | solution.py:400
  23.7 7.3 %collective-permute-start.12 = (bf16[128,512]{1,0:T(8,128)(2,1)S(1)}, bf16[128,512]{1,0:T(8,128)(2,1)S(1)}, u32[]{:S(2)}, u32[]{:S(2)}) collective-permute-start(bf16[128,512]{1,0:T(8,128)(2,1)S(1)} %collective-permute-done.10.refs_12_), channel_id=1, source_target_pairs={{0,2},{1,3},{2,0},{3,1},{4,6},{5,7},{6,4},{7,5},{8,10},{9,11},{10,... | collective-permute-start | bytes 393224 | tf_op jit(solution)/shard_map/ppermute | solution.py:400
  25.3 6.3 %collective-permute-start.11 = (bf16[128,512]{1,0:T(8,128)(2,1)S(1)}, bf16[128,512]{1,0:T(8,128)(2,1)S(1)}, u32[]{:S(2)}, u32[]{:S(2)}) collective-permute-start(bf16[128,512]{1,0:T(8,128)(2,1)S(1)} %collective-permute-done.10.refs_12_), channel_id=1, source_target_pairs={{0,1},{1,0},{2,3},{3,2},{4,5},{5,4},{6,7},{7,6},{8,9},{9,8},{10,11... | collective-permute-start | bytes 393224 | tf_op jit(solution)/shard_map/ppermute | solution.py:400
  25.4 6.1 %collective-permute-start.9 = (bf16[128,512]{1,0:T(8,128)(2,1)S(1)}, bf16[128,512]{1,0:T(8,128)(2,1)S(1)}, u32[]{:S(2)}, u32[]{:S(2)}) collective-permute-start(bf16[128,512]{1,0:T(8,128)(2,1)S(1)} %collective-permute-done.8.refs_10_), channel_id=1, source_target_pairs={{0,1},{1,0},{2,3},{3,2},{4,5},{5,4},{6,7},{7,6},{8,9},{9,8},{10,11... | collective-permute-start | bytes 393224 | tf_op jit(solution)/shard_map/ppermute | solution.py:400
  29.5 5.0 %collective-permute-start.30 = (bf16[128,512]{1,0:T(8,128)(2,1)S(1)}, bf16[128,512]{1,0:T(8,128)(2,1)S(1)}, u32[]{:S(2)}, u32[]{:S(2)}) collective-permute-start(bf16[128,512]{1,0:T(8,128)(2,1)S(1)} %collective-permute-done.22.refs_24_), channel_id=1, source_target_pairs={{0,8},{4,12},{8,0},{12,4},{16,24},{20,28},{24,16},{28,20},{1,9},{5... | collective-permute-start | bytes 393224 | tf_op jit(solution)/shard_map/ppermute | solution.py:400
  29.5 5.5 %collective-permute-start.26 = (bf16[128,512]{1,0:T(8,128)(2,1)S(1)}, bf16[128,512]{1,0:T(8,128)(2,1)S(1)}, u32[]{:S(2)}, u32[]{:S(2)}) collective-permute-start(bf16[128,512]{1,0:T(8,128)(2,1)S(1)} %collective-permute-done.22.refs_24_), channel_id=1, source_target_pairs={{0,4},{4,0},{8,12},{12,8},{16,20},{20,16},{24,28},{28,24},{1,5},{5... | collective-permute-start | bytes 393224 | tf_op jit(solution)/shard_map/ppermute | solution.py:400
  31.0 5.5 %collective-permute-start.24 = (bf16[128,512]{1,0:T(8,128)(2,1)S(1)}, bf16[128,512]{1,0:T(8,128)(2,1)S(1)}, u32[]{:S(2)}, u32[]{:S(2)}) collective-permute-start(bf16[128,512]{1,0:T(8,128)(2,1)S(1)} %collective-permute-done.22.refs_24_), channel_id=1, source_target_pairs={{0,2},{1,3},{2,0},{3,1},{4,6},{5,7},{6,4},{7,5},{8,10},{9,11},{10,... | collective-permute-start | bytes 393224 | tf_op jit(solution)/shard_map/ppermute | solution.py:400
  31.6 5.1 %collective-permute-start.23 = (bf16[128,512]{1,0:T(8,128)(2,1)S(1)}, bf16[128,512]{1,0:T(8,128)(2,1)S(1)}, u32[]{:S(2)}, u32[]{:S(2)}) collective-permute-start(bf16[128,512]{1,0:T(8,128)(2,1)S(1)} %collective-permute-done.22.refs_24_), channel_id=1, source_target_pairs={{0,1},{1,0},{2,3},{3,2},{4,5},{5,4},{6,7},{7,6},{8,9},{9,8},{10,11... | collective-permute-start | bytes 393224 | tf_op jit(solution)/shard_map/ppermute | solution.py:400
  31.6 6.3 %collective-permute-start.5 = (bf16[144,512]{1,0:T(8,128)(2,1)S(1)}, bf16[144,512]{1,0:T(8,128)(2,1)S(1)}, u32[]{:S(2)}, u32[]{:S(2)}) collective-permute-start(bf16[144,512]{1,0:T(8,128)(2,1)S(1)} %collective-permute-done.3.refs_4_), channel_id=1, source_target_pairs={{0,8},{4,12},{8,0},{12,4},{16,24},{20,28},{24,16},{28,20},{1,9},{5... | collective-permute-start | bytes 442376 | tf_op jit(solution)/shard_map/ppermute | solution.py:400
  34.5 5.2 %collective-permute-start.4 = (bf16[144,512]{1,0:T(8,128)(2,1)S(1)}, bf16[144,512]{1,0:T(8,128)(2,1)S(1)}, u32[]{:S(2)}, u32[]{:S(2)}) collective-permute-start(bf16[144,512]{1,0:T(8,128)(2,1)S(1)} %collective-permute-done.3.refs_4_), channel_id=1, source_target_pairs={{0,4},{4,0},{8,12},{12,8},{16,20},{20,16},{24,28},{28,24},{1,5},{5... | collective-permute-start | bytes 442376 | tf_op jit(solution)/shard_map/ppermute | solution.py:400
  35.0 6.3 %collective-permute-start.2 = (bf16[144,512]{1,0:T(8,128)(2,1)S(1)}, bf16[144,512]{1,0:T(8,128)(2,1)S(1)}, u32[]{:S(2)}, u32[]{:S(2)}) collective-permute-start(bf16[144,512]{1,0:T(8,128)(2,1)S(1)} %collective-permute-done.1.refs_2_), channel_id=1, source_target_pairs={{0,4},{4,0},{8,12},{12,8},{16,20},{20,16},{24,28},{28,24},{1,5},{5... | collective-permute-start | bytes 442376 | tf_op jit(solution)/shard_map/ppermute | solution.py:400
  36.5 6.3 %collective-permute-start.20 = (bf16[128,512]{1,0:T(8,128)(2,1)S(1)}, bf16[128,512]{1,0:T(8,128)(2,1)S(1)}, u32[]{:S(2)}, u32[]{:S(2)}) collective-permute-start(bf16[128,512]{1,0:T(8,128)(2,1)S(1)} %collective-permute-done.18.refs_20_), channel_id=1, source_target_pairs={{0,2},{1,3},{2,0},{3,1},{4,6},{5,7},{6,4},{7,5},{8,10},{9,11},{10,... | collective-permute-start | bytes 393224 | tf_op jit(solution)/shard_map/ppermute | solution.py:400
  36.6 8.2 %collective-permute-start.19 = (bf16[128,512]{1,0:T(8,128)(2,1)S(1)}, bf16[128,512]{1,0:T(8,128)(2,1)S(1)}, u32[]{:S(2)}, u32[]{:S(2)}) collective-permute-start(bf16[128,512]{1,0:T(8,128)(2,1)S(1)} %collective-permute-done.18.refs_20_), channel_id=1, source_target_pairs={{0,1},{1,0},{2,3},{3,2},{4,5},{5,4},{6,7},{7,6},{8,9},{9,8},{10,11... | collective-permute-start | bytes 393224 | tf_op jit(solution)/shard_map/ppermute | solution.py:400
  37.8 6.9 %collective-permute-start.17 = (bf16[128,512]{1,0:T(8,128)(2,1)S(1)}, bf16[128,512]{1,0:T(8,128)(2,1)S(1)}, u32[]{:S(2)}, u32[]{:S(2)}) collective-permute-start(bf16[128,512]{1,0:T(8,128)(2,1)S(1)} %collective-permute-done.16.refs_18_), channel_id=1, source_target_pairs={{0,1},{1,0},{2,3},{3,2},{4,5},{5,4},{6,7},{7,6},{8,9},{9,8},{10,11... | collective-permute-start | bytes 393224 | tf_op jit(solution)/shard_map/ppermute | solution.py:400
  39.7 5.6 %collective-permute-start.13 = (bf16[128,512]{1,0:T(8,128)(2,1)S(1)}, bf16[128,512]{1,0:T(8,128)(2,1)S(1)}, u32[]{:S(2)}, u32[]{:S(2)}) collective-permute-start(bf16[128,512]{1,0:T(8,128)(2,1)S(1)} %collective-permute-done.12.refs_14_), channel_id=1, source_target_pairs={{0,1},{1,0},{2,3},{3,2},{4,5},{5,4},{6,7},{7,6},{8,9},{9,8},{10,11... | collective-permute-start | bytes 393224 | tf_op jit(solution)/shard_map/ppermute | solution.py:400
  41.3 5.1 %collective-permute-start.34 = (bf16[128,512]{1,0:T(8,128)(2,1)S(1)}, bf16[128,512]{1,0:T(8,128)(2,1)}, u32[]{:S(2)}, u32[]{:S(2)}) collective-permute-start(bf16[128,512]{1,0:T(8,128)(2,1)S(1)} %collective-permute-done.30.refs_32_), channel_id=1, source_target_pairs={{0,4},{4,0},{8,12},{12,8},{16,20},{20,16},{24,28},{28,24},{1,5},{5... | collective-permute-start | bytes 393224 | tf_op jit(solution)/shard_map/ppermute | solution.py:400
  42.8 5.8 %collective-permute-start.32 = (bf16[128,512]{1,0:T(8,128)(2,1)S(1)}, bf16[128,512]{1,0:T(8,128)(2,1)}, u32[]{:S(2)}, u32[]{:S(2)}) collective-permute-start(bf16[128,512]{1,0:T(8,128)(2,1)S(1)} %collective-permute-done.30.refs_32_), channel_id=1, source_target_pairs={{0,2},{1,3},{2,0},{3,1},{4,6},{5,7},{6,4},{7,5},{8,10},{9,11},{10,... | collective-permute-start | bytes 393224 | tf_op jit(solution)/shard_map/ppermute | solution.py:400
  44.8 9.1 %collective-permute-start.6 = (bf16[144,512]{1,0:T(8,128)(2,1)S(1)}, bf16[144,512]{1,0:T(8,128)(2,1)S(1)}, u32[]{:S(2)}, u32[]{:S(2)}) collective-permute-start(bf16[144,512]{1,0:T(8,128)(2,1)S(1)} %collective-permute-done.5.refs_6_), channel_id=1, source_target_pairs={{0,4},{4,0},{8,12},{12,8},{16,20},{20,16},{24,28},{28,24},{1,5},{5... | collective-permute-start | bytes 442376 | tf_op jit(solution)/shard_map/ppermute | solution.py:400
  45.3 6.5 %collective-permute-start.28 = (bf16[128,512]{1,0:T(8,128)(2,1)S(1)}, bf16[128,512]{1,0:T(8,128)(2,1)}, u32[]{:S(2)}, u32[]{:S(2)}) collective-permute-start(bf16[128,512]{1,0:T(8,128)(2,1)S(1)} %collective-permute-done.26.refs_28_), channel_id=1, source_target_pairs={{0,2},{1,3},{2,0},{3,1},{4,6},{5,7},{6,4},{7,5},{8,10},{9,11},{10,... | collective-permute-start | bytes 393224 | tf_op jit(solution)/shard_map/ppermute | solution.py:400
  46.4 5.7 %collective-permute-start.27 = (bf16[128,512]{1,0:T(8,128)(2,1)S(1)}, bf16[128,512]{1,0:T(8,128)(2,1)S(1)}, u32[]{:S(2)}, u32[]{:S(2)}) collective-permute-start(bf16[128,512]{1,0:T(8,128)(2,1)S(1)} %collective-permute-done.26.refs_28_), channel_id=1, source_target_pairs={{0,1},{1,0},{2,3},{3,2},{4,5},{5,4},{6,7},{7,6},{8,9},{9,8},{10,11... | collective-permute-start | bytes 393224 | tf_op jit(solution)/shard_map/ppermute | solution.py:400
  48.6 4.4 %collective-permute-start.25 = (bf16[128,512]{1,0:T(8,128)(2,1)S(1)}, bf16[128,512]{1,0:T(8,128)(2,1)S(1)}, u32[]{:S(2)}, u32[]{:S(2)}) collective-permute-start(bf16[128,512]{1,0:T(8,128)(2,1)S(1)} %collective-permute-done.24.refs_26_), channel_id=1, source_target_pairs={{0,1},{1,0},{2,3},{3,2},{4,5},{5,4},{6,7},{7,6},{8,9},{9,8},{10,11... | collective-permute-start | bytes 393224 | tf_op jit(solution)/shard_map/ppermute | solution.py:400
  49.3 7.1 %collective-permute-start.36 = (bf16[128,512]{1,0:T(8,128)(2,1)}, bf16[128,512]{1,0:T(8,128)(2,1)}, u32[]{:S(2)}, u32[]{:S(2)}) collective-permute-start(bf16[128,512]{1,0:T(8,128)(2,1)} %collective-permute-done.34.refs_36_), channel_id=1, source_target_pairs={{0,2},{1,3},{2,0},{3,1},{4,6},{5,7},{6,4},{7,5},{8,10},{9,11},{10,... | collective-permute-start | bytes 393224 | tf_op jit(solution)/shard_map/ppermute | solution.py:400
  51.9 4.5 %collective-permute-start.35 = (bf16[128,512]{1,0:T(8,128)(2,1)}, bf16[128,512]{1,0:T(8,128)(2,1)}, u32[]{:S(2)}, u32[]{:S(2)}) collective-permute-start(bf16[128,512]{1,0:T(8,128)(2,1)} %collective-permute-done.34.refs_36_), channel_id=1, source_target_pairs={{0,1},{1,0},{2,3},{3,2},{4,5},{5,4},{6,7},{7,6},{8,9},{9,8},{10,11... | collective-permute-start | bytes 393224 | tf_op jit(solution)/shard_map/ppermute | solution.py:400
  (13 other events, 25.5 us)

commit v3 on v2

--- a/solution.py
+++ b/solution.py
@@ -237,8 +237,8 @@
         code = code_ref[head : head + 1, :]
         high = lax.shift_right_logical(code, 1)
         for digit, at in ((high, 2 * head), (code - 2 * high, 2 * head + 1)):
-            digit = jnp.broadcast_to(digit.astype(F32), (16, rows)).astype(BF16)
-            out_ref[rows : rows + 16, at * rows : (at + 1) * rows] = digit
+            digit = jnp.broadcast_to(digit.astype(F32), (8, rows)).astype(BF16)
+            out_ref[rows : rows + 8, at * rows : (at + 1) * rows] = digit
 
 
 def main_kernel(blocks, heads, width, code_total, me_ref, quarter_ref, *refs):
@@ -256,13 +256,14 @@
     me = me_ref[0]
     quarter = quarter_ref[0]
 
-    inputs, late = [pltpu.make_async_copy(book_any, book_ref, out_sems.at[2 + heads])], []
+    inputs = [pltpu.make_async_copy(book_any, book_ref, out_sems.at[2 + heads])]
+    codes_in, late = [], []
     for at in range(blocks):
         block = slot_block(me, at // 2, at % 2)
         rows = pl.ds(pl.multiple_of(block * BLOCK, BLOCK), BLOCK)
         source = slots[at]
-        inputs.append(pltpu.make_async_copy(
-            source.at[pl.ds(BLOCK, 16), :], codes_ref.at[block], sems.at[2, at]))
+        codes_in.append(pltpu.make_async_copy(
+            source.at[pl.ds(BLOCK, 8), :], codes_ref.at[block], sems.at[2, at]))
         inputs.append(pltpu.make_async_copy(
             source.at[pl.ds(0, BLOCK), pl.ds(0, wide)], q_ref.at[rows, :], sems.at[0, at]))
         inputs.append(pltpu.make_async_copy(
@@ -276,9 +277,9 @@
             late.append(pltpu.make_async_copy(
                 grads[4 * at + piece].at[pl.ds(0, BLOCK), :],
                 go_ref.at[rows, pl.ds(column, part)], go_sems.at[at, piece]))
-    for copy in inputs + late:
+    for copy in codes_in + inputs:
         copy.start()
-    for copy in inputs:
+    for copy in codes_in:
         copy.wait()
 
     for head in range(heads):
@@ -291,24 +292,39 @@
             rows = lax.broadcasted_iota(jnp.int32, (code_total, BLOCK), 0)
             hot = jnp.where(rows == code, 1.0, 0.0).astype(BF16)
             hot_ref[head, :, block * BLOCK : (block + 1) * BLOCK] = hot
+    for copy in inputs:
+        copy.wait()
+    for copy in late:
+        copy.start()
+    for head in range(heads):
+        columns = slice(head * width, (head + 1) * width)
         key_t = dot_nn(book_ref[head].astype(F32).T.astype(BF16), hot_ref[head])
         k_t_ref[columns, :] = key_t.astype(BF16)
         k_ref[:, columns] = key_t.T.astype(BF16)
         v_t_ref[columns, :] = v_ref[:, columns].astype(F32).T.astype(BF16)
-    for head in range(heads):
-        columns = slice(head * width, (head + 1) * width)
-        for tile in range(tokens // TILE):
-            here = slice(tile * TILE, (tile + 1) * TILE)
-            seen = (tile + 1) * TILE
-            scores = dot_nt(k_ref[:seen, columns], q_ref[here, columns])
-            last = jnp.where(causal_tile(), scores[seen - TILE :], -jnp.inf)
-            scores = last if tile == 0 else jnp.concatenate([scores[: seen - TILE], last], axis=0)
-            top = jnp.max(scores, axis=0, keepdims=True)
-            weights = jnp.exp(scores - top)
-            total = jnp.sum(weights, axis=0, keepdims=True)
-            mixed = dot_nn(v_t_ref[columns, :seen], weights.astype(BF16))
-            att_t_ref[columns, here] = (mixed / total).astype(BF16)
-            lse_ref[head : head + 1, here] = top + jnp.log(total)
+
+    def scored(head, tile):
+        columns = slice(head * width, (head + 1) * width)
+        seen = (tile + 1) * TILE
+        return dot_nt(k_ref[:seen, columns], q_ref[tile * TILE : seen, columns])
+
+    steps = [(head, tile) for tile in range(tokens // TILE) for head in range(heads)]
+    ahead = scored(*steps[0])
+    for at, (head, tile) in enumerate(steps):
+        columns = slice(head * width, (head + 1) * width)
+        here = slice(tile * TILE, (tile + 1) * TILE)
+        seen = (tile + 1) * TILE
+        scores = ahead
+        if at + 1 < len(steps):
+            ahead = scored(*steps[at + 1])
+        last = jnp.where(causal_tile(), scores[seen - TILE :], -jnp.inf)
+        scores = last if tile == 0 else jnp.concatenate([scores[: seen - TILE], last], axis=0)
+        top = jnp.max(scores, axis=0, keepdims=True)
+        weights = jnp.exp(scores - top)
+        total = jnp.sum(weights, axis=0, keepdims=True)
+        mixed = dot_nn(v_t_ref[columns, :seen], weights.astype(BF16))
+        att_t_ref[columns, here] = (mixed / total).astype(BF16)
+        lse_ref[head : head + 1, here] = top + jnp.log(total)
 
     for copy in late:
         copy.wait()
@@ -327,22 +343,34 @@
         columns = slice(head * width, (head + 1) * width)
         delta_ref[head : head + 1, :] = jnp.sum(
             do_t_ref[columns, :].astype(F32) * att_t_ref[columns, :].astype(F32), axis=0, keepdims=True)
-        for tile in range(tokens // TILE):
-            here = slice(tile * TILE, (tile + 1) * TILE)
-            seen = (tile + 1) * TILE
-            scores = dot_nt(k_ref[:seen, columns], q_ref[here, columns])
-            weights = jnp.exp(scores - lse_ref[head : head + 1, here])
-            last = jnp.where(causal_tile(), weights[seen - TILE :], 0.0)
-            weights = last if tile == 0 else jnp.concatenate([weights[: seen - TILE], last], axis=0)
-            grad = dot_nn(v_ref[:seen, columns], do_t_ref[columns, here])
-            grad = (weights * (grad - delta_ref[head : head + 1, here])).astype(BF16)
-            term = dot_nn(grad, q_ref[here, columns])
-            if tile == 0:
-                dk_ref[:seen, :] = term
-            else:
-                dk_ref[: seen - TILE, :] += term[: seen - TILE]
-                dk_ref[seen - TILE : seen, :] = term[seen - TILE :]
-        dbook_ref[head] = dot_nn(hot_ref[head], dk_ref[...].astype(BF16))
+
+    def products(head, tile):
+        columns = slice(head * width, (head + 1) * width)
+        seen = (tile + 1) * TILE
+        grad = dot_nn(v_ref[:seen, columns], do_t_ref[columns, tile * TILE : seen])
+        return scored(head, tile), grad
+
+    ahead = products(*steps[0])
+    for at, (head, tile) in enumerate(steps):
+        columns = slice(head * width, (head + 1) * width)
+        here = slice(tile * TILE, (tile + 1) * TILE)
+        seen = (tile + 1) * TILE
+        scores, grad = ahead
+        if at + 1 < len(steps):
+            ahead = products(*steps[at + 1])
+        weights = jnp.exp(scores - lse_ref[head : head + 1, here])
+        last = jnp.where(causal_tile(), weights[seen - TILE :], 0.0)
+        weights = last if tile == 0 else jnp.concatenate([weights[: seen - TILE], last], axis=0)
+        grad = (weights * (grad - delta_ref[head : head + 1, here])).astype(BF16)
+        term = dot_nn(grad, q_ref[here, columns])
+        if tile == 0:
+            dk_ref[head, :seen, :] = term
+        else:
+            dk_ref[head, : seen - TILE, :] += term[: seen - TILE]
+            dk_ref[head, seen - TILE : seen, :] = term[seen - TILE :]
+    for head in range(heads):
+        columns = slice(head * width, (head + 1) * width)
+        dbook_ref[head] = dot_nn(hot_ref[head], dk_ref[head].astype(BF16))
         outputs.append(pltpu.make_async_copy(dbook_ref.at[head], dbook_any.at[head], out_sems.at[2 + head]))
         outputs[-1].start()
         scores = dot_nt(k_ref[mine, columns], q_ref[:, columns])
@@ -389,7 +417,7 @@
 
     payload = pl.pallas_call(
         pack_kernel,
-        out_shape=jax.ShapeDtypeStruct((BLOCK + 16, part), BF16),
+        out_shape=jax.ShapeDtypeStruct((BLOCK + 8, part), BF16),
         in_specs=[VMEM] * 3,
         out_specs=VMEM,
         name="pack",
@@ -430,13 +458,13 @@
             pltpu.VMEM((wide, tokens), BF16),
             pltpu.VMEM((wide, tokens), BF16),
             pltpu.VMEM((heads, code_total, tokens), BF16),
-            pltpu.VMEM((blocks, 16, 4 * BLOCK), BF16),
+            pltpu.VMEM((blocks, 8, 4 * BLOCK), BF16),
             pltpu.VMEM((wide, tokens), BF16),
             pltpu.VMEM((8, tokens), F32),
             pltpu.VMEM((wide, 4 * part), BF16),
             pltpu.VMEM((tokens, 4 * part), BF16),
             pltpu.VMEM((wide, tokens), BF16),
-            pltpu.VMEM((tokens, width), F32),
+            pltpu.VMEM((heads, tokens, width), F32),
             pltpu.VMEM((8, tokens), F32),
             pltpu.VMEM((2, blocks, BLOCK), F32),
             pltpu.VMEM((blocks, width, BLOCK), BF16),

time: 74.7 us -> 72.6 us (0.972)
  Pallas kernels: 15.4 us -> 14 us
    pallas_call x1, Pallas kernels: 13.6 us -> 12.3 us  [gathered_body(): main(me, quarter, *slots, *grads, codebook, out_weight)]
where the time goes in v3:
time: 72.6 us; the launch traced here: 72.4 us
  waiting for transfers between devices  27.1 us (37%)
  starting transfers between devices  25.8 us (36%)
  Pallas kernels  14 us (19%)
  local copies, waits for them, and re-layouts  4.69 us (6%)
  between operations  0.87 us (1%)
    ppermute x38, waiting for transfers between devices, exchange(): return lax.ppermute(array, axis, pairs)  27.1 us
    ppermute x38, starting transfers between devices, exchange(): return lax.ppermute(array, axis, pairs)  25.8 us
    pallas_call x1, Pallas kernels, gathered_body(): main(me, quarter, *slots, *grads, codebook, out_weight)  12.3 us
    unnamed x14, local copies, waits for them, and re-layouts  4.69 us
    pallas_call x1, Pallas kernels, gathered_body(): pl.pallas_call(pack_kernel, out_shape=jax.ShapeDtypeStruct((BLOCK + 8, pa...  1.75 us
  transfers between devices with their start and end apart: 38, of which 11 were waited for; matrix products, arithmetic and copies ran while one was open for 0% of the time, Pallas kernels for 2%

profile of v3, /device:TPU:0, one launch (start us, length us, event | category | flops | bytes accessed | tf_op | source)
XLA Modules:
  0.0 72.4 jit_solution(5776137787926840802)
XLA Ops:
  0.6 3.1 %collective-permute-start.14 = (bf16[128,512]{1,0:T(8,128)(2,1)}, bf16[128,512]{1,0:T(8,128)(2,1)S(1)}, u32[]{:S(2)}, u32[]{:S(2)}) collective-permute-start(bf16[128,512]{1,0:T(8,128)(2,1)} %refs_8_.1), channel_id=1, source_target_pairs={{0,8},{4,12},{8,0},{12,4},{16,24},{20,28},{24,16},{28,20},{1,9},{5... | collective-permute-start | bytes 393224 | tf_op jit(solution)/shard_map/ppermute | solution.py:428
  3.7 1.5 %collective-permute-start.10 = (bf16[128,512]{1,0:T(8,128)(2,1)}, bf16[128,512]{1,0:T(8,128)(2,1)S(1)}, u32[]{:S(2)}, u32[]{:S(2)}) collective-permute-start(bf16[128,512]{1,0:T(8,128)(2,1)} %refs_8_.1), channel_id=1, source_target_pairs={{0,4},{4,0},{8,12},{12,8},{16,20},{20,16},{24,28},{28,24},{1,5},{5... | collective-permute-start | bytes 393224 | tf_op jit(solution)/shard_map/ppermute | solution.py:428
  5.3 1.5 %collective-permute-start.8 = (bf16[128,512]{1,0:T(8,128)(2,1)}, bf16[128,512]{1,0:T(8,128)(2,1)S(1)}, u32[]{:S(2)}, u32[]{:S(2)}) collective-permute-start(bf16[128,512]{1,0:T(8,128)(2,1)} %refs_8_.1), channel_id=1, source_target_pairs={{0,2},{1,3},{2,0},{3,1},{4,6},{5,7},{6,4},{7,5},{8,10},{9,11},{10,... | collective-permute-start | bytes 393224 | tf_op jit(solution)/shard_map/ppermute | solution.py:428
  6.8 1.8 %pack.1.refs_0_ = bf16[136,512]{1,0:T(8,128)(2,1)} custom-call(bf16[256,128]{1,0:T(8,128)(2,1)} %bitcast.6, bf16[256,128]{1,0:T(8,128)(2,1)} %bitcast.7, s32[2,128]{1,0:T(2,128)} %code_ref.1), custom_call_target="tpu_custom_call" | custom-call | tf_op jit(solution)/shard_map/pack/pallas_call | solution.py:418
  8.5 2.6 %collective-permute-start.3 = (bf16[136,512]{1,0:T(8,128)(2,1)}, bf16[136,512]{1,0:T(8,128)(2,1)S(1)}, u32[]{:S(2)}, u32[]{:S(2)}) collective-permute-start(bf16[136,512]{1,0:T(8,128)(2,1)} %pack.1.refs_0_), channel_id=1, source_target_pairs={{0,16},{4,20},{8,24},{12,28},{16,0},{20,4},{24,8},{28,12},{1,17},{... | collective-permute-start | bytes 417800 | tf_op jit(solution)/shard_map/ppermute | solution.py:428
  12.0 1.3 %collective-permute-start = (bf16[136,512]{1,0:T(8,128)(2,1)}, bf16[136,512]{1,0:T(8,128)(2,1)S(1)}, u32[]{:S(2)}, u32[]{:S(2)}) collective-permute-start(bf16[136,512]{1,0:T(8,128)(2,1)} %pack.1.refs_0_), channel_id=1, source_target_pairs={{0,4},{4,0},{8,12},{12,8},{16,20},{20,16},{24,28},{28,24},{1,5},{5... | collective-permute-start | bytes 417800 | tf_op jit(solution)/shard_map/ppermute | solution.py:428
  13.3 0.7 collective-permute-start.18
  14.0 8.8 %collective-permute-done.22.refs_24_ = bf16[128,512]{1,0:T(8,128)(2,1)S(1)} collective-permute-done((bf16[128,512]{1,0:T(8,128)(2,1)S(1)}, bf16[128,512]{1,0:T(8,128)(2,1)S(1)}, u32[]{:S(2)}, u32[]{:S(2)}) %collective-permute-start.22) | collective-permute-done | bytes 131104 | tf_op jit(solution)/shard_map/ppermute | solution.py:428
  23.3 1.6 %collective-permute-start.12 = (bf16[128,512]{1,0:T(8,128)(2,1)S(1)}, bf16[128,512]{1,0:T(8,128)(2,1)S(1)}, u32[]{:S(2)}, u32[]{:S(2)}) collective-permute-start(bf16[128,512]{1,0:T(8,128)(2,1)S(1)} %collective-permute-done.10.refs_12_), channel_id=1, source_target_pairs={{0,2},{1,3},{2,0},{3,1},{4,6},{5,7},{6,4},{7,5},{8,10},{9,11},{10,... | collective-permute-start | bytes 393224 | tf_op jit(solution)/shard_map/ppermute | solution.py:428
  25.4 3.7 %collective-permute-done.16.refs_18_ = bf16[128,512]{1,0:T(8,128)(2,1)S(1)} collective-permute-done((bf16[128,512]{1,0:T(8,128)(2,1)S(1)}, bf16[128,512]{1,0:T(8,128)(2,1)S(1)}, u32[]{:S(2)}, u32[]{:S(2)}) %collective-permute-start.16) | collective-permute-done | bytes 131104 | tf_op jit(solution)/shard_map/ppermute | solution.py:428
  29.6 1.0 %collective-permute-done.12.refs_14_ = bf16[128,512]{1,0:T(8,128)(2,1)S(1)} collective-permute-done((bf16[128,512]{1,0:T(8,128)(2,1)S(1)}, bf16[128,512]{1,0:T(8,128)(2,1)S(1)}, u32[]{:S(2)}, u32[]{:S(2)}) %collective-permute-start.12) | collective-permute-done | bytes 131104 | tf_op jit(solution)/shard_map/ppermute | solution.py:428
  31.1 0.6 collective-permute-start.5
  31.8 2.3 %collective-permute-done.30.refs_32_ = bf16[128,512]{1,0:T(8,128)(2,1)S(1)} collective-permute-done((bf16[128,512]{1,0:T(8,128)(2,1)S(1)}, bf16[128,512]{1,0:T(8,128)(2,1)S(1)}, u32[]{:S(2)}, u32[]{:S(2)}) %collective-permute-start.30) | collective-permute-done | bytes 131104 | tf_op jit(solution)/shard_map/ppermute | solution.py:428
  34.5 1.6 %collective-permute-start.2 = (bf16[136,512]{1,0:T(8,128)(2,1)S(1)}, bf16[136,512]{1,0:T(8,128)(2,1)S(1)}, u32[]{:S(2)}, u32[]{:S(2)}) collective-permute-start(bf16[136,512]{1,0:T(8,128)(2,1)S(1)} %collective-permute-done.1.refs_2_), channel_id=1, source_target_pairs={{0,4},{4,0},{8,12},{12,8},{16,20},{20,16},{24,28},{28,24},{1,5},{5... | collective-permute-start | bytes 417800 | tf_op jit(solution)/shard_map/ppermute | solution.py:428
  36.3 0.9 %collective-permute-done.5.refs_6_ = bf16[136,512]{1,0:T(8,128)(2,1)S(1)} collective-permute-done((bf16[136,512]{1,0:T(8,128)(2,1)S(1)}, bf16[136,512]{1,0:T(8,128)(2,1)S(1)}, u32[]{:S(2)}, u32[]{:S(2)}) %collective-permute-start.5) | collective-permute-done | bytes 139296 | tf_op jit(solution)/shard_map/ppermute | solution.py:428
  37.2 1.9 %collective-permute-done.4.refs_5_ = bf16[136,512]{1,0:T(8,128)(2,1)S(1)} collective-permute-done((bf16[136,512]{1,0:T(8,128)(2,1)S(1)}, bf16[136,512]{1,0:T(8,128)(2,1)S(1)}, u32[]{:S(2)}, u32[]{:S(2)}) %collective-permute-start.4) | collective-permute-done | bytes 139296 | tf_op jit(solution)/shard_map/ppermute | solution.py:428
  39.1 1.5 %collective-permute-done.2.refs_3_ = bf16[136,512]{1,0:T(8,128)(2,1)S(1)} collective-permute-done((bf16[136,512]{1,0:T(8,128)(2,1)S(1)}, bf16[136,512]{1,0:T(8,128)(2,1)S(1)}, u32[]{:S(2)}, u32[]{:S(2)}) %collective-permute-start.2) | collective-permute-done | bytes 139296 | tf_op jit(solution)/shard_map/ppermute | solution.py:428
  40.6 1.4 %collective-permute-start.34 = (bf16[128,512]{1,0:T(8,128)(2,1)S(1)}, bf16[128,512]{1,0:T(8,128)(2,1)}, u32[]{:S(2)}, u32[]{:S(2)}) collective-permute-start(bf16[128,512]{1,0:T(8,128)(2,1)S(1)} %collective-permute-done.30.refs_32_), channel_id=1, source_target_pairs={{0,4},{4,0},{8,12},{12,8},{16,20},{20,16},{24,28},{28,24},{1,5},{5... | collective-permute-start | bytes 393224 | tf_op jit(solution)/shard_map/ppermute | solution.py:428
  42.0 2.0 %collective-permute-start.32 = (bf16[128,512]{1,0:T(8,128)(2,1)S(1)}, bf16[128,512]{1,0:T(8,128)(2,1)}, u32[]{:S(2)}, u32[]{:S(2)}) collective-permute-start(bf16[128,512]{1,0:T(8,128)(2,1)S(1)} %collective-permute-done.30.refs_32_), channel_id=1, source_target_pairs={{0,2},{1,3},{2,0},{3,1},{4,6},{5,7},{6,4},{7,5},{8,10},{9,11},{10,... | collective-permute-start | bytes 393224 | tf_op jit(solution)/shard_map/ppermute | solution.py:428
  44.0 0.5 collective-permute-start.6
  44.7 0.9 %collective-permute-done.34.refs_36_ = bf16[128,512]{1,0:T(8,128)(2,1)} collective-permute-done((bf16[128,512]{1,0:T(8,128)(2,1)S(1)}, bf16[128,512]{1,0:T(8,128)(2,1)}, u32[]{:S(2)}, u32[]{:S(2)}) %collective-permute-start.34) | collective-permute-done | bytes 131104 | tf_op jit(solution)/shard_map/ppermute | solution.py:428
  45.7 2.2 %collective-permute-done.32.refs_34_ = bf16[128,512]{1,0:T(8,128)(2,1)} collective-permute-done((bf16[128,512]{1,0:T(8,128)(2,1)S(1)}, bf16[128,512]{1,0:T(8,128)(2,1)}, u32[]{:S(2)}, u32[]{:S(2)}) %collective-permute-start.32) | collective-permute-done | bytes 131104 | tf_op jit(solution)/shard_map/ppermute | solution.py:428
  47.9 0.7 copy-done
  48.5 2.6 %collective-permute-start.36 = (bf16[128,512]{1,0:T(8,128)(2,1)}, bf16[128,512]{1,0:T(8,128)(2,1)}, u32[]{:S(2)}, u32[]{:S(2)}) collective-permute-start(bf16[128,512]{1,0:T(8,128)(2,1)} %collective-permute-done.34.refs_36_), channel_id=1, source_target_pairs={{0,2},{1,3},{2,0},{3,1},{4,6},{5,7},{6,4},{7,5},{8,10},{9,11},{10,... | collective-permute-start | bytes 393224 | tf_op jit(solution)/shard_map/ppermute | solution.py:428
  51.3 0.7 copy-done.2
  52.3 0.7 copy-done.4
  53.5 2.1 %collective-permute-done.36.refs_38_ = bf16[128,512]{1,0:T(8,128)(2,1)} collective-permute-done((bf16[128,512]{1,0:T(8,128)(2,1)}, bf16[128,512]{1,0:T(8,128)(2,1)}, u32[]{:S(2)}, u32[]{:S(2)}) %collective-permute-start.36) | collective-permute-done | bytes 131104 | tf_op jit(solution)/shard_map/ppermute | solution.py:428
  55.6 1.7 %collective-permute-done.37.refs_39_ = bf16[128,512]{1,0:T(8,128)(2,1)} collective-permute-done((bf16[128,512]{1,0:T(8,128)(2,1)}, bf16[128,512]{1,0:T(8,128)(2,1)}, u32[]{:S(2)}, u32[]{:S(2)}) %collective-permute-start.37) | collective-permute-done | bytes 131104 | tf_op jit(solution)/shard_map/ppermute | solution.py:428
  57.3 0.9 %copy-done.1 = bf16[128,512]{1,0:T(8,128)(2,1)S(1)} copy-done((bf16[128,512]{1,0:T(8,128)(2,1)S(1)}, bf16[128,512]{1,0:T(8,128)(2,1)}, u32[]{:S(2)}) %copy-start.1) | copy-done | bytes 131096
  58.2 0.9 %copy-done.3 = bf16[128,512]{1,0:T(8,128)(2,1)S(1)} copy-done((bf16[128,512]{1,0:T(8,128)(2,1)S(1)}, bf16[128,512]{1,0:T(8,128)(2,1)}, u32[]{:S(2)}) %copy-start.3) | copy-done | bytes 131096
  59.1 0.9 %copy-done.5 = bf16[128,512]{1,0:T(8,128)(2,1)S(1)} copy-done((bf16[128,512]{1,0:T(8,128)(2,1)S(1)}, bf16[128,512]{1,0:T(8,128)(2,1)}, u32[]{:S(2)}) %copy-start.5) | copy-done | bytes 131096
  60.0 12.3 %main.1 = (bf16[256,128]{1,0:T(8,128)(2,1)}, bf16[256,128]{1,0:T(8,128)(2,1)}, f32[2,512,128]{2,1,0:T(8,128)}, bf16[256,2048]{1,0:T(8,128)(2,1)}) custom-call(s32[1]{0:T(128)} %bitcast.me_ref, s32[1]{0:T(128)} %bitcast.1.quarter_ref, bf16[136,512]{1,0:T(8,128)(2,1)} %pack.1.refs_0_, bf16[136,512]{1,0:T(8,128)(2,1)S(1)} %collective-permute-done.refs_1_, ...), custom_call_target="tpu_custom_call" | custom-call | flops 5000000000 | bytes 8000000 | tf_op jit(solution)/shard_map/main/pallas_call | solution.py:486
  (60 shorter events, 4.9 us)
Async XLA Ops:
  0.6 10.5 %collective-permute-start.14 = (bf16[128,512]{1,0:T(8,128)(2,1)}, bf16[128,512]{1,0:T(8,128)(2,1)S(1)}, u32[]{:S(2)}, u32[]{:S(2)}) collective-permute-start(bf16[128,512]{1,0:T(8,128)(2,1)} %refs_8_.1), channel_id=1, source_target_pairs={{0,8},{4,12},{8,0},{12,4},{16,24},{20,28},{24,16},{28,20},{1,9},{5... | collective-permute-start | bytes 393224 | tf_op jit(solution)/shard_map/ppermute | solution.py:428
  3.7 7.8 %collective-permute-start.10 = (bf16[128,512]{1,0:T(8,128)(2,1)}, bf16[128,512]{1,0:T(8,128)(2,1)S(1)}, u32[]{:S(2)}, u32[]{:S(2)}) collective-permute-start(bf16[128,512]{1,0:T(8,128)(2,1)} %refs_8_.1), channel_id=1, source_target_pairs={{0,4},{4,0},{8,12},{12,8},{16,20},{20,16},{24,28},{28,24},{1,5},{5... | collective-permute-start | bytes 393224 | tf_op jit(solution)/shard_map/ppermute | solution.py:428
  5.3 6.7 %collective-permute-start.8 = (bf16[128,512]{1,0:T(8,128)(2,1)}, bf16[128,512]{1,0:T(8,128)(2,1)S(1)}, u32[]{:S(2)}, u32[]{:S(2)}) collective-permute-start(bf16[128,512]{1,0:T(8,128)(2,1)} %refs_8_.1), channel_id=1, source_target_pairs={{0,2},{1,3},{2,0},{3,1},{4,6},{5,7},{6,4},{7,5},{8,10},{9,11},{10,... | collective-permute-start | bytes 393224 | tf_op jit(solution)/shard_map/ppermute | solution.py:428
  8.5 14.8 %collective-permute-start.3 = (bf16[136,512]{1,0:T(8,128)(2,1)}, bf16[136,512]{1,0:T(8,128)(2,1)S(1)}, u32[]{:S(2)}, u32[]{:S(2)}) collective-permute-start(bf16[136,512]{1,0:T(8,128)(2,1)} %pack.1.refs_0_), channel_id=1, source_target_pairs={{0,16},{4,20},{8,24},{12,28},{16,0},{20,4},{24,8},{28,12},{1,17},{... | collective-permute-start | bytes 417800 | tf_op jit(solution)/shard_map/ppermute | solution.py:428
  11.1 11.7 %collective-permute-start.22 = (bf16[128,512]{1,0:T(8,128)(2,1)S(1)}, bf16[128,512]{1,0:T(8,128)(2,1)S(1)}, u32[]{:S(2)}, u32[]{:S(2)}) collective-permute-start(bf16[128,512]{1,0:T(8,128)(2,1)S(1)} %copy-done.6), channel_id=1, source_target_pairs={{0,16},{4,20},{8,24},{12,28},{16,0},{20,4},{24,8},{28,12},{1,17},{... | collective-permute-start | bytes 393224 | tf_op jit(solution)/shard_map/ppermute | solution.py:428
  11.5 11.8 %collective-permute-start.1 = (bf16[136,512]{1,0:T(8,128)(2,1)}, bf16[136,512]{1,0:T(8,128)(2,1)S(1)}, u32[]{:S(2)}, u32[]{:S(2)}) collective-permute-start(bf16[136,512]{1,0:T(8,128)(2,1)} %pack.1.refs_0_), channel_id=1, source_target_pairs={{0,8},{4,12},{8,0},{12,4},{16,24},{20,28},{24,16},{28,20},{1,9},{5... | collective-permute-start | bytes 417800 | tf_op jit(solution)/shard_map/ppermute | solution.py:428
  12.0 12.9 %collective-permute-start = (bf16[136,512]{1,0:T(8,128)(2,1)}, bf16[136,512]{1,0:T(8,128)(2,1)S(1)}, u32[]{:S(2)}, u32[]{:S(2)}) collective-permute-start(bf16[136,512]{1,0:T(8,128)(2,1)} %pack.1.refs_0_), channel_id=1, source_target_pairs={{0,4},{4,0},{8,12},{12,8},{16,20},{20,16},{24,28},{28,24},{1,5},{5... | collective-permute-start | bytes 417800 | tf_op jit(solution)/shard_map/ppermute | solution.py:428
  13.3 11.7 %collective-permute-start.18 = (bf16[128,512]{1,0:T(8,128)(2,1)S(1)}, bf16[128,512]{1,0:T(8,128)(2,1)S(1)}, u32[]{:S(2)}, u32[]{:S(2)}) collective-permute-start(bf16[128,512]{1,0:T(8,128)(2,1)S(1)} %collective-permute-done.14.refs_16_), channel_id=1, source_target_pairs={{0,4},{4,0},{8,12},{12,8},{16,20},{20,16},{24,28},{28,24},{1,5},{5... | collective-permute-start | bytes 393224 | tf_op jit(solution)/shard_map/ppermute | solution.py:428
  22.8 6.3 %collective-permute-start.16 = (bf16[128,512]{1,0:T(8,128)(2,1)S(1)}, bf16[128,512]{1,0:T(8,128)(2,1)S(1)}, u32[]{:S(2)}, u32[]{:S(2)}) collective-permute-start(bf16[128,512]{1,0:T(8,128)(2,1)S(1)} %collective-permute-done.14.refs_16_), channel_id=1, source_target_pairs={{0,2},{1,3},{2,0},{3,1},{4,6},{5,7},{6,4},{7,5},{8,10},{9,11},{10,... | collective-permute-start | bytes 393224 | tf_op jit(solution)/shard_map/ppermute | solution.py:428
  23.3 5.8 %collective-permute-start.15 = (bf16[128,512]{1,0:T(8,128)(2,1)S(1)}, bf16[128,512]{1,0:T(8,128)(2,1)S(1)}, u32[]{:S(2)}, u32[]{:S(2)}) collective-permute-start(bf16[128,512]{1,0:T(8,128)(2,1)S(1)} %collective-permute-done.14.refs_16_), channel_id=1, source_target_pairs={{0,1},{1,0},{2,3},{3,2},{4,5},{5,4},{6,7},{7,6},{8,9},{9,8},{10,11... | collective-permute-start | bytes 393224 | tf_op jit(solution)/shard_map/ppermute | solution.py:428
  23.3 7.2 %collective-permute-start.12 = (bf16[128,512]{1,0:T(8,128)(2,1)S(1)}, bf16[128,512]{1,0:T(8,128)(2,1)S(1)}, u32[]{:S(2)}, u32[]{:S(2)}) collective-permute-start(bf16[128,512]{1,0:T(8,128)(2,1)S(1)} %collective-permute-done.10.refs_12_), channel_id=1, source_target_pairs={{0,2},{1,3},{2,0},{3,1},{4,6},{5,7},{6,4},{7,5},{8,10},{9,11},{10,... | collective-permute-start | bytes 393224 | tf_op jit(solution)/shard_map/ppermute | solution.py:428
  24.9 6.2 %collective-permute-start.11 = (bf16[128,512]{1,0:T(8,128)(2,1)S(1)}, bf16[128,512]{1,0:T(8,128)(2,1)S(1)}, u32[]{:S(2)}, u32[]{:S(2)}) collective-permute-start(bf16[128,512]{1,0:T(8,128)(2,1)S(1)} %collective-permute-done.10.refs_12_), channel_id=1, source_target_pairs={{0,1},{1,0},{2,3},{3,2},{4,5},{5,4},{6,7},{7,6},{8,9},{9,8},{10,11... | collective-permute-start | bytes 393224 | tf_op jit(solution)/shard_map/ppermute | solution.py:428
  25.1 6.1 %collective-permute-start.9 = (bf16[128,512]{1,0:T(8,128)(2,1)S(1)}, bf16[128,512]{1,0:T(8,128)(2,1)S(1)}, u32[]{:S(2)}, u32[]{:S(2)}) collective-permute-start(bf16[128,512]{1,0:T(8,128)(2,1)S(1)} %collective-permute-done.8.refs_10_), channel_id=1, source_target_pairs={{0,1},{1,0},{2,3},{3,2},{4,5},{5,4},{6,7},{7,6},{8,9},{9,8},{10,11... | collective-permute-start | bytes 393224 | tf_op jit(solution)/shard_map/ppermute | solution.py:428
  29.1 5.0 %collective-permute-start.30 = (bf16[128,512]{1,0:T(8,128)(2,1)S(1)}, bf16[128,512]{1,0:T(8,128)(2,1)S(1)}, u32[]{:S(2)}, u32[]{:S(2)}) collective-permute-start(bf16[128,512]{1,0:T(8,128)(2,1)S(1)} %collective-permute-done.22.refs_24_), channel_id=1, source_target_pairs={{0,8},{4,12},{8,0},{12,4},{16,24},{20,28},{24,16},{28,20},{1,9},{5... | collective-permute-start | bytes 393224 | tf_op jit(solution)/shard_map/ppermute | solution.py:428
  29.1 5.4 %collective-permute-start.26 = (bf16[128,512]{1,0:T(8,128)(2,1)S(1)}, bf16[128,512]{1,0:T(8,128)(2,1)S(1)}, u32[]{:S(2)}, u32[]{:S(2)}) collective-permute-start(bf16[128,512]{1,0:T(8,128)(2,1)S(1)} %collective-permute-done.22.refs_24_), channel_id=1, source_target_pairs={{0,4},{4,0},{8,12},{12,8},{16,20},{20,16},{24,28},{28,24},{1,5},{5... | collective-permute-start | bytes 393224 | tf_op jit(solution)/shard_map/ppermute | solution.py:428
  30.6 5.5 %collective-permute-start.24 = (bf16[128,512]{1,0:T(8,128)(2,1)S(1)}, bf16[128,512]{1,0:T(8,128)(2,1)S(1)}, u32[]{:S(2)}, u32[]{:S(2)}) collective-permute-start(bf16[128,512]{1,0:T(8,128)(2,1)S(1)} %collective-permute-done.22.refs_24_), channel_id=1, source_target_pairs={{0,2},{1,3},{2,0},{3,1},{4,6},{5,7},{6,4},{7,5},{8,10},{9,11},{10,... | collective-permute-start | bytes 393224 | tf_op jit(solution)/shard_map/ppermute | solution.py:428
  31.1 5.1 %collective-permute-start.23 = (bf16[128,512]{1,0:T(8,128)(2,1)S(1)}, bf16[128,512]{1,0:T(8,128)(2,1)S(1)}, u32[]{:S(2)}, u32[]{:S(2)}) collective-permute-start(bf16[128,512]{1,0:T(8,128)(2,1)S(1)} %collective-permute-done.22.refs_24_), channel_id=1, source_target_pairs={{0,1},{1,0},{2,3},{3,2},{4,5},{5,4},{6,7},{7,6},{8,9},{9,8},{10,11... | collective-permute-start | bytes 393224 | tf_op jit(solution)/shard_map/ppermute | solution.py:428
  31.1 6.1 %collective-permute-start.5 = (bf16[136,512]{1,0:T(8,128)(2,1)S(1)}, bf16[136,512]{1,0:T(8,128)(2,1)S(1)}, u32[]{:S(2)}, u32[]{:S(2)}) collective-permute-start(bf16[136,512]{1,0:T(8,128)(2,1)S(1)} %collective-permute-done.3.refs_4_), channel_id=1, source_target_pairs={{0,8},{4,12},{8,0},{12,4},{16,24},{20,28},{24,16},{28,20},{1,9},{5... | collective-permute-start | bytes 417800 | tf_op jit(solution)/shard_map/ppermute | solution.py:428
  34.1 5.1 %collective-permute-start.4 = (bf16[136,512]{1,0:T(8,128)(2,1)S(1)}, bf16[136,512]{1,0:T(8,128)(2,1)S(1)}, u32[]{:S(2)}, u32[]{:S(2)}) collective-permute-start(bf16[136,512]{1,0:T(8,128)(2,1)S(1)} %collective-permute-done.3.refs_4_), channel_id=1, source_target_pairs={{0,4},{4,0},{8,12},{12,8},{16,20},{20,16},{24,28},{28,24},{1,5},{5... | collective-permute-start | bytes 417800 | tf_op jit(solution)/shard_map/ppermute | solution.py:428
  34.5 6.1 %collective-permute-start.2 = (bf16[136,512]{1,0:T(8,128)(2,1)S(1)}, bf16[136,512]{1,0:T(8,128)(2,1)S(1)}, u32[]{:S(2)}, u32[]{:S(2)}) collective-permute-start(bf16[136,512]{1,0:T(8,128)(2,1)S(1)} %collective-permute-done.1.refs_2_), channel_id=1, source_target_pairs={{0,4},{4,0},{8,12},{12,8},{16,20},{20,16},{24,28},{28,24},{1,5},{5... | collective-permute-start | bytes 417800 | tf_op jit(solution)/shard_map/ppermute | solution.py:428
  36.1 5.9 %collective-permute-start.20 = (bf16[128,512]{1,0:T(8,128)(2,1)S(1)}, bf16[128,512]{1,0:T(8,128)(2,1)S(1)}, u32[]{:S(2)}, u32[]{:S(2)}) collective-permute-start(bf16[128,512]{1,0:T(8,128)(2,1)S(1)} %collective-permute-done.18.refs_20_), channel_id=1, source_target_pairs={{0,2},{1,3},{2,0},{3,1},{4,6},{5,7},{6,4},{7,5},{8,10},{9,11},{10,... | collective-permute-start | bytes 393224 | tf_op jit(solution)/shard_map/ppermute | solution.py:428
  36.3 7.7 %collective-permute-start.19 = (bf16[128,512]{1,0:T(8,128)(2,1)S(1)}, bf16[128,512]{1,0:T(8,128)(2,1)S(1)}, u32[]{:S(2)}, u32[]{:S(2)}) collective-permute-start(bf16[128,512]{1,0:T(8,128)(2,1)S(1)} %collective-permute-done.18.refs_20_), channel_id=1, source_target_pairs={{0,1},{1,0},{2,3},{3,2},{4,5},{5,4},{6,7},{7,6},{8,9},{9,8},{10,11... | collective-permute-start | bytes 393224 | tf_op jit(solution)/shard_map/ppermute | solution.py:428
  37.2 6.8 %collective-permute-start.17 = (bf16[128,512]{1,0:T(8,128)(2,1)S(1)}, bf16[128,512]{1,0:T(8,128)(2,1)S(1)}, u32[]{:S(2)}, u32[]{:S(2)}) collective-permute-start(bf16[128,512]{1,0:T(8,128)(2,1)S(1)} %collective-permute-done.16.refs_18_), channel_id=1, source_target_pairs={{0,1},{1,0},{2,3},{3,2},{4,5},{5,4},{6,7},{7,6},{8,9},{9,8},{10,11... | collective-permute-start | bytes 393224 | tf_op jit(solution)/shard_map/ppermute | solution.py:428
  39.1 5.4 %collective-permute-start.13 = (bf16[128,512]{1,0:T(8,128)(2,1)S(1)}, bf16[128,512]{1,0:T(8,128)(2,1)S(1)}, u32[]{:S(2)}, u32[]{:S(2)}) collective-permute-start(bf16[128,512]{1,0:T(8,128)(2,1)S(1)} %collective-permute-done.12.refs_14_), channel_id=1, source_target_pairs={{0,1},{1,0},{2,3},{3,2},{4,5},{5,4},{6,7},{7,6},{8,9},{9,8},{10,11... | collective-permute-start | bytes 393224 | tf_op jit(solution)/shard_map/ppermute | solution.py:428
  40.6 5.1 %collective-permute-start.34 = (bf16[128,512]{1,0:T(8,128)(2,1)S(1)}, bf16[128,512]{1,0:T(8,128)(2,1)}, u32[]{:S(2)}, u32[]{:S(2)}) collective-permute-start(bf16[128,512]{1,0:T(8,128)(2,1)S(1)} %collective-permute-done.30.refs_32_), channel_id=1, source_target_pairs={{0,4},{4,0},{8,12},{12,8},{16,20},{20,16},{24,28},{28,24},{1,5},{5... | collective-permute-start | bytes 393224 | tf_op jit(solution)/shard_map/ppermute | solution.py:428
  42.0 5.8 %collective-permute-start.32 = (bf16[128,512]{1,0:T(8,128)(2,1)S(1)}, bf16[128,512]{1,0:T(8,128)(2,1)}, u32[]{:S(2)}, u32[]{:S(2)}) collective-permute-start(bf16[128,512]{1,0:T(8,128)(2,1)S(1)} %collective-permute-done.30.refs_32_), channel_id=1, source_target_pairs={{0,2},{1,3},{2,0},{3,1},{4,6},{5,7},{6,4},{7,5},{8,10},{9,11},{10,... | collective-permute-start | bytes 393224 | tf_op jit(solution)/shard_map/ppermute | solution.py:428
  44.0 9.2 %collective-permute-start.6 = (bf16[136,512]{1,0:T(8,128)(2,1)S(1)}, bf16[136,512]{1,0:T(8,128)(2,1)S(1)}, u32[]{:S(2)}, u32[]{:S(2)}) collective-permute-start(bf16[136,512]{1,0:T(8,128)(2,1)S(1)} %collective-permute-done.5.refs_6_), channel_id=1, source_target_pairs={{0,4},{4,0},{8,12},{12,8},{16,20},{20,16},{24,28},{28,24},{1,5},{5... | collective-permute-start | bytes 417800 | tf_op jit(solution)/shard_map/ppermute | solution.py:428
  44.5 6.6 %collective-permute-start.28 = (bf16[128,512]{1,0:T(8,128)(2,1)S(1)}, bf16[128,512]{1,0:T(8,128)(2,1)}, u32[]{:S(2)}, u32[]{:S(2)}) collective-permute-start(bf16[128,512]{1,0:T(8,128)(2,1)S(1)} %collective-permute-done.26.refs_28_), channel_id=1, source_target_pairs={{0,2},{1,3},{2,0},{3,1},{4,6},{5,7},{6,4},{7,5},{8,10},{9,11},{10,... | collective-permute-start | bytes 393224 | tf_op jit(solution)/shard_map/ppermute | solution.py:428
  45.7 5.7 %collective-permute-start.27 = (bf16[128,512]{1,0:T(8,128)(2,1)S(1)}, bf16[128,512]{1,0:T(8,128)(2,1)S(1)}, u32[]{:S(2)}, u32[]{:S(2)}) collective-permute-start(bf16[128,512]{1,0:T(8,128)(2,1)S(1)} %collective-permute-done.26.refs_28_), channel_id=1, source_target_pairs={{0,1},{1,0},{2,3},{3,2},{4,5},{5,4},{6,7},{7,6},{8,9},{9,8},{10,11... | collective-permute-start | bytes 393224 | tf_op jit(solution)/shard_map/ppermute | solution.py:428
  47.8 4.4 %collective-permute-start.25 = (bf16[128,512]{1,0:T(8,128)(2,1)S(1)}, bf16[128,512]{1,0:T(8,128)(2,1)S(1)}, u32[]{:S(2)}, u32[]{:S(2)}) collective-permute-start(bf16[128,512]{1,0:T(8,128)(2,1)S(1)} %collective-permute-done.24.refs_26_), channel_id=1, source_target_pairs={{0,1},{1,0},{2,3},{3,2},{4,5},{5,4},{6,7},{7,6},{8,9},{9,8},{10,11... | collective-permute-start | bytes 393224 | tf_op jit(solution)/shard_map/ppermute | solution.py:428
  48.5 7.1 %collective-permute-start.36 = (bf16[128,512]{1,0:T(8,128)(2,1)}, bf16[128,512]{1,0:T(8,128)(2,1)}, u32[]{:S(2)}, u32[]{:S(2)}) collective-permute-start(bf16[128,512]{1,0:T(8,128)(2,1)} %collective-permute-done.34.refs_36_), channel_id=1, source_target_pairs={{0,2},{1,3},{2,0},{3,1},{4,6},{5,7},{6,4},{7,5},{8,10},{9,11},{10,... | collective-permute-start | bytes 393224 | tf_op jit(solution)/shard_map/ppermute | solution.py:428
  51.1 4.5 %collective-permute-start.35 = (bf16[128,512]{1,0:T(8,128)(2,1)}, bf16[128,512]{1,0:T(8,128)(2,1)}, u32[]{:S(2)}, u32[]{:S(2)}) collective-permute-start(bf16[128,512]{1,0:T(8,128)(2,1)} %collective-permute-done.34.refs_36_), channel_id=1, source_target_pairs={{0,1},{1,0},{2,3},{3,2},{4,5},{5,4},{6,7},{7,6},{8,9},{9,8},{10,11... | collective-permute-start | bytes 393224 | tf_op jit(solution)/shard_map/ppermute | solution.py:428
  (13 other events, 25.5 us)

commit v4 on v3

--- a/solution.py
+++ b/solution.py
@@ -252,7 +252,6 @@
     tokens = blocks * BLOCK
     wide = heads * width
     part = grads[0].shape[1]
-    model = 4 * part
     me = me_ref[0]
     quarter = quarter_ref[0]
 
@@ -309,6 +308,7 @@
         return dot_nt(k_ref[:seen, columns], q_ref[tile * TILE : seen, columns])
 
     steps = [(head, tile) for tile in range(tokens // TILE) for head in range(heads)]
+    half = len(steps) - tokens // TILE
     ahead = scored(*steps[0])
     for at, (head, tile) in enumerate(steps):
         columns = slice(head * width, (head + 1) * width)
@@ -317,6 +317,12 @@
         scores = ahead
         if at + 1 < len(steps):
             ahead = scored(*steps[at + 1])
+        if at == half:
+            for copy in late:
+                copy.wait()
+        if at >= half:
+            span = slice((at - half) * TILE, (at - half + 1) * TILE)
+            do_t_ref[:, span] = dot_nt(weight_ref[...], go_ref[span, :]).astype(BF16)
         last = jnp.where(causal_tile(), scores[seen - TILE :], -jnp.inf)
         scores = last if tile == 0 else jnp.concatenate([scores[: seen - TILE], last], axis=0)
         top = jnp.max(scores, axis=0, keepdims=True)
@@ -326,17 +332,6 @@
         att_t_ref[columns, here] = (mixed / total).astype(BF16)
         lse_ref[head : head + 1, here] = top + jnp.log(total)
 
-    for copy in late:
-        copy.wait()
-    for tile in range(model // TILE):
-        columns = slice(tile * TILE, (tile + 1) * TILE)
-        dweight_ref[:, columns] = dot_nn(att_t_ref[...], go_ref[:, columns]).astype(BF16)
-    outputs = [pltpu.make_async_copy(dweight_ref, dweight_any, out_sems.at[1])]
-    outputs[0].start()
-    for tile in range(tokens // TILE):
-        here = slice(tile * TILE, (tile + 1) * TILE)
-        do_t_ref[:, here] = dot_nt(weight_ref[...], go_ref[here, :]).astype(BF16)
-
     mine = pl.ds(pl.multiple_of(me * BLOCK, BLOCK), BLOCK)
     dq_heads, dv_heads = [], []
     for head in range(heads):
@@ -358,6 +353,8 @@
         scores, grad = ahead
         if at + 1 < len(steps):
             ahead = products(*steps[at + 1])
+        span = slice(at * TILE, (at + 1) * TILE)
+        dweight_ref[:, span] = dot_nn(att_t_ref[...], go_ref[:, span]).astype(BF16)
         weights = jnp.exp(scores - lse_ref[head : head + 1, here])
         last = jnp.where(causal_tile(), weights[seen - TILE :], 0.0)
         weights = last if tile == 0 else jnp.concatenate([weights[: seen - TILE], last], axis=0)
@@ -368,28 +365,38 @@
         else:
             dk_ref[head, : seen - TILE, :] += term[: seen - TILE]
             dk_ref[head, seen - TILE : seen, :] = term[seen - TILE :]
+    outputs = [pltpu.make_async_copy(dweight_ref, dweight_any, out_sems.at[1])]
+    outputs[0].start()
     for head in range(heads):
         columns = slice(head * width, (head + 1) * width)
         dbook_ref[head] = dot_nn(hot_ref[head], dk_ref[head].astype(BF16))
         outputs.append(pltpu.make_async_copy(dbook_ref.at[head], dbook_any.at[head], out_sems.at[2 + head]))
         outputs[-1].start()
-        scores = dot_nt(k_ref[mine, columns], q_ref[:, columns])
-        key_at = lax.broadcasted_iota(jnp.int32, (BLOCK, tokens), 0) + me * BLOCK
-        query_at = lax.broadcasted_iota(jnp.int32, (BLOCK, tokens), 1)
-        weights = jnp.exp(jnp.where(key_at <= query_at, scores - lse_ref[head : head + 1, :], -jnp.inf))
-        dv_heads.append(dot_nt(weights.astype(BF16), do_t_ref[columns, :]).astype(BF16))
+    early_key = lax.broadcasted_iota(jnp.int32, (BLOCK, tokens), 0) + me * BLOCK
+    later_query = lax.broadcasted_iota(jnp.int32, (BLOCK, tokens), 1)
+    any_key = lax.broadcasted_iota(jnp.int32, (tokens, BLOCK), 0)
+    own_query = lax.broadcasted_iota(jnp.int32, (tokens, BLOCK), 1) + me * BLOCK
+    staged = []
+    for head in range(heads):
+        columns = slice(head * width, (head + 1) * width)
         for block in range(blocks):
             span = slice(block * BLOCK, (block + 1) * BLOCK)
-            rows_ref[0, block : block + 1, :] = lse_ref[head : head + 1, span]
-            rows_ref[1, block : block + 1, :] = delta_ref[head : head + 1, span]
-            own_ref[block] = do_t_ref[columns, span]
-        own_lse = rows_ref[0, pl.ds(me, 1), :]
-        own_delta = rows_ref[1, pl.ds(me, 1), :]
-        scores = dot_nt(k_ref[:, columns], q_ref[mine, columns])
-        key_at = lax.broadcasted_iota(jnp.int32, (tokens, BLOCK), 0)
-        query_at = lax.broadcasted_iota(jnp.int32, (tokens, BLOCK), 1) + me * BLOCK
-        weights = jnp.exp(jnp.where(key_at <= query_at, scores - own_lse, -jnp.inf))
-        grad = dot_nn(v_ref[:, columns], own_ref[me])
+            rows_ref[2 * head, block : block + 1, :] = lse_ref[head : head + 1, span]
+            rows_ref[2 * head + 1, block : block + 1, :] = delta_ref[head : head + 1, span]
+            own_ref[head, block] = do_t_ref[columns, span]
+        staged.append((
+            dot_nt(k_ref[mine, columns], q_ref[:, columns]),
+            dot_nt(k_ref[:, columns], q_ref[mine, columns]),
+            dot_nn(v_ref[:, columns], own_ref[head, me]),
+        ))
+    for head, (key_scores, query_scores, grad) in enumerate(staged):
+        columns = slice(head * width, (head + 1) * width)
+        weights = jnp.exp(jnp.where(
+            early_key <= later_query, key_scores - lse_ref[head : head + 1, :], -jnp.inf))
+        dv_heads.append(dot_nt(weights.astype(BF16), do_t_ref[columns, :]).astype(BF16))
+        own_lse = rows_ref[2 * head, pl.ds(me, 1), :]
+        own_delta = rows_ref[2 * head + 1, pl.ds(me, 1), :]
+        weights = jnp.exp(jnp.where(any_key <= own_query, query_scores - own_lse, -jnp.inf))
         grad = (weights * (grad - own_delta)).astype(BF16)
         dq_heads.append(dot_nn(k_t_ref[columns, :], grad).T.astype(BF16))
     mix = by_head(BLOCK, 1)
@@ -420,8 +427,12 @@
         out_shape=jax.ShapeDtypeStruct((BLOCK + 8, part), BF16),
         in_specs=[VMEM] * 3,
         out_specs=VMEM,
+        compiler_params=pltpu.CompilerParams(vmem_limit_bytes=4 * 2**20),
         name="pack",
-    )(queries.reshape(heads * BLOCK, width), values.reshape(heads * BLOCK, width), codes)
+    )(*(
+        pltpu.with_memory_space_constraint(array, pltpu.HBM)
+        for array in (queries.reshape(heads * BLOCK, width), values.reshape(heads * BLOCK, width), codes)
+    ))
 
     def exchange(array, axis, flip):
         pairs = [(i, i ^ flip) for i in range(lax.axis_size(axis))]
@@ -466,8 +477,8 @@
             pltpu.VMEM((wide, tokens), BF16),
             pltpu.VMEM((heads, tokens, width), F32),
             pltpu.VMEM((8, tokens), F32),
-            pltpu.VMEM((2, blocks, BLOCK), F32),
-            pltpu.VMEM((blocks, width, BLOCK), BF16),
+            pltpu.VMEM((2 * heads, blocks, BLOCK), F32),
+            pltpu.VMEM((heads, blocks, width, BLOCK), BF16),
             pltpu.VMEM((heads, code_total, width), F32),
             pltpu.VMEM((wide, 4 * part), BF16),
             pltpu.VMEM((heads, code_total, width), BF16),
@@ -479,9 +490,9 @@
         cost_estimate=pl.CostEstimate(flops=5 * 10**9, bytes_accessed=8 * 10**6, transcendentals=10**6),
         name="main",
     )
-    slots[0], grads[0], codebook, out_weight = (
+    grads[0], codebook, out_weight = (
         pltpu.with_memory_space_constraint(array, pltpu.HBM)
-        for array in (slots[0], grads[0], codebook, out_weight)
+        for array in (grads[0], codebook, out_weight)
     )
     dq, dv, dbook, dweight = main(me, quarter, *slots, *grads, codebook, out_weight)
     shape = (tok_here, heads, width)

time: 72.6 us -> 70.9 us (0.977)
  waiting for transfers between devices: 27.1 us -> 24.5 us
  local copies, waits for them, and re-layouts: 4.69 us -> 6.24 us
  Pallas kernels: 14 us -> 12.5 us
  starting transfers between devices: 25.8 us -> 26.6 us
    ppermute x38, waiting for transfers between devices: 27.1 us -> 24.5 us  [exchange(): return lax.ppermute(array, axis, pairs)]
    unnamed x14 -> x18, local copies, waits for them, and re-layouts: 4.69 us -> 6.24 us
    pallas_call x1, Pallas kernels: 12.3 us -> 11.4 us  [gathered_body(): main(me, quarter, *slots, *grads, codebook, out_weight)]
    ppermute x38, starting transfers between devices: 25.8 us -> 26.6 us  [exchange(): return lax.ppermute(array, axis, pairs)]
  transfers between devices with their start and end apart: 38 -> 38, of which waited for: 11 -> 13; matrix products, arithmetic and copies ran while one was open for 0% -> 0% of each run, Pallas kernels for 2% -> 2%
where the time goes in v4:
time: 70.9 us; the launch traced here: 70.7 us
  starting transfers between devices  26.6 us (38%)
  waiting for transfers between devices  24.5 us (35%)
  Pallas kernels  12.5 us (18%)
  local copies, waits for them, and re-layouts  6.24 us (9%)
  between operations  0.88 us (1%)
    ppermute x38, starting transfers between devices, exchange(): return lax.ppermute(array, axis, pairs)  26.6 us
    ppermute x38, waiting for transfers between devices, exchange(): return lax.ppermute(array, axis, pairs)  24.5 us
    pallas_call x1, Pallas kernels, gathered_body(): main(me, quarter, *slots, *grads, codebook, out_weight)  11.4 us
    unnamed x18, local copies, waits for them, and re-layouts  6.24 us
  transfers between devices with their start and end apart: 38, of which 13 were waited for; matrix products, arithmetic and copies ran while one was open for 0% of the time, Pallas kernels for 2%

profile of v4, /device:TPU:0, one launch (start us, length us, event | category | flops | bytes accessed | tf_op | source)
XLA Modules:
  0.0 70.7 jit_solution(3536688658347724713)
XLA Ops:
  0.6 3.1 %collective-permute-start.14 = (bf16[128,512]{1,0:T(8,128)(2,1)}, bf16[128,512]{1,0:T(8,128)(2,1)S(1)}, u32[]{:S(2)}, u32[]{:S(2)}) collective-permute-start(bf16[128,512]{1,0:T(8,128)(2,1)} %refs_8_.1), channel_id=1, source_target_pairs={{0,8},{4,12},{8,0},{12,4},{16,24},{20,28},{24,16},{28,20},{1,9},{5... | collective-permute-start | bytes 393224 | tf_op jit(solution)/shard_map/ppermute | solution.py:439
  3.7 1.5 %collective-permute-start.10 = (bf16[128,512]{1,0:T(8,128)(2,1)}, bf16[128,512]{1,0:T(8,128)(2,1)S(1)}, u32[]{:S(2)}, u32[]{:S(2)}) collective-permute-start(bf16[128,512]{1,0:T(8,128)(2,1)} %refs_8_.1), channel_id=1, source_target_pairs={{0,4},{4,0},{8,12},{12,8},{16,20},{20,16},{24,28},{28,24},{1,5},{5... | collective-permute-start | bytes 393224 | tf_op jit(solution)/shard_map/ppermute | solution.py:439
  5.3 1.5 %collective-permute-start.8 = (bf16[128,512]{1,0:T(8,128)(2,1)}, bf16[128,512]{1,0:T(8,128)(2,1)S(1)}, u32[]{:S(2)}, u32[]{:S(2)}) collective-permute-start(bf16[128,512]{1,0:T(8,128)(2,1)} %refs_8_.1), channel_id=1, source_target_pairs={{0,2},{1,3},{2,0},{3,1},{4,6},{5,7},{6,4},{7,5},{8,10},{9,11},{10,... | collective-permute-start | bytes 393224 | tf_op jit(solution)/shard_map/ppermute | solution.py:439
  6.8 1.1 %pack.1.refs_0_ = bf16[136,512]{1,0:T(8,128)(2,1)S(1)} custom-call(bf16[256,128]{1,0:T(8,128)(2,1)} %bitcast.6, bf16[256,128]{1,0:T(8,128)(2,1)} %bitcast.7, s32[2,128]{1,0:T(2,128)} %code_ref.1), custom_call_target="tpu_custom_call" | custom-call | tf_op jit(solution)/shard_map/pack/pallas_call | solution.py:425
  7.9 2.7 %collective-permute-start.3 = (bf16[136,512]{1,0:T(8,128)(2,1)S(1)}, bf16[136,512]{1,0:T(8,128)(2,1)S(1)}, u32[]{:S(2)}, u32[]{:S(2)}) collective-permute-start(bf16[136,512]{1,0:T(8,128)(2,1)S(1)} %pack.1.refs_0_), channel_id=1, source_target_pairs={{0,16},{4,20},{8,24},{12,28},{16,0},{20,4},{24,8},{28,12},{1,17},{... | collective-permute-start | bytes 417800 | tf_op jit(solution)/shard_map/ppermute | solution.py:439
  10.9 0.9 %collective-permute-start.1 = (bf16[136,512]{1,0:T(8,128)(2,1)S(1)}, bf16[136,512]{1,0:T(8,128)(2,1)S(1)}, u32[]{:S(2)}, u32[]{:S(2)}) collective-permute-start(bf16[136,512]{1,0:T(8,128)(2,1)S(1)} %pack.1.refs_0_), channel_id=1, source_target_pairs={{0,8},{4,12},{8,0},{12,4},{16,24},{20,28},{24,16},{28,20},{1,9},{5... | collective-permute-start | bytes 417800 | tf_op jit(solution)/shard_map/ppermute | solution.py:439
  11.8 1.5 %collective-permute-start = (bf16[136,512]{1,0:T(8,128)(2,1)S(1)}, bf16[136,512]{1,0:T(8,128)(2,1)S(1)}, u32[]{:S(2)}, u32[]{:S(2)}) collective-permute-start(bf16[136,512]{1,0:T(8,128)(2,1)S(1)} %pack.1.refs_0_), channel_id=1, source_target_pairs={{0,4},{4,0},{8,12},{12,8},{16,20},{20,16},{24,28},{28,24},{1,5},{5... | collective-permute-start | bytes 417800 | tf_op jit(solution)/shard_map/ppermute | solution.py:439
  13.8 8.2 %collective-permute-done.22.refs_24_ = bf16[128,512]{1,0:T(8,128)(2,1)S(1)} collective-permute-done((bf16[128,512]{1,0:T(8,128)(2,1)S(1)}, bf16[128,512]{1,0:T(8,128)(2,1)S(1)}, u32[]{:S(2)}, u32[]{:S(2)}) %collective-permute-start.22) | collective-permute-done | bytes 131104 | tf_op jit(solution)/shard_map/ppermute | solution.py:439
  22.6 1.5 %collective-permute-start.12 = (bf16[128,512]{1,0:T(8,128)(2,1)S(1)}, bf16[128,512]{1,0:T(8,128)(2,1)S(1)}, u32[]{:S(2)}, u32[]{:S(2)}) collective-permute-start(bf16[128,512]{1,0:T(8,128)(2,1)S(1)} %collective-permute-done.10.refs_12_), channel_id=1, source_target_pairs={{0,2},{1,3},{2,0},{3,1},{4,6},{5,7},{6,4},{7,5},{8,10},{9,11},{10,... | collective-permute-start | bytes 393224 | tf_op jit(solution)/shard_map/ppermute | solution.py:439
  24.6 3.6 %collective-permute-done.16.refs_18_ = bf16[128,512]{1,0:T(8,128)(2,1)S(1)} collective-permute-done((bf16[128,512]{1,0:T(8,128)(2,1)S(1)}, bf16[128,512]{1,0:T(8,128)(2,1)S(1)}, u32[]{:S(2)}, u32[]{:S(2)}) %collective-permute-start.16) | collective-permute-done | bytes 131104 | tf_op jit(solution)/shard_map/ppermute | solution.py:439
  28.2 0.7 collective-permute-start.26
  28.9 0.8 %collective-permute-done.12.refs_14_ = bf16[128,512]{1,0:T(8,128)(2,1)S(1)} collective-permute-done((bf16[128,512]{1,0:T(8,128)(2,1)S(1)}, bf16[128,512]{1,0:T(8,128)(2,1)S(1)}, u32[]{:S(2)}, u32[]{:S(2)}) %collective-permute-start.12) | collective-permute-done | bytes 131104 | tf_op jit(solution)/shard_map/ppermute | solution.py:439
  30.4 0.7 collective-permute-start.5
  31.1 2.1 %collective-permute-done.30.refs_32_ = bf16[128,512]{1,0:T(8,128)(2,1)S(1)} collective-permute-done((bf16[128,512]{1,0:T(8,128)(2,1)S(1)}, bf16[128,512]{1,0:T(8,128)(2,1)S(1)}, u32[]{:S(2)}, u32[]{:S(2)}) %collective-permute-start.30) | collective-permute-done | bytes 131104 | tf_op jit(solution)/shard_map/ppermute | solution.py:439
  33.2 0.7 collective-permute-start.4
  33.9 1.3 %collective-permute-start.2 = (bf16[136,512]{1,0:T(8,128)(2,1)S(1)}, bf16[136,512]{1,0:T(8,128)(2,1)S(1)}, u32[]{:S(2)}, u32[]{:S(2)}) collective-permute-start(bf16[136,512]{1,0:T(8,128)(2,1)S(1)} %collective-permute-done.1.refs_2_), channel_id=1, source_target_pairs={{0,4},{4,0},{8,12},{12,8},{16,20},{20,16},{24,28},{28,24},{1,5},{5... | collective-permute-start | bytes 417800 | tf_op jit(solution)/shard_map/ppermute | solution.py:439
  35.5 1.1 %collective-permute-done.5.refs_6_ = bf16[136,512]{1,0:T(8,128)(2,1)S(1)} collective-permute-done((bf16[136,512]{1,0:T(8,128)(2,1)S(1)}, bf16[136,512]{1,0:T(8,128)(2,1)S(1)}, u32[]{:S(2)}, u32[]{:S(2)}) %collective-permute-start.5) | collective-permute-done | bytes 139296 | tf_op jit(solution)/shard_map/ppermute | solution.py:439
  36.5 1.8 %collective-permute-done.4.refs_5_ = bf16[136,512]{1,0:T(8,128)(2,1)S(1)} collective-permute-done((bf16[136,512]{1,0:T(8,128)(2,1)S(1)}, bf16[136,512]{1,0:T(8,128)(2,1)S(1)}, u32[]{:S(2)}, u32[]{:S(2)}) %collective-permute-start.4) | collective-permute-done | bytes 139296 | tf_op jit(solution)/shard_map/ppermute | solution.py:439
  38.3 1.5 %collective-permute-done.2.refs_3_ = bf16[136,512]{1,0:T(8,128)(2,1)S(1)} collective-permute-done((bf16[136,512]{1,0:T(8,128)(2,1)S(1)}, bf16[136,512]{1,0:T(8,128)(2,1)S(1)}, u32[]{:S(2)}, u32[]{:S(2)}) %collective-permute-start.2) | collective-permute-done | bytes 139296 | tf_op jit(solution)/shard_map/ppermute | solution.py:439
  39.8 1.3 %collective-permute-start.34 = (bf16[128,512]{1,0:T(8,128)(2,1)S(1)}, bf16[128,512]{1,0:T(8,128)(2,1)}, u32[]{:S(2)}, u32[]{:S(2)}) collective-permute-start(bf16[128,512]{1,0:T(8,128)(2,1)S(1)} %collective-permute-done.30.refs_32_), channel_id=1, source_target_pairs={{0,4},{4,0},{8,12},{12,8},{16,20},{20,16},{24,28},{28,24},{1,5},{5... | collective-permute-start | bytes 393224 | tf_op jit(solution)/shard_map/ppermute | solution.py:439
  41.2 2.0 %collective-permute-start.32 = (bf16[128,512]{1,0:T(8,128)(2,1)S(1)}, bf16[128,512]{1,0:T(8,128)(2,1)}, u32[]{:S(2)}, u32[]{:S(2)}) collective-permute-start(bf16[128,512]{1,0:T(8,128)(2,1)S(1)} %collective-permute-done.30.refs_32_), channel_id=1, source_target_pairs={{0,2},{1,3},{2,0},{3,1},{4,6},{5,7},{6,4},{7,5},{8,10},{9,11},{10,... | collective-permute-start | bytes 393224 | tf_op jit(solution)/shard_map/ppermute | solution.py:439
  43.1 0.8 %collective-permute-start.6 = (bf16[136,512]{1,0:T(8,128)(2,1)S(1)}, bf16[136,512]{1,0:T(8,128)(2,1)S(1)}, u32[]{:S(2)}, u32[]{:S(2)}) collective-permute-start(bf16[136,512]{1,0:T(8,128)(2,1)S(1)} %collective-permute-done.5.refs_6_), channel_id=1, source_target_pairs={{0,4},{4,0},{8,12},{12,8},{16,20},{20,16},{24,28},{28,24},{1,5},{5... | collective-permute-start | bytes 417800 | tf_op jit(solution)/shard_map/ppermute | solution.py:439
  44.9 1.3 %collective-permute-done.32.refs_34_ = bf16[128,512]{1,0:T(8,128)(2,1)} collective-permute-done((bf16[128,512]{1,0:T(8,128)(2,1)S(1)}, bf16[128,512]{1,0:T(8,128)(2,1)}, u32[]{:S(2)}, u32[]{:S(2)}) %collective-permute-start.32) | collective-permute-done | bytes 131104 | tf_op jit(solution)/shard_map/ppermute | solution.py:439
  46.9 2.5 %collective-permute-start.36 = (bf16[128,512]{1,0:T(8,128)(2,1)}, bf16[128,512]{1,0:T(8,128)(2,1)}, u32[]{:S(2)}, u32[]{:S(2)}) collective-permute-start(bf16[128,512]{1,0:T(8,128)(2,1)} %collective-permute-done.34.refs_36_), channel_id=1, source_target_pairs={{0,2},{1,3},{2,0},{3,1},{4,6},{5,7},{6,4},{7,5},{8,10},{9,11},{10,... | collective-permute-start | bytes 393224 | tf_op jit(solution)/shard_map/ppermute | solution.py:439
  49.4 0.9 %collective-permute-done.28.refs_30_ = bf16[128,512]{1,0:T(8,128)(2,1)} collective-permute-done((bf16[128,512]{1,0:T(8,128)(2,1)S(1)}, bf16[128,512]{1,0:T(8,128)(2,1)}, u32[]{:S(2)}, u32[]{:S(2)}) %collective-permute-start.28) | collective-permute-done | bytes 131104 | tf_op jit(solution)/shard_map/ppermute | solution.py:439
  52.6 1.3 %collective-permute-done.36.refs_38_ = bf16[128,512]{1,0:T(8,128)(2,1)} collective-permute-done((bf16[128,512]{1,0:T(8,128)(2,1)}, bf16[128,512]{1,0:T(8,128)(2,1)}, u32[]{:S(2)}, u32[]{:S(2)}) %collective-permute-start.36) | collective-permute-done | bytes 131104 | tf_op jit(solution)/shard_map/ppermute | solution.py:439
  53.9 1.6 %collective-permute-done.37.refs_39_ = bf16[128,512]{1,0:T(8,128)(2,1)} collective-permute-done((bf16[128,512]{1,0:T(8,128)(2,1)}, bf16[128,512]{1,0:T(8,128)(2,1)}, u32[]{:S(2)}, u32[]{:S(2)}) %collective-permute-start.37) | collective-permute-done | bytes 131104 | tf_op jit(solution)/shard_map/ppermute | solution.py:439
  55.5 0.9 %copy-done.1 = bf16[128,512]{1,0:T(8,128)(2,1)S(1)} copy-done((bf16[128,512]{1,0:T(8,128)(2,1)S(1)}, bf16[128,512]{1,0:T(8,128)(2,1)}, u32[]{:S(2)}) %copy-start.1) | copy-done | bytes 131096
  56.4 0.9 %copy-done.3 = bf16[128,512]{1,0:T(8,128)(2,1)S(1)} copy-done((bf16[128,512]{1,0:T(8,128)(2,1)S(1)}, bf16[128,512]{1,0:T(8,128)(2,1)}, u32[]{:S(2)}) %copy-start.3) | copy-done | bytes 131096
  57.4 0.9 %copy-done.5 = bf16[128,512]{1,0:T(8,128)(2,1)S(1)} copy-done((bf16[128,512]{1,0:T(8,128)(2,1)S(1)}, bf16[128,512]{1,0:T(8,128)(2,1)}, u32[]{:S(2)}) %copy-start.5) | copy-done | bytes 131096
  58.3 0.9 %copy-done.7 = bf16[128,512]{1,0:T(8,128)(2,1)S(1)} copy-done((bf16[128,512]{1,0:T(8,128)(2,1)S(1)}, bf16[128,512]{1,0:T(8,128)(2,1)}, u32[]{:S(2)}) %copy-start.7) | copy-done | bytes 131096
  59.2 11.4 %main.1 = (bf16[256,128]{1,0:T(8,128)(2,1)}, bf16[256,128]{1,0:T(8,128)(2,1)}, f32[2,512,128]{2,1,0:T(8,128)}, bf16[256,2048]{1,0:T(8,128)(2,1)}) custom-call(s32[1]{0:T(128)} %bitcast.me_ref, s32[1]{0:T(128)} %bitcast.1.quarter_ref, bf16[136,512]{1,0:T(8,128)(2,1)S(1)} %pack.1.refs_0_, bf16[136,512]{1,0:T(8,128)(2,1)S(1)} %collective-permute-done.refs_1_, ...), custom_call_target="tpu_custom_call" | custom-call | flops 5000000000 | bytes 8000000 | tf_op jit(solution)/shard_map/main/pallas_call | solution.py:497
  (64 shorter events, 7.0 us)
Async XLA Ops:
  0.6 9.9 %collective-permute-start.14 = (bf16[128,512]{1,0:T(8,128)(2,1)}, bf16[128,512]{1,0:T(8,128)(2,1)S(1)}, u32[]{:S(2)}, u32[]{:S(2)}) collective-permute-start(bf16[128,512]{1,0:T(8,128)(2,1)} %refs_8_.1), channel_id=1, source_target_pairs={{0,8},{4,12},{8,0},{12,4},{16,24},{20,28},{24,16},{28,20},{1,9},{5... | collective-permute-start | bytes 393224 | tf_op jit(solution)/shard_map/ppermute | solution.py:439
  3.7 7.2 %collective-permute-start.10 = (bf16[128,512]{1,0:T(8,128)(2,1)}, bf16[128,512]{1,0:T(8,128)(2,1)S(1)}, u32[]{:S(2)}, u32[]{:S(2)}) collective-permute-start(bf16[128,512]{1,0:T(8,128)(2,1)} %refs_8_.1), channel_id=1, source_target_pairs={{0,4},{4,0},{8,12},{12,8},{16,20},{20,16},{24,28},{28,24},{1,5},{5... | collective-permute-start | bytes 393224 | tf_op jit(solution)/shard_map/ppermute | solution.py:439
  5.3 6.5 %collective-permute-start.8 = (bf16[128,512]{1,0:T(8,128)(2,1)}, bf16[128,512]{1,0:T(8,128)(2,1)S(1)}, u32[]{:S(2)}, u32[]{:S(2)}) collective-permute-start(bf16[128,512]{1,0:T(8,128)(2,1)} %refs_8_.1), channel_id=1, source_target_pairs={{0,2},{1,3},{2,0},{3,1},{4,6},{5,7},{6,4},{7,5},{8,10},{9,11},{10,... | collective-permute-start | bytes 393224 | tf_op jit(solution)/shard_map/ppermute | solution.py:439
  7.9 14.7 %collective-permute-start.3 = (bf16[136,512]{1,0:T(8,128)(2,1)S(1)}, bf16[136,512]{1,0:T(8,128)(2,1)S(1)}, u32[]{:S(2)}, u32[]{:S(2)}) collective-permute-start(bf16[136,512]{1,0:T(8,128)(2,1)S(1)} %pack.1.refs_0_), channel_id=1, source_target_pairs={{0,16},{4,20},{8,24},{12,28},{16,0},{20,4},{24,8},{28,12},{1,17},{... | collective-permute-start | bytes 417800 | tf_op jit(solution)/shard_map/ppermute | solution.py:439
  10.5 11.5 %collective-permute-start.22 = (bf16[128,512]{1,0:T(8,128)(2,1)S(1)}, bf16[128,512]{1,0:T(8,128)(2,1)S(1)}, u32[]{:S(2)}, u32[]{:S(2)}) collective-permute-start(bf16[128,512]{1,0:T(8,128)(2,1)S(1)} %copy-done.8), channel_id=1, source_target_pairs={{0,16},{4,20},{8,24},{12,28},{16,0},{20,4},{24,8},{28,12},{1,17},{... | collective-permute-start | bytes 393224 | tf_op jit(solution)/shard_map/ppermute | solution.py:439
  10.9 11.7 %collective-permute-start.1 = (bf16[136,512]{1,0:T(8,128)(2,1)S(1)}, bf16[136,512]{1,0:T(8,128)(2,1)S(1)}, u32[]{:S(2)}, u32[]{:S(2)}) collective-permute-start(bf16[136,512]{1,0:T(8,128)(2,1)S(1)} %pack.1.refs_0_), channel_id=1, source_target_pairs={{0,8},{4,12},{8,0},{12,4},{16,24},{20,28},{24,16},{28,20},{1,9},{5... | collective-permute-start | bytes 417800 | tf_op jit(solution)/shard_map/ppermute | solution.py:439
  11.8 12.3 %collective-permute-start = (bf16[136,512]{1,0:T(8,128)(2,1)S(1)}, bf16[136,512]{1,0:T(8,128)(2,1)S(1)}, u32[]{:S(2)}, u32[]{:S(2)}) collective-permute-start(bf16[136,512]{1,0:T(8,128)(2,1)S(1)} %pack.1.refs_0_), channel_id=1, source_target_pairs={{0,4},{4,0},{8,12},{12,8},{16,20},{20,16},{24,28},{28,24},{1,5},{5... | collective-permute-start | bytes 417800 | tf_op jit(solution)/shard_map/ppermute | solution.py:439
  13.3 10.9 %collective-permute-start.18 = (bf16[128,512]{1,0:T(8,128)(2,1)S(1)}, bf16[128,512]{1,0:T(8,128)(2,1)S(1)}, u32[]{:S(2)}, u32[]{:S(2)}) collective-permute-start(bf16[128,512]{1,0:T(8,128)(2,1)S(1)} %collective-permute-done.14.refs_16_), channel_id=1, source_target_pairs={{0,4},{4,0},{8,12},{12,8},{16,20},{20,16},{24,28},{28,24},{1,5},{5... | collective-permute-start | bytes 393224 | tf_op jit(solution)/shard_map/ppermute | solution.py:439
  22.0 6.2 %collective-permute-start.16 = (bf16[128,512]{1,0:T(8,128)(2,1)S(1)}, bf16[128,512]{1,0:T(8,128)(2,1)S(1)}, u32[]{:S(2)}, u32[]{:S(2)}) collective-permute-start(bf16[128,512]{1,0:T(8,128)(2,1)S(1)} %collective-permute-done.14.refs_16_), channel_id=1, source_target_pairs={{0,2},{1,3},{2,0},{3,1},{4,6},{5,7},{6,4},{7,5},{8,10},{9,11},{10,... | collective-permute-start | bytes 393224 | tf_op jit(solution)/shard_map/ppermute | solution.py:439
  22.6 5.7 %collective-permute-start.15 = (bf16[128,512]{1,0:T(8,128)(2,1)S(1)}, bf16[128,512]{1,0:T(8,128)(2,1)S(1)}, u32[]{:S(2)}, u32[]{:S(2)}) collective-permute-start(bf16[128,512]{1,0:T(8,128)(2,1)S(1)} %collective-permute-done.14.refs_16_), channel_id=1, source_target_pairs={{0,1},{1,0},{2,3},{3,2},{4,5},{5,4},{6,7},{7,6},{8,9},{9,8},{10,11... | collective-permute-start | bytes 393224 | tf_op jit(solution)/shard_map/ppermute | solution.py:439
  22.6 7.2 %collective-permute-start.12 = (bf16[128,512]{1,0:T(8,128)(2,1)S(1)}, bf16[128,512]{1,0:T(8,128)(2,1)S(1)}, u32[]{:S(2)}, u32[]{:S(2)}) collective-permute-start(bf16[128,512]{1,0:T(8,128)(2,1)S(1)} %collective-permute-done.10.refs_12_), channel_id=1, source_target_pairs={{0,2},{1,3},{2,0},{3,1},{4,6},{5,7},{6,4},{7,5},{8,10},{9,11},{10,... | collective-permute-start | bytes 393224 | tf_op jit(solution)/shard_map/ppermute | solution.py:439
  24.1 6.3 %collective-permute-start.11 = (bf16[128,512]{1,0:T(8,128)(2,1)S(1)}, bf16[128,512]{1,0:T(8,128)(2,1)S(1)}, u32[]{:S(2)}, u32[]{:S(2)}) collective-permute-start(bf16[128,512]{1,0:T(8,128)(2,1)S(1)} %collective-permute-done.10.refs_12_), channel_id=1, source_target_pairs={{0,1},{1,0},{2,3},{3,2},{4,5},{5,4},{6,7},{7,6},{8,9},{9,8},{10,11... | collective-permute-start | bytes 393224 | tf_op jit(solution)/shard_map/ppermute | solution.py:439
  24.3 6.2 %collective-permute-start.9 = (bf16[128,512]{1,0:T(8,128)(2,1)S(1)}, bf16[128,512]{1,0:T(8,128)(2,1)S(1)}, u32[]{:S(2)}, u32[]{:S(2)}) collective-permute-start(bf16[128,512]{1,0:T(8,128)(2,1)S(1)} %collective-permute-done.8.refs_10_), channel_id=1, source_target_pairs={{0,1},{1,0},{2,3},{3,2},{4,5},{5,4},{6,7},{7,6},{8,9},{9,8},{10,11... | collective-permute-start | bytes 393224 | tf_op jit(solution)/shard_map/ppermute | solution.py:439
  28.2 5.0 %collective-permute-start.30 = (bf16[128,512]{1,0:T(8,128)(2,1)S(1)}, bf16[128,512]{1,0:T(8,128)(2,1)S(1)}, u32[]{:S(2)}, u32[]{:S(2)}) collective-permute-start(bf16[128,512]{1,0:T(8,128)(2,1)S(1)} %collective-permute-done.22.refs_24_), channel_id=1, source_target_pairs={{0,8},{4,12},{8,0},{12,4},{16,24},{20,28},{24,16},{28,20},{1,9},{5... | collective-permute-start | bytes 393224 | tf_op jit(solution)/shard_map/ppermute | solution.py:439
  28.2 5.7 %collective-permute-start.26 = (bf16[128,512]{1,0:T(8,128)(2,1)S(1)}, bf16[128,512]{1,0:T(8,128)(2,1)S(1)}, u32[]{:S(2)}, u32[]{:S(2)}) collective-permute-start(bf16[128,512]{1,0:T(8,128)(2,1)S(1)} %collective-permute-done.22.refs_24_), channel_id=1, source_target_pairs={{0,4},{4,0},{8,12},{12,8},{16,20},{20,16},{24,28},{28,24},{1,5},{5... | collective-permute-start | bytes 393224 | tf_op jit(solution)/shard_map/ppermute | solution.py:439
  29.8 5.5 %collective-permute-start.24 = (bf16[128,512]{1,0:T(8,128)(2,1)S(1)}, bf16[128,512]{1,0:T(8,128)(2,1)S(1)}, u32[]{:S(2)}, u32[]{:S(2)}) collective-permute-start(bf16[128,512]{1,0:T(8,128)(2,1)S(1)} %collective-permute-done.22.refs_24_), channel_id=1, source_target_pairs={{0,2},{1,3},{2,0},{3,1},{4,6},{5,7},{6,4},{7,5},{8,10},{9,11},{10,... | collective-permute-start | bytes 393224 | tf_op jit(solution)/shard_map/ppermute | solution.py:439
  30.4 5.0 %collective-permute-start.23 = (bf16[128,512]{1,0:T(8,128)(2,1)S(1)}, bf16[128,512]{1,0:T(8,128)(2,1)S(1)}, u32[]{:S(2)}, u32[]{:S(2)}) collective-permute-start(bf16[128,512]{1,0:T(8,128)(2,1)S(1)} %collective-permute-done.22.refs_24_), channel_id=1, source_target_pairs={{0,1},{1,0},{2,3},{3,2},{4,5},{5,4},{6,7},{7,6},{8,9},{9,8},{10,11... | collective-permute-start | bytes 393224 | tf_op jit(solution)/shard_map/ppermute | solution.py:439
  30.4 6.1 %collective-permute-start.5 = (bf16[136,512]{1,0:T(8,128)(2,1)S(1)}, bf16[136,512]{1,0:T(8,128)(2,1)S(1)}, u32[]{:S(2)}, u32[]{:S(2)}) collective-permute-start(bf16[136,512]{1,0:T(8,128)(2,1)S(1)} %collective-permute-done.3.refs_4_), channel_id=1, source_target_pairs={{0,8},{4,12},{8,0},{12,4},{16,24},{20,28},{24,16},{28,20},{1,9},{5... | collective-permute-start | bytes 417800 | tf_op jit(solution)/shard_map/ppermute | solution.py:439
  33.2 5.1 %collective-permute-start.4 = (bf16[136,512]{1,0:T(8,128)(2,1)S(1)}, bf16[136,512]{1,0:T(8,128)(2,1)S(1)}, u32[]{:S(2)}, u32[]{:S(2)}) collective-permute-start(bf16[136,512]{1,0:T(8,128)(2,1)S(1)} %collective-permute-done.3.refs_4_), channel_id=1, source_target_pairs={{0,4},{4,0},{8,12},{12,8},{16,20},{20,16},{24,28},{28,24},{1,5},{5... | collective-permute-start | bytes 417800 | tf_op jit(solution)/shard_map/ppermute | solution.py:439
  33.9 5.9 %collective-permute-start.2 = (bf16[136,512]{1,0:T(8,128)(2,1)S(1)}, bf16[136,512]{1,0:T(8,128)(2,1)S(1)}, u32[]{:S(2)}, u32[]{:S(2)}) collective-permute-start(bf16[136,512]{1,0:T(8,128)(2,1)S(1)} %collective-permute-done.1.refs_2_), channel_id=1, source_target_pairs={{0,4},{4,0},{8,12},{12,8},{16,20},{20,16},{24,28},{28,24},{1,5},{5... | collective-permute-start | bytes 417800 | tf_op jit(solution)/shard_map/ppermute | solution.py:439
  35.2 5.9 %collective-permute-start.20 = (bf16[128,512]{1,0:T(8,128)(2,1)S(1)}, bf16[128,512]{1,0:T(8,128)(2,1)S(1)}, u32[]{:S(2)}, u32[]{:S(2)}) collective-permute-start(bf16[128,512]{1,0:T(8,128)(2,1)S(1)} %collective-permute-done.18.refs_20_), channel_id=1, source_target_pairs={{0,2},{1,3},{2,0},{3,1},{4,6},{5,7},{6,4},{7,5},{8,10},{9,11},{10,... | collective-permute-start | bytes 393224 | tf_op jit(solution)/shard_map/ppermute | solution.py:439
  35.5 7.7 %collective-permute-start.19 = (bf16[128,512]{1,0:T(8,128)(2,1)S(1)}, bf16[128,512]{1,0:T(8,128)(2,1)S(1)}, u32[]{:S(2)}, u32[]{:S(2)}) collective-permute-start(bf16[128,512]{1,0:T(8,128)(2,1)S(1)} %collective-permute-done.18.refs_20_), channel_id=1, source_target_pairs={{0,1},{1,0},{2,3},{3,2},{4,5},{5,4},{6,7},{7,6},{8,9},{9,8},{10,11... | collective-permute-start | bytes 393224 | tf_op jit(solution)/shard_map/ppermute | solution.py:439
  36.5 6.6 %collective-permute-start.17 = (bf16[128,512]{1,0:T(8,128)(2,1)S(1)}, bf16[128,512]{1,0:T(8,128)(2,1)S(1)}, u32[]{:S(2)}, u32[]{:S(2)}) collective-permute-start(bf16[128,512]{1,0:T(8,128)(2,1)S(1)} %collective-permute-done.16.refs_18_), channel_id=1, source_target_pairs={{0,1},{1,0},{2,3},{3,2},{4,5},{5,4},{6,7},{7,6},{8,9},{9,8},{10,11... | collective-permute-start | bytes 393224 | tf_op jit(solution)/shard_map/ppermute | solution.py:439
  38.3 5.6 %collective-permute-start.13 = (bf16[128,512]{1,0:T(8,128)(2,1)S(1)}, bf16[128,512]{1,0:T(8,128)(2,1)S(1)}, u32[]{:S(2)}, u32[]{:S(2)}) collective-permute-start(bf16[128,512]{1,0:T(8,128)(2,1)S(1)} %collective-permute-done.12.refs_14_), channel_id=1, source_target_pairs={{0,1},{1,0},{2,3},{3,2},{4,5},{5,4},{6,7},{7,6},{8,9},{9,8},{10,11... | collective-permute-start | bytes 393224 | tf_op jit(solution)/shard_map/ppermute | solution.py:439
  39.8 5.1 %collective-permute-start.34 = (bf16[128,512]{1,0:T(8,128)(2,1)S(1)}, bf16[128,512]{1,0:T(8,128)(2,1)}, u32[]{:S(2)}, u32[]{:S(2)}) collective-permute-start(bf16[128,512]{1,0:T(8,128)(2,1)S(1)} %collective-permute-done.30.refs_32_), channel_id=1, source_target_pairs={{0,4},{4,0},{8,12},{12,8},{16,20},{20,16},{24,28},{28,24},{1,5},{5... | collective-permute-start | bytes 393224 | tf_op jit(solution)/shard_map/ppermute | solution.py:439
  41.2 5.1 %collective-permute-start.32 = (bf16[128,512]{1,0:T(8,128)(2,1)S(1)}, bf16[128,512]{1,0:T(8,128)(2,1)}, u32[]{:S(2)}, u32[]{:S(2)}) collective-permute-start(bf16[128,512]{1,0:T(8,128)(2,1)S(1)} %collective-permute-done.30.refs_32_), channel_id=1, source_target_pairs={{0,2},{1,3},{2,0},{3,1},{4,6},{5,7},{6,4},{7,5},{8,10},{9,11},{10,... | collective-permute-start | bytes 393224 | tf_op jit(solution)/shard_map/ppermute | solution.py:439
  43.1 8.9 %collective-permute-start.6 = (bf16[136,512]{1,0:T(8,128)(2,1)S(1)}, bf16[136,512]{1,0:T(8,128)(2,1)S(1)}, u32[]{:S(2)}, u32[]{:S(2)}) collective-permute-start(bf16[136,512]{1,0:T(8,128)(2,1)S(1)} %collective-permute-done.5.refs_6_), channel_id=1, source_target_pairs={{0,4},{4,0},{8,12},{12,8},{16,20},{20,16},{24,28},{28,24},{1,5},{5... | collective-permute-start | bytes 417800 | tf_op jit(solution)/shard_map/ppermute | solution.py:439
  44.6 5.7 %collective-permute-start.28 = (bf16[128,512]{1,0:T(8,128)(2,1)S(1)}, bf16[128,512]{1,0:T(8,128)(2,1)}, u32[]{:S(2)}, u32[]{:S(2)}) collective-permute-start(bf16[128,512]{1,0:T(8,128)(2,1)S(1)} %collective-permute-done.26.refs_28_), channel_id=1, source_target_pairs={{0,2},{1,3},{2,0},{3,1},{4,6},{5,7},{6,4},{7,5},{8,10},{9,11},{10,... | collective-permute-start | bytes 393224 | tf_op jit(solution)/shard_map/ppermute | solution.py:439
  44.9 5.3 %collective-permute-start.27 = (bf16[128,512]{1,0:T(8,128)(2,1)S(1)}, bf16[128,512]{1,0:T(8,128)(2,1)S(1)}, u32[]{:S(2)}, u32[]{:S(2)}) collective-permute-start(bf16[128,512]{1,0:T(8,128)(2,1)S(1)} %collective-permute-done.26.refs_28_), channel_id=1, source_target_pairs={{0,1},{1,0},{2,3},{3,2},{4,5},{5,4},{6,7},{7,6},{8,9},{9,8},{10,11... | collective-permute-start | bytes 393224 | tf_op jit(solution)/shard_map/ppermute | solution.py:439
  46.2 5.1 %collective-permute-start.25 = (bf16[128,512]{1,0:T(8,128)(2,1)S(1)}, bf16[128,512]{1,0:T(8,128)(2,1)S(1)}, u32[]{:S(2)}, u32[]{:S(2)}) collective-permute-start(bf16[128,512]{1,0:T(8,128)(2,1)S(1)} %collective-permute-done.24.refs_26_), channel_id=1, source_target_pairs={{0,1},{1,0},{2,3},{3,2},{4,5},{5,4},{6,7},{7,6},{8,9},{9,8},{10,11... | collective-permute-start | bytes 393224 | tf_op jit(solution)/shard_map/ppermute | solution.py:439
  46.9 6.9 %collective-permute-start.36 = (bf16[128,512]{1,0:T(8,128)(2,1)}, bf16[128,512]{1,0:T(8,128)(2,1)}, u32[]{:S(2)}, u32[]{:S(2)}) collective-permute-start(bf16[128,512]{1,0:T(8,128)(2,1)} %collective-permute-done.34.refs_36_), channel_id=1, source_target_pairs={{0,2},{1,3},{2,0},{3,1},{4,6},{5,7},{6,4},{7,5},{8,10},{9,11},{10,... | collective-permute-start | bytes 393224 | tf_op jit(solution)/shard_map/ppermute | solution.py:439
  50.2 3.6 %collective-permute-start.35 = (bf16[128,512]{1,0:T(8,128)(2,1)}, bf16[128,512]{1,0:T(8,128)(2,1)}, u32[]{:S(2)}, u32[]{:S(2)}) collective-permute-start(bf16[128,512]{1,0:T(8,128)(2,1)} %collective-permute-done.34.refs_36_), channel_id=1, source_target_pairs={{0,1},{1,0},{2,3},{3,2},{4,5},{5,4},{6,7},{7,6},{8,9},{9,8},{10,11... | collective-permute-start | bytes 393224 | tf_op jit(solution)/shard_map/ppermute | solution.py:439
  (15 other events, 24.3 us)

commit v5 on v4

--- a/solution.py
+++ b/solution.py
@@ -247,7 +247,7 @@
     book_any, weight_any = refs[5 * blocks : 5 * blocks + 2]
     dq_ref, dv_ref, dbook_any, dweight_any = refs[5 * blocks + 2 : 5 * blocks + 6]
     (q_ref, k_ref, v_ref, k_t_ref, v_t_ref, hot_ref, codes_ref, att_t_ref, lse_ref, weight_ref, go_ref,
-     do_t_ref, dk_ref, delta_ref, rows_ref, own_ref, dbook_ref, dweight_ref, book_ref, sems, go_sems, out_sems,
+     do_t_ref, dk_ref, delta_ref, rows_ref, own_ref, dbook_ref, dweight_ref, book_ref, kept_ref, sems, go_sems, out_sems,
      ) = refs[5 * blocks + 6 :]
     tokens = blocks * BLOCK
     wide = heads * width
@@ -328,8 +328,12 @@
         top = jnp.max(scores, axis=0, keepdims=True)
         weights = jnp.exp(scores - top)
         total = jnp.sum(weights, axis=0, keepdims=True)
-        mixed = dot_nn(v_t_ref[columns, :seen], weights.astype(BF16))
-        att_t_ref[columns, here] = (mixed / total).astype(BF16)
+        weights = weights.astype(BF16)
+        kept_ref[head, :seen, here] = weights
+        mixed = dot_nn(v_t_ref[columns, :seen], weights)
+        share = 1.0 / total
+        att_t_ref[columns, here] = (mixed * share).astype(BF16)
+        lse_ref[heads + head : heads + head + 1, here] = share
         lse_ref[head : head + 1, here] = top + jnp.log(total)
 
     mine = pl.ds(pl.multiple_of(me * BLOCK, BLOCK), BLOCK)
@@ -343,22 +347,20 @@
         columns = slice(head * width, (head + 1) * width)
         seen = (tile + 1) * TILE
         grad = dot_nn(v_ref[:seen, columns], do_t_ref[columns, tile * TILE : seen])
-        return scored(head, tile), grad
+        return grad
 
     ahead = products(*steps[0])
     for at, (head, tile) in enumerate(steps):
         columns = slice(head * width, (head + 1) * width)
         here = slice(tile * TILE, (tile + 1) * TILE)
         seen = (tile + 1) * TILE
-        scores, grad = ahead
+        grad = ahead
         if at + 1 < len(steps):
             ahead = products(*steps[at + 1])
         span = slice(at * TILE, (at + 1) * TILE)
         dweight_ref[:, span] = dot_nn(att_t_ref[...], go_ref[:, span]).astype(BF16)
-        weights = jnp.exp(scores - lse_ref[head : head + 1, here])
-        last = jnp.where(causal_tile(), weights[seen - TILE :], 0.0)
-        weights = last if tile == 0 else jnp.concatenate([weights[: seen - TILE], last], axis=0)
-        grad = (weights * (grad - delta_ref[head : head + 1, here])).astype(BF16)
+        grad = (grad - delta_ref[head : head + 1, here]) * lse_ref[heads + head : heads + head + 1, here]
+        grad = (kept_ref[head, :seen, here].astype(F32) * grad).astype(BF16)
         term = dot_nn(grad, q_ref[here, columns])
         if tile == 0:
             dk_ref[head, :seen, :] = term
@@ -482,11 +484,12 @@
             pltpu.VMEM((heads, code_total, width), F32),
             pltpu.VMEM((wide, 4 * part), BF16),
             pltpu.VMEM((heads, code_total, width), BF16),
+            pltpu.VMEM((heads, tokens, tokens), BF16),
             pltpu.SemaphoreType.DMA((3, blocks)),
             pltpu.SemaphoreType.DMA((blocks, 4)),
             pltpu.SemaphoreType.DMA((3 + heads,)),
         ],
-        compiler_params=pltpu.CompilerParams(vmem_limit_bytes=28 * 2**20),
+        compiler_params=pltpu.CompilerParams(vmem_limit_bytes=32 * 2**20),
         cost_estimate=pl.CostEstimate(flops=5 * 10**9, bytes_accessed=8 * 10**6, transcendentals=10**6),
         name="main",
     )

time: 70.9 us -> 70.3 us (level)
  no operation moved by 1% of the time
where the time goes in v5:
time: 70.3 us; the launch traced here: 70.1 us
  starting transfers between devices  26.6 us (38%)
  waiting for transfers between devices  24.5 us (35%)
  Pallas kernels  11.9 us (17%)
  local copies, waits for them, and re-layouts  6.24 us (9%)
  between operations  0.88 us (1%)
    ppermute x38, starting transfers between devices, exchange(): return lax.ppermute(array, axis, pairs)  26.6 us
    ppermute x38, waiting for transfers between devices, exchange(): return lax.ppermute(array, axis, pairs)  24.5 us
    pallas_call x1, Pallas kernels, gathered_body(): main(me, quarter, *slots, *grads, codebook, out_weight)  10.8 us
    unnamed x18, local copies, waits for them, and re-layouts  6.24 us
  transfers between devices with their start and end apart: 38, of which 13 were waited for; matrix products, arithmetic and copies ran while one was open for 0% of the time, Pallas kernels for 2%

profile of v5, /device:TPU:0, one launch (start us, length us, event | category | flops | bytes accessed | tf_op | source)
XLA Modules:
  0.0 70.1 jit_solution(6923928147773227803)
XLA Ops:
  0.6 3.1 %collective-permute-start.14 = (bf16[128,512]{1,0:T(8,128)(2,1)}, bf16[128,512]{1,0:T(8,128)(2,1)S(1)}, u32[]{:S(2)}, u32[]{:S(2)}) collective-permute-start(bf16[128,512]{1,0:T(8,128)(2,1)} %refs_8_.1), channel_id=1, source_target_pairs={{0,8},{4,12},{8,0},{12,4},{16,24},{20,28},{24,16},{28,20},{1,9},{5... | collective-permute-start | bytes 393224 | tf_op jit(solution)/shard_map/ppermute | solution.py:441
  3.7 1.5 %collective-permute-start.10 = (bf16[128,512]{1,0:T(8,128)(2,1)}, bf16[128,512]{1,0:T(8,128)(2,1)S(1)}, u32[]{:S(2)}, u32[]{:S(2)}) collective-permute-start(bf16[128,512]{1,0:T(8,128)(2,1)} %refs_8_.1), channel_id=1, source_target_pairs={{0,4},{4,0},{8,12},{12,8},{16,20},{20,16},{24,28},{28,24},{1,5},{5... | collective-permute-start | bytes 393224 | tf_op jit(solution)/shard_map/ppermute | solution.py:441
  5.3 1.5 %collective-permute-start.8 = (bf16[128,512]{1,0:T(8,128)(2,1)}, bf16[128,512]{1,0:T(8,128)(2,1)S(1)}, u32[]{:S(2)}, u32[]{:S(2)}) collective-permute-start(bf16[128,512]{1,0:T(8,128)(2,1)} %refs_8_.1), channel_id=1, source_target_pairs={{0,2},{1,3},{2,0},{3,1},{4,6},{5,7},{6,4},{7,5},{8,10},{9,11},{10,... | collective-permute-start | bytes 393224 | tf_op jit(solution)/shard_map/ppermute | solution.py:441
  6.8 1.1 %pack.1.refs_0_ = bf16[136,512]{1,0:T(8,128)(2,1)S(1)} custom-call(bf16[256,128]{1,0:T(8,128)(2,1)} %bitcast.6, bf16[256,128]{1,0:T(8,128)(2,1)} %bitcast.7, s32[2,128]{1,0:T(2,128)} %code_ref.1), custom_call_target="tpu_custom_call" | custom-call | tf_op jit(solution)/shard_map/pack/pallas_call | solution.py:427
  7.9 2.7 %collective-permute-start.3 = (bf16[136,512]{1,0:T(8,128)(2,1)S(1)}, bf16[136,512]{1,0:T(8,128)(2,1)S(1)}, u32[]{:S(2)}, u32[]{:S(2)}) collective-permute-start(bf16[136,512]{1,0:T(8,128)(2,1)S(1)} %pack.1.refs_0_), channel_id=1, source_target_pairs={{0,16},{4,20},{8,24},{12,28},{16,0},{20,4},{24,8},{28,12},{1,17},{... | collective-permute-start | bytes 417800 | tf_op jit(solution)/shard_map/ppermute | solution.py:441
  10.9 0.9 %collective-permute-start.1 = (bf16[136,512]{1,0:T(8,128)(2,1)S(1)}, bf16[136,512]{1,0:T(8,128)(2,1)S(1)}, u32[]{:S(2)}, u32[]{:S(2)}) collective-permute-start(bf16[136,512]{1,0:T(8,128)(2,1)S(1)} %pack.1.refs_0_), channel_id=1, source_target_pairs={{0,8},{4,12},{8,0},{12,4},{16,24},{20,28},{24,16},{28,20},{1,9},{5... | collective-permute-start | bytes 417800 | tf_op jit(solution)/shard_map/ppermute | solution.py:441
  11.8 1.5 %collective-permute-start = (bf16[136,512]{1,0:T(8,128)(2,1)S(1)}, bf16[136,512]{1,0:T(8,128)(2,1)S(1)}, u32[]{:S(2)}, u32[]{:S(2)}) collective-permute-start(bf16[136,512]{1,0:T(8,128)(2,1)S(1)} %pack.1.refs_0_), channel_id=1, source_target_pairs={{0,4},{4,0},{8,12},{12,8},{16,20},{20,16},{24,28},{28,24},{1,5},{5... | collective-permute-start | bytes 417800 | tf_op jit(solution)/shard_map/ppermute | solution.py:441
  13.8 8.2 %collective-permute-done.22.refs_24_ = bf16[128,512]{1,0:T(8,128)(2,1)S(1)} collective-permute-done((bf16[128,512]{1,0:T(8,128)(2,1)S(1)}, bf16[128,512]{1,0:T(8,128)(2,1)S(1)}, u32[]{:S(2)}, u32[]{:S(2)}) %collective-permute-start.22) | collective-permute-done | bytes 131104 | tf_op jit(solution)/shard_map/ppermute | solution.py:441
  22.6 1.5 %collective-permute-start.12 = (bf16[128,512]{1,0:T(8,128)(2,1)S(1)}, bf16[128,512]{1,0:T(8,128)(2,1)S(1)}, u32[]{:S(2)}, u32[]{:S(2)}) collective-permute-start(bf16[128,512]{1,0:T(8,128)(2,1)S(1)} %collective-permute-done.10.refs_12_), channel_id=1, source_target_pairs={{0,2},{1,3},{2,0},{3,1},{4,6},{5,7},{6,4},{7,5},{8,10},{9,11},{10,... | collective-permute-start | bytes 393224 | tf_op jit(solution)/shard_map/ppermute | solution.py:441
  24.6 3.6 %collective-permute-done.16.refs_18_ = bf16[128,512]{1,0:T(8,128)(2,1)S(1)} collective-permute-done((bf16[128,512]{1,0:T(8,128)(2,1)S(1)}, bf16[128,512]{1,0:T(8,128)(2,1)S(1)}, u32[]{:S(2)}, u32[]{:S(2)}) %collective-permute-start.16) | collective-permute-done | bytes 131104 | tf_op jit(solution)/shard_map/ppermute | solution.py:441
  28.2 0.7 collective-permute-start.26
  28.9 0.8 %collective-permute-done.12.refs_14_ = bf16[128,512]{1,0:T(8,128)(2,1)S(1)} collective-permute-done((bf16[128,512]{1,0:T(8,128)(2,1)S(1)}, bf16[128,512]{1,0:T(8,128)(2,1)S(1)}, u32[]{:S(2)}, u32[]{:S(2)}) %collective-permute-start.12) | collective-permute-done | bytes 131104 | tf_op jit(solution)/shard_map/ppermute | solution.py:441
  30.4 0.7 collective-permute-start.5
  31.1 2.1 %collective-permute-done.30.refs_32_ = bf16[128,512]{1,0:T(8,128)(2,1)S(1)} collective-permute-done((bf16[128,512]{1,0:T(8,128)(2,1)S(1)}, bf16[128,512]{1,0:T(8,128)(2,1)S(1)}, u32[]{:S(2)}, u32[]{:S(2)}) %collective-permute-start.30) | collective-permute-done | bytes 131104 | tf_op jit(solution)/shard_map/ppermute | solution.py:441
  33.2 0.7 collective-permute-start.4
  33.9 1.3 %collective-permute-start.2 = (bf16[136,512]{1,0:T(8,128)(2,1)S(1)}, bf16[136,512]{1,0:T(8,128)(2,1)S(1)}, u32[]{:S(2)}, u32[]{:S(2)}) collective-permute-start(bf16[136,512]{1,0:T(8,128)(2,1)S(1)} %collective-permute-done.1.refs_2_), channel_id=1, source_target_pairs={{0,4},{4,0},{8,12},{12,8},{16,20},{20,16},{24,28},{28,24},{1,5},{5... | collective-permute-start | bytes 417800 | tf_op jit(solution)/shard_map/ppermute | solution.py:441
  35.5 1.1 %collective-permute-done.5.refs_6_ = bf16[136,512]{1,0:T(8,128)(2,1)S(1)} collective-permute-done((bf16[136,512]{1,0:T(8,128)(2,1)S(1)}, bf16[136,512]{1,0:T(8,128)(2,1)S(1)}, u32[]{:S(2)}, u32[]{:S(2)}) %collective-permute-start.5) | collective-permute-done | bytes 139296 | tf_op jit(solution)/shard_map/ppermute | solution.py:441
  36.5 1.8 %collective-permute-done.4.refs_5_ = bf16[136,512]{1,0:T(8,128)(2,1)S(1)} collective-permute-done((bf16[136,512]{1,0:T(8,128)(2,1)S(1)}, bf16[136,512]{1,0:T(8,128)(2,1)S(1)}, u32[]{:S(2)}, u32[]{:S(2)}) %collective-permute-start.4) | collective-permute-done | bytes 139296 | tf_op jit(solution)/shard_map/ppermute | solution.py:441
  38.3 1.5 %collective-permute-done.2.refs_3_ = bf16[136,512]{1,0:T(8,128)(2,1)S(1)} collective-permute-done((bf16[136,512]{1,0:T(8,128)(2,1)S(1)}, bf16[136,512]{1,0:T(8,128)(2,1)S(1)}, u32[]{:S(2)}, u32[]{:S(2)}) %collective-permute-start.2) | collective-permute-done | bytes 139296 | tf_op jit(solution)/shard_map/ppermute | solution.py:441
  39.8 1.3 %collective-permute-start.34 = (bf16[128,512]{1,0:T(8,128)(2,1)S(1)}, bf16[128,512]{1,0:T(8,128)(2,1)}, u32[]{:S(2)}, u32[]{:S(2)}) collective-permute-start(bf16[128,512]{1,0:T(8,128)(2,1)S(1)} %collective-permute-done.30.refs_32_), channel_id=1, source_target_pairs={{0,4},{4,0},{8,12},{12,8},{16,20},{20,16},{24,28},{28,24},{1,5},{5... | collective-permute-start | bytes 393224 | tf_op jit(solution)/shard_map/ppermute | solution.py:441
  41.2 2.0 %collective-permute-start.32 = (bf16[128,512]{1,0:T(8,128)(2,1)S(1)}, bf16[128,512]{1,0:T(8,128)(2,1)}, u32[]{:S(2)}, u32[]{:S(2)}) collective-permute-start(bf16[128,512]{1,0:T(8,128)(2,1)S(1)} %collective-permute-done.30.refs_32_), channel_id=1, source_target_pairs={{0,2},{1,3},{2,0},{3,1},{4,6},{5,7},{6,4},{7,5},{8,10},{9,11},{10,... | collective-permute-start | bytes 393224 | tf_op jit(solution)/shard_map/ppermute | solution.py:441
  43.1 0.8 %collective-permute-start.6 = (bf16[136,512]{1,0:T(8,128)(2,1)S(1)}, bf16[136,512]{1,0:T(8,128)(2,1)S(1)}, u32[]{:S(2)}, u32[]{:S(2)}) collective-permute-start(bf16[136,512]{1,0:T(8,128)(2,1)S(1)} %collective-permute-done.5.refs_6_), channel_id=1, source_target_pairs={{0,4},{4,0},{8,12},{12,8},{16,20},{20,16},{24,28},{28,24},{1,5},{5... | collective-permute-start | bytes 417800 | tf_op jit(solution)/shard_map/ppermute | solution.py:441
  44.9 1.3 %collective-permute-done.32.refs_34_ = bf16[128,512]{1,0:T(8,128)(2,1)} collective-permute-done((bf16[128,512]{1,0:T(8,128)(2,1)S(1)}, bf16[128,512]{1,0:T(8,128)(2,1)}, u32[]{:S(2)}, u32[]{:S(2)}) %collective-permute-start.32) | collective-permute-done | bytes 131104 | tf_op jit(solution)/shard_map/ppermute | solution.py:441
  46.9 2.5 %collective-permute-start.36 = (bf16[128,512]{1,0:T(8,128)(2,1)}, bf16[128,512]{1,0:T(8,128)(2,1)}, u32[]{:S(2)}, u32[]{:S(2)}) collective-permute-start(bf16[128,512]{1,0:T(8,128)(2,1)} %collective-permute-done.34.refs_36_), channel_id=1, source_target_pairs={{0,2},{1,3},{2,0},{3,1},{4,6},{5,7},{6,4},{7,5},{8,10},{9,11},{10,... | collective-permute-start | bytes 393224 | tf_op jit(solution)/shard_map/ppermute | solution.py:441
  49.4 0.9 %collective-permute-done.28.refs_30_ = bf16[128,512]{1,0:T(8,128)(2,1)} collective-permute-done((bf16[128,512]{1,0:T(8,128)(2,1)S(1)}, bf16[128,512]{1,0:T(8,128)(2,1)}, u32[]{:S(2)}, u32[]{:S(2)}) %collective-permute-start.28) | collective-permute-done | bytes 131104 | tf_op jit(solution)/shard_map/ppermute | solution.py:441
  52.6 1.3 %collective-permute-done.36.refs_38_ = bf16[128,512]{1,0:T(8,128)(2,1)} collective-permute-done((bf16[128,512]{1,0:T(8,128)(2,1)}, bf16[128,512]{1,0:T(8,128)(2,1)}, u32[]{:S(2)}, u32[]{:S(2)}) %collective-permute-start.36) | collective-permute-done | bytes 131104 | tf_op jit(solution)/shard_map/ppermute | solution.py:441
  53.9 1.6 %collective-permute-done.37.refs_39_ = bf16[128,512]{1,0:T(8,128)(2,1)} collective-permute-done((bf16[128,512]{1,0:T(8,128)(2,1)}, bf16[128,512]{1,0:T(8,128)(2,1)}, u32[]{:S(2)}, u32[]{:S(2)}) %collective-permute-start.37) | collective-permute-done | bytes 131104 | tf_op jit(solution)/shard_map/ppermute | solution.py:441
  55.5 0.9 %copy-done.1 = bf16[128,512]{1,0:T(8,128)(2,1)S(1)} copy-done((bf16[128,512]{1,0:T(8,128)(2,1)S(1)}, bf16[128,512]{1,0:T(8,128)(2,1)}, u32[]{:S(2)}) %copy-start.1) | copy-done | bytes 131096
  56.4 0.9 %copy-done.3 = bf16[128,512]{1,0:T(8,128)(2,1)S(1)} copy-done((bf16[128,512]{1,0:T(8,128)(2,1)S(1)}, bf16[128,512]{1,0:T(8,128)(2,1)}, u32[]{:S(2)}) %copy-start.3) | copy-done | bytes 131096
  57.4 0.9 %copy-done.5 = bf16[128,512]{1,0:T(8,128)(2,1)S(1)} copy-done((bf16[128,512]{1,0:T(8,128)(2,1)S(1)}, bf16[128,512]{1,0:T(8,128)(2,1)}, u32[]{:S(2)}) %copy-start.5) | copy-done | bytes 131096
  58.3 0.9 %copy-done.7 = bf16[128,512]{1,0:T(8,128)(2,1)S(1)} copy-done((bf16[128,512]{1,0:T(8,128)(2,1)S(1)}, bf16[128,512]{1,0:T(8,128)(2,1)}, u32[]{:S(2)}) %copy-start.7) | copy-done | bytes 131096
  59.2 10.8 %main.1 = (bf16[256,128]{1,0:T(8,128)(2,1)}, bf16[256,128]{1,0:T(8,128)(2,1)}, f32[2,512,128]{2,1,0:T(8,128)}, bf16[256,2048]{1,0:T(8,128)(2,1)}) custom-call(s32[1]{0:T(128)} %bitcast.me_ref, s32[1]{0:T(128)} %bitcast.1.quarter_ref, bf16[136,512]{1,0:T(8,128)(2,1)S(1)} %pack.1.refs_0_, bf16[136,512]{1,0:T(8,128)(2,1)S(1)} %collective-permute-done.refs_1_, ...), custom_call_target="tpu_custom_call" | custom-call | flops 5000000000 | bytes 8000000 | tf_op jit(solution)/shard_map/main/pallas_call | solution.py:500
  (64 shorter events, 7.0 us)
Async XLA Ops:
  0.6 9.9 %collective-permute-start.14 = (bf16[128,512]{1,0:T(8,128)(2,1)}, bf16[128,512]{1,0:T(8,128)(2,1)S(1)}, u32[]{:S(2)}, u32[]{:S(2)}) collective-permute-start(bf16[128,512]{1,0:T(8,128)(2,1)} %refs_8_.1), channel_id=1, source_target_pairs={{0,8},{4,12},{8,0},{12,4},{16,24},{20,28},{24,16},{28,20},{1,9},{5... | collective-permute-start | bytes 393224 | tf_op jit(solution)/shard_map/ppermute | solution.py:441
  3.7 7.2 %collective-permute-start.10 = (bf16[128,512]{1,0:T(8,128)(2,1)}, bf16[128,512]{1,0:T(8,128)(2,1)S(1)}, u32[]{:S(2)}, u32[]{:S(2)}) collective-permute-start(bf16[128,512]{1,0:T(8,128)(2,1)} %refs_8_.1), channel_id=1, source_target_pairs={{0,4},{4,0},{8,12},{12,8},{16,20},{20,16},{24,28},{28,24},{1,5},{5... | collective-permute-start | bytes 393224 | tf_op jit(solution)/shard_map/ppermute | solution.py:441
  5.3 6.5 %collective-permute-start.8 = (bf16[128,512]{1,0:T(8,128)(2,1)}, bf16[128,512]{1,0:T(8,128)(2,1)S(1)}, u32[]{:S(2)}, u32[]{:S(2)}) collective-permute-start(bf16[128,512]{1,0:T(8,128)(2,1)} %refs_8_.1), channel_id=1, source_target_pairs={{0,2},{1,3},{2,0},{3,1},{4,6},{5,7},{6,4},{7,5},{8,10},{9,11},{10,... | collective-permute-start | bytes 393224 | tf_op jit(solution)/shard_map/ppermute | solution.py:441
  7.9 14.7 %collective-permute-start.3 = (bf16[136,512]{1,0:T(8,128)(2,1)S(1)}, bf16[136,512]{1,0:T(8,128)(2,1)S(1)}, u32[]{:S(2)}, u32[]{:S(2)}) collective-permute-start(bf16[136,512]{1,0:T(8,128)(2,1)S(1)} %pack.1.refs_0_), channel_id=1, source_target_pairs={{0,16},{4,20},{8,24},{12,28},{16,0},{20,4},{24,8},{28,12},{1,17},{... | collective-permute-start | bytes 417800 | tf_op jit(solution)/shard_map/ppermute | solution.py:441
  10.5 11.5 %collective-permute-start.22 = (bf16[128,512]{1,0:T(8,128)(2,1)S(1)}, bf16[128,512]{1,0:T(8,128)(2,1)S(1)}, u32[]{:S(2)}, u32[]{:S(2)}) collective-permute-start(bf16[128,512]{1,0:T(8,128)(2,1)S(1)} %copy-done.8), channel_id=1, source_target_pairs={{0,16},{4,20},{8,24},{12,28},{16,0},{20,4},{24,8},{28,12},{1,17},{... | collective-permute-start | bytes 393224 | tf_op jit(solution)/shard_map/ppermute | solution.py:441
  10.9 11.7 %collective-permute-start.1 = (bf16[136,512]{1,0:T(8,128)(2,1)S(1)}, bf16[136,512]{1,0:T(8,128)(2,1)S(1)}, u32[]{:S(2)}, u32[]{:S(2)}) collective-permute-start(bf16[136,512]{1,0:T(8,128)(2,1)S(1)} %pack.1.refs_0_), channel_id=1, source_target_pairs={{0,8},{4,12},{8,0},{12,4},{16,24},{20,28},{24,16},{28,20},{1,9},{5... | collective-permute-start | bytes 417800 | tf_op jit(solution)/shard_map/ppermute | solution.py:441
  11.8 12.3 %collective-permute-start = (bf16[136,512]{1,0:T(8,128)(2,1)S(1)}, bf16[136,512]{1,0:T(8,128)(2,1)S(1)}, u32[]{:S(2)}, u32[]{:S(2)}) collective-permute-start(bf16[136,512]{1,0:T(8,128)(2,1)S(1)} %pack.1.refs_0_), channel_id=1, source_target_pairs={{0,4},{4,0},{8,12},{12,8},{16,20},{20,16},{24,28},{28,24},{1,5},{5... | collective-permute-start | bytes 417800 | tf_op jit(solution)/shard_map/ppermute | solution.py:441
  13.3 10.9 %collective-permute-start.18 = (bf16[128,512]{1,0:T(8,128)(2,1)S(1)}, bf16[128,512]{1,0:T(8,128)(2,1)S(1)}, u32[]{:S(2)}, u32[]{:S(2)}) collective-permute-start(bf16[128,512]{1,0:T(8,128)(2,1)S(1)} %collective-permute-done.14.refs_16_), channel_id=1, source_target_pairs={{0,4},{4,0},{8,12},{12,8},{16,20},{20,16},{24,28},{28,24},{1,5},{5... | collective-permute-start | bytes 393224 | tf_op jit(solution)/shard_map/ppermute | solution.py:441
  22.0 6.2 %collective-permute-start.16 = (bf16[128,512]{1,0:T(8,128)(2,1)S(1)}, bf16[128,512]{1,0:T(8,128)(2,1)S(1)}, u32[]{:S(2)}, u32[]{:S(2)}) collective-permute-start(bf16[128,512]{1,0:T(8,128)(2,1)S(1)} %collective-permute-done.14.refs_16_), channel_id=1, source_target_pairs={{0,2},{1,3},{2,0},{3,1},{4,6},{5,7},{6,4},{7,5},{8,10},{9,11},{10,... | collective-permute-start | bytes 393224 | tf_op jit(solution)/shard_map/ppermute | solution.py:441
  22.6 5.7 %collective-permute-start.15 = (bf16[128,512]{1,0:T(8,128)(2,1)S(1)}, bf16[128,512]{1,0:T(8,128)(2,1)S(1)}, u32[]{:S(2)}, u32[]{:S(2)}) collective-permute-start(bf16[128,512]{1,0:T(8,128)(2,1)S(1)} %collective-permute-done.14.refs_16_), channel_id=1, source_target_pairs={{0,1},{1,0},{2,3},{3,2},{4,5},{5,4},{6,7},{7,6},{8,9},{9,8},{10,11... | collective-permute-start | bytes 393224 | tf_op jit(solution)/shard_map/ppermute | solution.py:441
  22.6 7.2 %collective-permute-start.12 = (bf16[128,512]{1,0:T(8,128)(2,1)S(1)}, bf16[128,512]{1,0:T(8,128)(2,1)S(1)}, u32[]{:S(2)}, u32[]{:S(2)}) collective-permute-start(bf16[128,512]{1,0:T(8,128)(2,1)S(1)} %collective-permute-done.10.refs_12_), channel_id=1, source_target_pairs={{0,2},{1,3},{2,0},{3,1},{4,6},{5,7},{6,4},{7,5},{8,10},{9,11},{10,... | collective-permute-start | bytes 393224 | tf_op jit(solution)/shard_map/ppermute | solution.py:441
  24.1 6.3 %collective-permute-start.11 = (bf16[128,512]{1,0:T(8,128)(2,1)S(1)}, bf16[128,512]{1,0:T(8,128)(2,1)S(1)}, u32[]{:S(2)}, u32[]{:S(2)}) collective-permute-start(bf16[128,512]{1,0:T(8,128)(2,1)S(1)} %collective-permute-done.10.refs_12_), channel_id=1, source_target_pairs={{0,1},{1,0},{2,3},{3,2},{4,5},{5,4},{6,7},{7,6},{8,9},{9,8},{10,11... | collective-permute-start | bytes 393224 | tf_op jit(solution)/shard_map/ppermute | solution.py:441
  24.3 6.2 %collective-permute-start.9 = (bf16[128,512]{1,0:T(8,128)(2,1)S(1)}, bf16[128,512]{1,0:T(8,128)(2,1)S(1)}, u32[]{:S(2)}, u32[]{:S(2)}) collective-permute-start(bf16[128,512]{1,0:T(8,128)(2,1)S(1)} %collective-permute-done.8.refs_10_), channel_id=1, source_target_pairs={{0,1},{1,0},{2,3},{3,2},{4,5},{5,4},{6,7},{7,6},{8,9},{9,8},{10,11... | collective-permute-start | bytes 393224 | tf_op jit(solution)/shard_map/ppermute | solution.py:441
  28.2 5.0 %collective-permute-start.30 = (bf16[128,512]{1,0:T(8,128)(2,1)S(1)}, bf16[128,512]{1,0:T(8,128)(2,1)S(1)}, u32[]{:S(2)}, u32[]{:S(2)}) collective-permute-start(bf16[128,512]{1,0:T(8,128)(2,1)S(1)} %collective-permute-done.22.refs_24_), channel_id=1, source_target_pairs={{0,8},{4,12},{8,0},{12,4},{16,24},{20,28},{24,16},{28,20},{1,9},{5... | collective-permute-start | bytes 393224 | tf_op jit(solution)/shard_map/ppermute | solution.py:441
  28.2 5.7 %collective-permute-start.26 = (bf16[128,512]{1,0:T(8,128)(2,1)S(1)}, bf16[128,512]{1,0:T(8,128)(2,1)S(1)}, u32[]{:S(2)}, u32[]{:S(2)}) collective-permute-start(bf16[128,512]{1,0:T(8,128)(2,1)S(1)} %collective-permute-done.22.refs_24_), channel_id=1, source_target_pairs={{0,4},{4,0},{8,12},{12,8},{16,20},{20,16},{24,28},{28,24},{1,5},{5... | collective-permute-start | bytes 393224 | tf_op jit(solution)/shard_map/ppermute | solution.py:441
  29.8 5.5 %collective-permute-start.24 = (bf16[128,512]{1,0:T(8,128)(2,1)S(1)}, bf16[128,512]{1,0:T(8,128)(2,1)S(1)}, u32[]{:S(2)}, u32[]{:S(2)}) collective-permute-start(bf16[128,512]{1,0:T(8,128)(2,1)S(1)} %collective-permute-done.22.refs_24_), channel_id=1, source_target_pairs={{0,2},{1,3},{2,0},{3,1},{4,6},{5,7},{6,4},{7,5},{8,10},{9,11},{10,... | collective-permute-start | bytes 393224 | tf_op jit(solution)/shard_map/ppermute | solution.py:441
  30.4 5.0 %collective-permute-start.23 = (bf16[128,512]{1,0:T(8,128)(2,1)S(1)}, bf16[128,512]{1,0:T(8,128)(2,1)S(1)}, u32[]{:S(2)}, u32[]{:S(2)}) collective-permute-start(bf16[128,512]{1,0:T(8,128)(2,1)S(1)} %collective-permute-done.22.refs_24_), channel_id=1, source_target_pairs={{0,1},{1,0},{2,3},{3,2},{4,5},{5,4},{6,7},{7,6},{8,9},{9,8},{10,11... | collective-permute-start | bytes 393224 | tf_op jit(solution)/shard_map/ppermute | solution.py:441
  30.4 6.1 %collective-permute-start.5 = (bf16[136,512]{1,0:T(8,128)(2,1)S(1)}, bf16[136,512]{1,0:T(8,128)(2,1)S(1)}, u32[]{:S(2)}, u32[]{:S(2)}) collective-permute-start(bf16[136,512]{1,0:T(8,128)(2,1)S(1)} %collective-permute-done.3.refs_4_), channel_id=1, source_target_pairs={{0,8},{4,12},{8,0},{12,4},{16,24},{20,28},{24,16},{28,20},{1,9},{5... | collective-permute-start | bytes 417800 | tf_op jit(solution)/shard_map/ppermute | solution.py:441
  33.2 5.1 %collective-permute-start.4 = (bf16[136,512]{1,0:T(8,128)(2,1)S(1)}, bf16[136,512]{1,0:T(8,128)(2,1)S(1)}, u32[]{:S(2)}, u32[]{:S(2)}) collective-permute-start(bf16[136,512]{1,0:T(8,128)(2,1)S(1)} %collective-permute-done.3.refs_4_), channel_id=1, source_target_pairs={{0,4},{4,0},{8,12},{12,8},{16,20},{20,16},{24,28},{28,24},{1,5},{5... | collective-permute-start | bytes 417800 | tf_op jit(solution)/shard_map/ppermute | solution.py:441
  33.9 5.9 %collective-permute-start.2 = (bf16[136,512]{1,0:T(8,128)(2,1)S(1)}, bf16[136,512]{1,0:T(8,128)(2,1)S(1)}, u32[]{:S(2)}, u32[]{:S(2)}) collective-permute-start(bf16[136,512]{1,0:T(8,128)(2,1)S(1)} %collective-permute-done.1.refs_2_), channel_id=1, source_target_pairs={{0,4},{4,0},{8,12},{12,8},{16,20},{20,16},{24,28},{28,24},{1,5},{5... | collective-permute-start | bytes 417800 | tf_op jit(solution)/shard_map/ppermute | solution.py:441
  35.2 5.9 %collective-permute-start.20 = (bf16[128,512]{1,0:T(8,128)(2,1)S(1)}, bf16[128,512]{1,0:T(8,128)(2,1)S(1)}, u32[]{:S(2)}, u32[]{:S(2)}) collective-permute-start(bf16[128,512]{1,0:T(8,128)(2,1)S(1)} %collective-permute-done.18.refs_20_), channel_id=1, source_target_pairs={{0,2},{1,3},{2,0},{3,1},{4,6},{5,7},{6,4},{7,5},{8,10},{9,11},{10,... | collective-permute-start | bytes 393224 | tf_op jit(solution)/shard_map/ppermute | solution.py:441
  35.5 7.7 %collective-permute-start.19 = (bf16[128,512]{1,0:T(8,128)(2,1)S(1)}, bf16[128,512]{1,0:T(8,128)(2,1)S(1)}, u32[]{:S(2)}, u32[]{:S(2)}) collective-permute-start(bf16[128,512]{1,0:T(8,128)(2,1)S(1)} %collective-permute-done.18.refs_20_), channel_id=1, source_target_pairs={{0,1},{1,0},{2,3},{3,2},{4,5},{5,4},{6,7},{7,6},{8,9},{9,8},{10,11... | collective-permute-start | bytes 393224 | tf_op jit(solution)/shard_map/ppermute | solution.py:441
  36.5 6.6 %collective-permute-start.17 = (bf16[128,512]{1,0:T(8,128)(2,1)S(1)}, bf16[128,512]{1,0:T(8,128)(2,1)S(1)}, u32[]{:S(2)}, u32[]{:S(2)}) collective-permute-start(bf16[128,512]{1,0:T(8,128)(2,1)S(1)} %collective-permute-done.16.refs_18_), channel_id=1, source_target_pairs={{0,1},{1,0},{2,3},{3,2},{4,5},{5,4},{6,7},{7,6},{8,9},{9,8},{10,11... | collective-permute-start | bytes 393224 | tf_op jit(solution)/shard_map/ppermute | solution.py:441
  38.3 5.6 %collective-permute-start.13 = (bf16[128,512]{1,0:T(8,128)(2,1)S(1)}, bf16[128,512]{1,0:T(8,128)(2,1)S(1)}, u32[]{:S(2)}, u32[]{:S(2)}) collective-permute-start(bf16[128,512]{1,0:T(8,128)(2,1)S(1)} %collective-permute-done.12.refs_14_), channel_id=1, source_target_pairs={{0,1},{1,0},{2,3},{3,2},{4,5},{5,4},{6,7},{7,6},{8,9},{9,8},{10,11... | collective-permute-start | bytes 393224 | tf_op jit(solution)/shard_map/ppermute | solution.py:441
  39.8 5.1 %collective-permute-start.34 = (bf16[128,512]{1,0:T(8,128)(2,1)S(1)}, bf16[128,512]{1,0:T(8,128)(2,1)}, u32[]{:S(2)}, u32[]{:S(2)}) collective-permute-start(bf16[128,512]{1,0:T(8,128)(2,1)S(1)} %collective-permute-done.30.refs_32_), channel_id=1, source_target_pairs={{0,4},{4,0},{8,12},{12,8},{16,20},{20,16},{24,28},{28,24},{1,5},{5... | collective-permute-start | bytes 393224 | tf_op jit(solution)/shard_map/ppermute | solution.py:441
  41.2 5.1 %collective-permute-start.32 = (bf16[128,512]{1,0:T(8,128)(2,1)S(1)}, bf16[128,512]{1,0:T(8,128)(2,1)}, u32[]{:S(2)}, u32[]{:S(2)}) collective-permute-start(bf16[128,512]{1,0:T(8,128)(2,1)S(1)} %collective-permute-done.30.refs_32_), channel_id=1, source_target_pairs={{0,2},{1,3},{2,0},{3,1},{4,6},{5,7},{6,4},{7,5},{8,10},{9,11},{10,... | collective-permute-start | bytes 393224 | tf_op jit(solution)/shard_map/ppermute | solution.py:441
  43.1 8.9 %collective-permute-start.6 = (bf16[136,512]{1,0:T(8,128)(2,1)S(1)}, bf16[136,512]{1,0:T(8,128)(2,1)S(1)}, u32[]{:S(2)}, u32[]{:S(2)}) collective-permute-start(bf16[136,512]{1,0:T(8,128)(2,1)S(1)} %collective-permute-done.5.refs_6_), channel_id=1, source_target_pairs={{0,4},{4,0},{8,12},{12,8},{16,20},{20,16},{24,28},{28,24},{1,5},{5... | collective-permute-start | bytes 417800 | tf_op jit(solution)/shard_map/ppermute | solution.py:441
  44.6 5.7 %collective-permute-start.28 = (bf16[128,512]{1,0:T(8,128)(2,1)S(1)}, bf16[128,512]{1,0:T(8,128)(2,1)}, u32[]{:S(2)}, u32[]{:S(2)}) collective-permute-start(bf16[128,512]{1,0:T(8,128)(2,1)S(1)} %collective-permute-done.26.refs_28_), channel_id=1, source_target_pairs={{0,2},{1,3},{2,0},{3,1},{4,6},{5,7},{6,4},{7,5},{8,10},{9,11},{10,... | collective-permute-start | bytes 393224 | tf_op jit(solution)/shard_map/ppermute | solution.py:441
  44.9 5.3 %collective-permute-start.27 = (bf16[128,512]{1,0:T(8,128)(2,1)S(1)}, bf16[128,512]{1,0:T(8,128)(2,1)S(1)}, u32[]{:S(2)}, u32[]{:S(2)}) collective-permute-start(bf16[128,512]{1,0:T(8,128)(2,1)S(1)} %collective-permute-done.26.refs_28_), channel_id=1, source_target_pairs={{0,1},{1,0},{2,3},{3,2},{4,5},{5,4},{6,7},{7,6},{8,9},{9,8},{10,11... | collective-permute-start | bytes 393224 | tf_op jit(solution)/shard_map/ppermute | solution.py:441
  46.2 5.1 %collective-permute-start.25 = (bf16[128,512]{1,0:T(8,128)(2,1)S(1)}, bf16[128,512]{1,0:T(8,128)(2,1)S(1)}, u32[]{:S(2)}, u32[]{:S(2)}) collective-permute-start(bf16[128,512]{1,0:T(8,128)(2,1)S(1)} %collective-permute-done.24.refs_26_), channel_id=1, source_target_pairs={{0,1},{1,0},{2,3},{3,2},{4,5},{5,4},{6,7},{7,6},{8,9},{9,8},{10,11... | collective-permute-start | bytes 393224 | tf_op jit(solution)/shard_map/ppermute | solution.py:441
  46.9 6.9 %collective-permute-start.36 = (bf16[128,512]{1,0:T(8,128)(2,1)}, bf16[128,512]{1,0:T(8,128)(2,1)}, u32[]{:S(2)}, u32[]{:S(2)}) collective-permute-start(bf16[128,512]{1,0:T(8,128)(2,1)} %collective-permute-done.34.refs_36_), channel_id=1, source_target_pairs={{0,2},{1,3},{2,0},{3,1},{4,6},{5,7},{6,4},{7,5},{8,10},{9,11},{10,... | collective-permute-start | bytes 393224 | tf_op jit(solution)/shard_map/ppermute | solution.py:441
  50.2 3.6 %collective-permute-start.35 = (bf16[128,512]{1,0:T(8,128)(2,1)}, bf16[128,512]{1,0:T(8,128)(2,1)}, u32[]{:S(2)}, u32[]{:S(2)}) collective-permute-start(bf16[128,512]{1,0:T(8,128)(2,1)} %collective-permute-done.34.refs_36_), channel_id=1, source_target_pairs={{0,1},{1,0},{2,3},{3,2},{4,5},{5,4},{6,7},{7,6},{8,9},{9,8},{10,11... | collective-permute-start | bytes 393224 | tf_op jit(solution)/shard_map/ppermute | solution.py:441
  (15 other events, 24.3 us)
